TPU v7x, 256 devices: a whole 4x4x8 slice. The times are simulated.
256 devices in a mesh: band: 8 (over x, core), freq: 32 (over y, z).
Axes of the slice: x: 4, y: 4, z: 8, core: 2. Of those that a mesh axis runs over, the one named last changes fastest.
Arguments:
- spectrum: float32 [32, 36, 128, 256], P('freq', None, 'band'), may hold values from 0.05 to 1
- velocity: float32 [2, 24, 128, 256], P(None, None, 'band', 'freq'), may hold values from -3 to 3
- gain_matrix: bfloat16 [1152, 1152], replicated, may hold values from -0.1875 to 0.1875
- quad_matrix: bfloat16 [1152, 1152], replicated, may hold values from -0.1875 to 0.1875
- limiter_flags: int32 [8, 128, 256], replicated, may hold values 0 or 1
- sea_mask: int32 [128, 256], replicated, may hold values 0 or 1
- current_route: int32 [32], replicated, may hold values from 0 to 23
- stokes_route: int32 [32, 4], replicated, may hold values from 0 to 23
Outputs:
- spectrum_out: float32 [32, 36, 128, 256], P('freq', None, 'band')
- velocity_out: float32 [2, 24, 128, 256], P(None, None, 'band', 'freq')
All inputs are finite; a program needn't handle non-finite values.
Results may differ from a plain program's by a relative error of at most 0.00045.
Values sent between devices are 32-bit elements; how exact they have to be, the bound alone decides.
No kernel may reach another device: no remote copies, remote signals or barrier semaphores. Data moves between devices by JAX's collectives and lax.ppermute only.
A program may use at most 64 MiB of HBM per device.

v0:
```python
import jax
import jax.numpy as jnp
from jax import lax
from jax.sharding import PartitionSpec as P

DIR = 36
F_DEV = 1
LAYERS = 24
SUB = 4
CYCLES = 2
OSTEPS = 3


precise = lax.Precision.HIGHEST
ocean_dt = 0.2
viscous = 0.5
coriolis = 1.0
mixing = 0.5
friction = 0.1


def padded_2(cells, sides, width):
    for axis, dim in sides:
        count = lax.axis_size(axis)
        ends = count - 1
        head = lax.slice_in_dim(cells, 0, width, axis=dim)
        tail = lax.slice_in_dim(cells, cells.shape[dim] - width, cells.shape[dim], axis=dim)
        cells = jnp.concatenate(
            [
                lax.ppermute(tail, axis, [(i, (i + 1) % count) for i in range(ends)]),
                cells,
                lax.ppermute(head, axis, [((i + 1) % count, i) for i in range(ends)]),
            ],
            axis=dim,
        )
    return cells


def directions(how_many):
    angles = (jnp.arange(how_many, dtype=jnp.float32) + 0.5) * (2.0 * jnp.pi / how_many)
    return (jnp.cos(angles), jnp.sin(angles))


def speed_of(position, total_count):
    return 0.5 + 0.3 * (position.astype(jnp.float32) + 0.5) / total_count


def wavenumber(position, total_count):
    return 0.5 + 1.5 * (position.astype(jnp.float32) + 0.5) / total_count


def pad_last(values):
    zero_col = jnp.zeros(values.shape[:-1] + (1,), values.dtype)
    return jnp.concatenate([zero_col, values, zero_col], axis=-1)


def transport(lower_side, upper_side, courant, limiter):
    upwind = jnp.maximum(courant, 0.0) * lower_side + jnp.minimum(courant, 0.0) * upper_side
    wendroff = 0.5 * courant * (lower_side + upper_side) - 0.5 * courant * courant * (
        upper_side - lower_side
    )
    return upwind + limiter * (wendroff - upwind)


def substep(extended, current, limiter_rows, sea_rows, rate_now, cos_table, sin_table):
    limiter = limiter_rows.astype(jnp.float32)
    drifts = 0.15 * jnp.tanh(current)
    north_drift = drifts[..., 1:2, :, :]
    face_north = 0.5 * (north_drift[..., :-1, :] + north_drift[..., 1:, :])
    courant = rate_now * sin_table[:, None, None] + face_north
    flux_north = transport(extended[..., :-1, :], extended[..., 1:, :], courant, limiter[1:, :])
    shifted = extended[..., 1:-1, :] - (flux_north[..., 1:, :] - flux_north[..., :-1, :])
    east_drift = pad_last(drifts[..., 0:1, 1:-1, :])
    face_east = 0.5 * (east_drift[..., :-1] + east_drift[..., 1:])
    courant_east = rate_now * cos_table[:, None, None] + face_east
    padded = pad_last(shifted)
    limiter_east = pad_last(limiter[1:-1, :])[:, 1:]
    flux_east = transport(padded[..., :-1], padded[..., 1:], courant_east, limiter_east)
    result = shifted - (flux_east[..., 1:] - flux_east[..., :-1])
    return result * sea_rows.astype(jnp.float32)


def source(block, gain_matrix, quad_matrix):
    block_shape = block.shape
    flattened = block.reshape(block_shape[0] * block_shape[1], -1)
    gain_arg = jnp.dot(
        gain_matrix, flattened.astype(jnp.bfloat16), preferred_element_type=jnp.float32
    )
    quartic = jnp.dot(
        quad_matrix,
        (flattened * flattened).astype(jnp.bfloat16),
        preferred_element_type=jnp.float32,
    )
    updated = flattened * (1.0 + 0.5 * jnp.tanh(gain_arg) - 0.25 * jnp.tanh(quartic))
    return updated.reshape(block_shape)


def deposit_table(stokes_route):
    layer_ids = jnp.arange(LAYERS, dtype=jnp.int32)
    weights = 1.0 / (1.0 + jnp.arange(stokes_route.shape[1], dtype=jnp.float32))
    hits = (stokes_route[:, :, None] == layer_ids[None, None, :]).astype(jnp.float32)
    return jnp.sum(hits * weights[None, :, None], axis=1)


def stokes_profile(spectrum, numbers, deposit):
    cos_table, sin_table = directions(spectrum.shape[1])
    factor = numbers * spectrum.shape[1] ** (-0.5)
    eastward = (
        jnp.einsum("fdrc,d->frc", spectrum, cos_table, precision=precise) * factor[:, None, None]
    )
    northward = (
        jnp.einsum("fdrc,d->frc", spectrum, sin_table, precision=precise) * factor[:, None, None]
    )
    stacked = jnp.stack([eastward, northward], axis=1)
    return jnp.einsum("fl,fsrc->slrc", deposit, stacked, precision=precise)


def ocean_step(padded, stokes, sea_tile):
    inner = padded[:, :, 1:-1, 1:-1]
    laplace = (
        padded[:, :, 2:, 1:-1]
        + padded[:, :, :-2, 1:-1]
        + padded[:, :, 1:-1, 2:]
        + padded[:, :, 1:-1, :-2]
        - 4.0 * inner
    )
    vertical = jnp.pad(inner, ((0, 0), (1, 1), (0, 0), (0, 0)))
    mixing_term = vertical[:, 2:] + vertical[:, :-2] - 2.0 * inner
    moving = inner + stokes
    turning = jnp.stack([moving[1], -moving[0]])
    tendency = viscous * laplace + coriolis * turning + mixing * mixing_term - friction * inner
    return (inner + ocean_dt * tendency) * sea_tile.astype(jnp.float32)


def body(
    spectrum,
    velocity,
    gain_matrix,
    quad_matrix,
    limiter_flags,
    sea_mask,
    current_route,
    stokes_route,
):
    band_index = lax.axis_index("band")
    freq_index = lax.axis_index("freq")
    freq_count = lax.axis_size("freq")
    freq_total = F_DEV * freq_count
    local_rows = spectrum.shape[2]
    grid_cols = spectrum.shape[3]
    tile_cols = velocity.shape[3]
    cos_table, sin_table = directions(DIR)
    own_freqs = freq_index * F_DEV + jnp.arange(F_DEV, dtype=jnp.int32)
    rate_now = speed_of(own_freqs, freq_total).reshape(F_DEV, 1, 1, 1)
    deposit_all = deposit_table(stokes_route)
    layer_ids = jnp.arange(LAYERS, dtype=jnp.int32)
    picker = (current_route[:, None] == layer_ids[None, :]).astype(jnp.float32)
    outgoing = jnp.einsum("fl,slrc->fsrc", picker, velocity, precision=precise)
    current = lax.all_to_all(outgoing, "freq", split_axis=0, concat_axis=3, tiled=True)
    depth = 1
    current_ext = padded_2(current, (("band", 2),), depth)
    flag_pad = jnp.pad(limiter_flags, ((0, 0), (SUB, SUB), (0, 0)))
    sea_pad = jnp.pad(sea_mask, ((SUB, SUB), (0, 0)))
    row_base = band_index * local_rows + SUB
    field_now = spectrum
    drift_tile = None
    for cycle_index in range(CYCLES):
        for step_index in range(SUB):
            extended = padded_2(field_now, (("band", 2),), 1)
            flag_rows = lax.dynamic_slice_in_dim(
                flag_pad[cycle_index * SUB + step_index], row_base - 1, local_rows + 2 * 1, 0
            )
            sea_rows = lax.dynamic_slice_in_dim(
                sea_pad, row_base - 1 + 1, local_rows + 2 * 1 - 2, 0
            )
            field_now = substep(
                extended, current_ext, flag_rows, sea_rows, rate_now, cos_table, sin_table
            )
        if cycle_index == 0:
            own_deposit = lax.dynamic_slice_in_dim(deposit_all, freq_index * F_DEV, F_DEV, 0)
            own_numbers = wavenumber(own_freqs, freq_total)
            partial_value = stokes_profile(field_now, own_numbers, own_deposit)
            drift_tile = lax.psum_scatter(partial_value, "freq", scatter_dimension=3, tiled=True)
        grouped = field_now.reshape(F_DEV, DIR, local_rows, freq_count, tile_cols)
        grouped = jnp.transpose(grouped, (0, 1, 3, 2, 4)).reshape(
            F_DEV, DIR, freq_count, local_rows * tile_cols
        )
        whole = source(
            lax.all_to_all(grouped, "freq", split_axis=2, concat_axis=0, tiled=True),
            gain_matrix,
            quad_matrix,
        )
        moved = lax.all_to_all(whole, "freq", split_axis=0, concat_axis=2, tiled=True)
        moved = moved.reshape(F_DEV, DIR, freq_count, local_rows, tile_cols)
        field_now = jnp.transpose(moved, (0, 1, 3, 2, 4)).reshape(F_DEV, DIR, local_rows, grid_cols)
    sea_tile = lax.dynamic_slice(
        sea_mask, (band_index * local_rows, freq_index * tile_cols), (local_rows, tile_cols)
    )
    ocean_now = velocity
    for step_index in range(OSTEPS):
        padded = padded_2(ocean_now, (("band", 2), ("freq", 3)), 1)
        ocean_now = ocean_step(padded, drift_tile, sea_tile)
    return (field_now, ocean_now)


def solution(mesh):
    return jax.shard_map(
        body,
        mesh=mesh,
        in_specs=(
            P("freq", None, "band", None),
            P(None, None, "band", "freq"),
            P(),
            P(),
            P(),
            P(),
            P(),
            P(),
        ),
        out_specs=(P("freq", None, "band", None), P(None, None, "band", "freq")),
        check_vma=False,
    )
```

profile of v0, /device:TPU:34, one launch (start us, length us, event | category | flops | bytes accessed | tf_op | source)
XLA Modules:
  0.0 530.7 jit_solution(17986027290691417217)
XLA Ops:
  15.0 11.4 %all-to-all-start = ((f32[32,1,256]{2,1,0:T(1,128)}), f32[32,1,256]{2,1,0:T(1,128)S(1)}, u32[]{:S(2)}, u32[]{:S(2)}) async-start(f32[32,1,256]{2,1,0:T(1,128)} %reshape.1831), calls=%async_computation | async-start | bytes 65536 | tf_op jit(solution)/shard_map/all_to_all | solution.py:159
  26.4 3.0 copy.306
  42.0 3.0 collective-permute-start
  54.8 3.9 fusion.79
  61.9 3.5 collective-permute-start.4
  74.5 3.6 collective-permute-start.6
  87.1 3.6 collective-permute-start.8
  102.7 3.5 copy.308
  106.2 9.8 %all-to-all-start.1 = ((f32[1,36,32,128]{3,0,1,2:T(1,128)}), f32[1,36,32,128]{3,0,1,2:T(1,128)S(1)}, u32[]{:S(2)}, u32[]{:S(2)}) async-start(f32[1,36,32,128]{3,0,1,2:T(1,128)} %copy.308), calls=%async_computation.1 | async-start | bytes 1179648 | tf_op jit(solution)/shard_map/all_to_all | solution.py:189
  116.6 18.7 %all-to-all-done.1 = f32[1,36,32,128]{3,0,1,2:T(1,128)S(1)} async-done(((f32[1,36,32,128]{3,0,1,2:T(1,128)}), f32[1,36,32,128]{3,0,1,2:T(1,128)S(1)}, u32[]{:S(2)}, u32[]{:S(2)}) %all-to-all-start.1) | async-done | bytes 589856 | tf_op jit(solution)/shard_map/all_to_all | solution.py:189
  144.6 5.6 %all-to-all-start.2 = ((f32[32,36,1,128]{3,2,1,0:T(1,128)}), f32[32,36,1,128]{3,2,1,0:T(1,128)S(1)}, u32[]{:S(2)}, u32[]{:S(2)}) async-start(f32[32,36,1,128]{3,2,1,0:T(1,128)} %bitcast.19), calls=%async_computation.2 | async-start | bytes 1179648 | tf_op jit(solution)/shard_map/all_to_all | solution.py:193
  155.2 4.1 fusion.181
  161.9 7.6 %all-to-all-done.2 = f32[32,36,1,128]{3,2,1,0:T(1,128)S(1)} async-done(((f32[32,36,1,128]{3,2,1,0:T(1,128)}), f32[32,36,1,128]{3,2,1,0:T(1,128)S(1)}, u32[]{:S(2)}, u32[]{:S(2)}) %all-to-all-start.2) | async-done | bytes 589856 | tf_op jit(solution)/shard_map/all_to_all | solution.py:193
  169.5 2.8 copy.314
  176.1 3.6 collective-permute-start.11
  187.1 3.8 collective-permute-start.12
  201.6 3.8 collective-permute-start.14
  210.0 4.0 fusion.103
  219.2 3.5 collective-permute-start.16
  224.8 202.7 %reduce-scatter.2.cloned.1.call-done = f32[2,24,16,8]{1,3,2,0:T(8,128)} async-done(((f32[2,24,16,256]{1,3,2,0:T(8,128)}), f32[2,24,16,8]{1,3,2,0:T(8,128)}) %reduce-scatter.2.cloned.1.call-update) | async-done | bytes 24592 | tf_op jit(solution)/shard_map/reduce_scatter | solution.py:183
  429.1 4.0 fusion.107
  437.3 3.5 copy.317
  440.8 7.9 %all-to-all-start.3 = ((f32[1,36,32,128]{3,0,1,2:T(1,128)}), f32[1,36,32,128]{3,0,1,2:T(1,128)S(1)}, u32[]{:S(2)}, u32[]{:S(2)}) async-start(f32[1,36,32,128]{3,0,1,2:T(1,128)} %copy.317), calls=%async_computation.3 | async-start | bytes 1179648 | tf_op jit(solution)/shard_map/all_to_all | solution.py:189
  453.2 3.7 collective-permute-start.21
  462.6 3.6 collective-permute-start.22
  470.2 3.9 collective-permute-start.25
  483.5 11.3 %all-to-all-start.4 = ((f32[32,36,1,128]{3,2,1,0:T(1,128)}), f32[32,36,1,128]{3,2,1,0:T(1,128)S(1)}, u32[]{:S(2)}, u32[]{:S(2)}) async-start(f32[32,36,1,128]{3,2,1,0:T(1,128)} %bitcast.39), calls=%async_computation.4 | async-start | bytes 1179648 | tf_op jit(solution)/shard_map/all_to_all | solution.py:193
  499.0 3.2 collective-permute-start.26
  505.7 3.7 collective-permute-start.29
  514.7 2.8 copy.323
  517.5 3.2 copy_bitcast_fusion
  520.7 3.1 copy.325
  (247 shorter events, 155.9 us)
Async XLA Ops:
  8.7 440.1 %collective-permute-start.18 = (f32[2,24,1,8]{1,3,2,0:T(8,128)}, f32[2,24,1,8]{1,3,2,0:T(8,128)}, u32[]{:S(2)}, u32[]{:S(2)}) collective-permute-start(f32[2,24,1,8]{1,3,2,0:T(8,128)} %get-tuple-element.58), channel_id=1, source_target_pairs={{32,0},{64,32},{96,64},{128,96},{160,128},{192,160},{224,192},{33,... | collective-permute-start | bytes 4616 | tf_op jit(solution)/shard_map/ppermute | solution.py:32
  10.6 143.2 %collective-permute-start.19 = (f32[2,24,1,8]{1,3,2,0:T(8,128)}, f32[2,24,1,8]{1,3,2,0:T(8,128)}, u32[]{:S(2)}, u32[]{:S(2)}) collective-permute-start(f32[2,24,1,8]{1,3,2,0:T(8,128)} %get-tuple-element.59), channel_id=1, source_target_pairs={{0,32},{32,64},{64,96},{96,128},{128,160},{160,192},{192,224},{1,3... | collective-permute-start | bytes 4616 | tf_op jit(solution)/shard_map/ppermute | solution.py:30
  15.0 24.7 %all-to-all-start = ((f32[32,1,256]{2,1,0:T(1,128)}), f32[32,1,256]{2,1,0:T(1,128)S(1)}, u32[]{:S(2)}, u32[]{:S(2)}) async-start(f32[32,1,256]{2,1,0:T(1,128)} %reshape.1831), calls=%async_computation | async-start | bytes 65536 | tf_op jit(solution)/shard_map/all_to_all | solution.py:159
  31.1 22.3 %collective-permute-start.2 = (f32[1,36,1,256]{1,3,2,0:T(8,128)}, f32[1,36,1,256]{1,3,2,0:T(8,128)}, u32[]{:S(2)}, u32[]{:S(2)}) collective-permute-start(f32[1,36,1,256]{1,3,2,0:T(8,128)} %get-tuple-element.32), channel_id=1, source_target_pairs={{0,32},{32,64},{64,96},{96,128},{128,160},{160,192},{192,224},{1,3... | collective-permute-start | bytes 110600 | tf_op jit(solution)/shard_map/ppermute | solution.py:30
  42.0 8.0 %collective-permute-start = (f32[1,2,1,256]{2,3,1,0:T(8,128)}, f32[1,2,1,256]{2,3,1,0:T(8,128)}, u32[]{:S(2)}, u32[]{:S(2)}) collective-permute-start(f32[1,2,1,256]{2,3,1,0:T(8,128)} %get-tuple-element.42), channel_id=1, source_target_pairs={{0,32},{32,64},{64,96},{96,128},{128,160},{160,192},{192,224},{1,3... | collective-permute-start | bytes 6152 | tf_op jit(solution)/shard_map/ppermute | solution.py:30
  45.0 8.0 %collective-permute-start.1 = (f32[1,2,1,256]{2,3,1,0:T(8,128)}, f32[1,2,1,256]{2,3,1,0:T(8,128)S(1)}, u32[]{:S(2)}, u32[]{:S(2)}) collective-permute-start(f32[1,2,1,256]{2,3,1,0:T(8,128)} %get-tuple-element.43), channel_id=1, source_target_pairs={{32,0},{64,32},{96,64},{128,96},{160,128},{192,160},{224,192},{33,... | collective-permute-start | bytes 6152 | tf_op jit(solution)/shard_map/ppermute | solution.py:32
  50.0 4.7 collective-permute-start.3
  61.9 6.4 %collective-permute-start.4 = (f32[1,36,1,256]{1,3,2,0:T(8,128)S(1)}, f32[1,36,1,256]{1,3,2,0:T(8,128)S(1)}, u32[]{:S(2)}, u32[]{:S(2)}) collective-permute-start(f32[1,36,1,256]{1,3,2,0:T(8,128)S(1)} %get-tuple-element.30), channel_id=1, source_target_pairs={{0,32},{32,64},{64,96},{96,128},{128,160},{160,192},{192,224},{1,3... | collective-permute-start | bytes 110600 | tf_op jit(solution)/shard_map/ppermute | solution.py:30
  65.4 4.6 collective-permute-start.5
  74.5 6.4 %collective-permute-start.6 = (f32[1,36,1,256]{1,3,2,0:T(8,128)S(1)}, f32[1,36,1,256]{1,3,2,0:T(8,128)S(1)}, u32[]{:S(2)}, u32[]{:S(2)}) collective-permute-start(f32[1,36,1,256]{1,3,2,0:T(8,128)S(1)} %get-tuple-element.28), channel_id=1, source_target_pairs={{0,32},{32,64},{64,96},{96,128},{128,160},{160,192},{192,224},{1,3... | collective-permute-start | bytes 110600 | tf_op jit(solution)/shard_map/ppermute | solution.py:30
  87.1 6.5 %collective-permute-start.8 = (f32[1,36,1,256]{1,3,2,0:T(8,128)S(1)}, f32[1,36,1,256]{1,3,2,0:T(8,128)S(1)}, u32[]{:S(2)}, u32[]{:S(2)}) collective-permute-start(f32[1,36,1,256]{1,3,2,0:T(8,128)S(1)} %get-tuple-element.26), channel_id=1, source_target_pairs={{0,32},{32,64},{64,96},{96,128},{128,160},{160,192},{192,224},{1,3... | collective-permute-start | bytes 110600 | tf_op jit(solution)/shard_map/ppermute | solution.py:30
  106.2 29.2 %all-to-all-start.1 = ((f32[1,36,32,128]{3,0,1,2:T(1,128)}), f32[1,36,32,128]{3,0,1,2:T(1,128)S(1)}, u32[]{:S(2)}, u32[]{:S(2)}) async-start(f32[1,36,32,128]{3,0,1,2:T(1,128)} %copy.308), calls=%async_computation.1 | async-start | bytes 1179648 | tf_op jit(solution)/shard_map/all_to_all | solution.py:189
  144.6 24.8 %all-to-all-start.2 = ((f32[32,36,1,128]{3,2,1,0:T(1,128)}), f32[32,36,1,128]{3,2,1,0:T(1,128)S(1)}, u32[]{:S(2)}, u32[]{:S(2)}) async-start(f32[32,36,1,128]{3,2,1,0:T(1,128)} %bitcast.19), calls=%async_computation.2 | async-start | bytes 1179648 | tf_op jit(solution)/shard_map/all_to_all | solution.py:193
  150.2 277.3 %reduce-scatter.2.cloned.1.call-start = ((), (), s32[]{:S(2)}) async-start(), calls=%async_computation.6 | async-start | bytes 4325376 | tf_op jit(solution)/shard_map/reduce_scatter | solution.py:183
  174.2 6.3 %collective-permute-start.10 = (f32[1,36,1,256]{1,3,2,0:T(8,128)S(1)}, f32[1,36,1,256]{1,3,2,0:T(8,128)S(1)}, u32[]{:S(2)}, u32[]{:S(2)}) collective-permute-start(f32[1,36,1,256]{1,3,2,0:T(8,128)S(1)} %get-tuple-element.24), channel_id=1, source_target_pairs={{0,32},{32,64},{64,96},{96,128},{128,160},{160,192},{192,224},{1,3... | collective-permute-start | bytes 110600 | tf_op jit(solution)/shard_map/ppermute | solution.py:30
  176.1 6.1 %collective-permute-start.11 = (f32[1,36,1,256]{1,3,2,0:T(8,128)S(1)}, f32[1,36,1,256]{1,3,2,0:T(8,128)S(1)}, u32[]{:S(2)}, u32[]{:S(2)}) collective-permute-start(f32[1,36,1,256]{1,3,2,0:T(8,128)S(1)} %get-tuple-element.25), channel_id=1, source_target_pairs={{32,0},{64,32},{96,64},{128,96},{160,128},{192,160},{224,192},{33,... | collective-permute-start | bytes 110600 | tf_op jit(solution)/shard_map/ppermute | solution.py:32
  187.1 6.4 %collective-permute-start.12 = (f32[1,36,1,256]{1,3,2,0:T(8,128)S(1)}, f32[1,36,1,256]{1,3,2,0:T(8,128)S(1)}, u32[]{:S(2)}, u32[]{:S(2)}) collective-permute-start(f32[1,36,1,256]{1,3,2,0:T(8,128)S(1)} %get-tuple-element.22), channel_id=1, source_target_pairs={{0,32},{32,64},{64,96},{96,128},{128,160},{160,192},{192,224},{1,3... | collective-permute-start | bytes 110600 | tf_op jit(solution)/shard_map/ppermute | solution.py:30
  201.6 8.4 %collective-permute-start.14 = (f32[1,36,1,256]{1,3,2,0:T(8,128)S(1)}, f32[1,36,1,256]{1,3,2,0:T(8,128)S(1)}, u32[]{:S(2)}, u32[]{:S(2)}) collective-permute-start(f32[1,36,1,256]{1,3,2,0:T(8,128)S(1)} %get-tuple-element.20), channel_id=1, source_target_pairs={{0,32},{32,64},{64,96},{96,128},{128,160},{160,192},{192,224},{1,3... | collective-permute-start | bytes 110600 | tf_op jit(solution)/shard_map/ppermute | solution.py:30
  205.4 4.6 collective-permute-start.15
  219.2 209.9 %collective-permute-start.16 = (f32[1,36,1,256]{1,3,2,0:T(8,128)}, f32[1,36,1,256]{1,3,2,0:T(8,128)S(1)}, u32[]{:S(2)}, u32[]{:S(2)}) collective-permute-start(f32[1,36,1,256]{1,3,2,0:T(8,128)} %get-tuple-element.18), channel_id=1, source_target_pairs={{0,32},{32,64},{64,96},{96,128},{128,160},{160,192},{192,224},{1,3... | collective-permute-start | bytes 110600 | tf_op jit(solution)/shard_map/ppermute | solution.py:30
  222.8 206.3 %collective-permute-start.17 = (f32[1,36,1,256]{1,3,2,0:T(8,128)S(1)}, f32[1,36,1,256]{1,3,2,0:T(8,128)S(1)}, u32[]{:S(2)}, u32[]{:S(2)}) collective-permute-start(f32[1,36,1,256]{1,3,2,0:T(8,128)S(1)} %get-tuple-element.19), channel_id=1, source_target_pairs={{32,0},{64,32},{96,64},{128,96},{160,128},{192,160},{224,192},{33,... | collective-permute-start | bytes 110600 | tf_op jit(solution)/shard_map/ppermute | solution.py:32
  440.8 33.3 %all-to-all-start.3 = ((f32[1,36,32,128]{3,0,1,2:T(1,128)}), f32[1,36,32,128]{3,0,1,2:T(1,128)S(1)}, u32[]{:S(2)}, u32[]{:S(2)}) async-start(f32[1,36,32,128]{3,0,1,2:T(1,128)} %copy.317), calls=%async_computation.3 | async-start | bytes 1179648 | tf_op jit(solution)/shard_map/all_to_all | solution.py:189
  451.1 6.7 %collective-permute-start.20 = (f32[2,24,18,1]{1,3,2,0:T(1,128)S(1)}, f32[2,24,18,1]{1,3,2,0:T(1,128)S(1)}, u32[]{:S(2)}, u32[]{:S(2)}) collective-permute-start(f32[2,24,18,1]{1,3,2,0:T(1,128)S(1)} %get-tuple-element.48), channel_id=1, source_target_pairs={{1,0},{2,1},{3,2},{4,3},{5,4},{6,5},{7,6},{8,7},{9,8},{10,9},{11,1... | collective-permute-start | bytes 10376 | tf_op jit(solution)/shard_map/ppermute | solution.py:32
  453.2 5.7 %collective-permute-start.21 = (f32[2,24,18,1]{1,3,2,0:T(1,128)S(1)}, f32[2,24,18,1]{1,3,2,0:T(1,128)S(1)}, u32[]{:S(2)}, u32[]{:S(2)}) collective-permute-start(f32[2,24,18,1]{1,3,2,0:T(1,128)S(1)} %get-tuple-element.49), channel_id=1, source_target_pairs={{0,1},{1,2},{2,3},{3,4},{4,5},{5,6},{6,7},{7,8},{8,9},{9,10},{10,1... | collective-permute-start | bytes 10376 | tf_op jit(solution)/shard_map/ppermute | solution.py:30
  460.7 5.6 %collective-permute-start.23 = (f32[2,24,1,8]{1,3,2,0:T(8,128)S(1)}, f32[2,24,1,8]{1,3,2,0:T(8,128)S(1)}, u32[]{:S(2)}, u32[]{:S(2)}) collective-permute-start(f32[2,24,1,8]{1,3,2,0:T(8,128)S(1)} %get-tuple-element.54), channel_id=1, source_target_pairs={{0,32},{32,64},{64,96},{96,128},{128,160},{160,192},{192,224},{1,3... | collective-permute-start | bytes 4616 | tf_op jit(solution)/shard_map/ppermute | solution.py:30
  462.6 5.0 collective-permute-start.22
  468.3 27.4 %collective-permute-start.24 = (f32[2,24,18,1]{1,3,2,0:T(1,128)}, f32[2,24,18,1]{1,3,2,0:T(1,128)S(1)}, u32[]{:S(2)}, u32[]{:S(2)}) collective-permute-start(f32[2,24,18,1]{1,3,2,0:T(1,128)} %get-tuple-element.46), channel_id=1, source_target_pairs={{1,0},{2,1},{3,2},{4,3},{5,4},{6,5},{7,6},{8,7},{9,8},{10,9},{11,1... | collective-permute-start | bytes 10376 | tf_op jit(solution)/shard_map/ppermute | solution.py:32
  470.2 25.5 %collective-permute-start.25 = (f32[2,24,18,1]{1,3,2,0:T(1,128)}, f32[2,24,18,1]{1,3,2,0:T(1,128)}, u32[]{:S(2)}, u32[]{:S(2)}) collective-permute-start(f32[2,24,18,1]{1,3,2,0:T(1,128)} %get-tuple-element.47), channel_id=1, source_target_pairs={{0,1},{1,2},{2,3},{3,4},{4,5},{5,6},{6,7},{7,8},{8,9},{9,10},{10,1... | collective-permute-start | bytes 10376 | tf_op jit(solution)/shard_map/ppermute | solution.py:30
  483.5 31.2 %all-to-all-start.4 = ((f32[32,36,1,128]{3,2,1,0:T(1,128)}), f32[32,36,1,128]{3,2,1,0:T(1,128)S(1)}, u32[]{:S(2)}, u32[]{:S(2)}) async-start(f32[32,36,1,128]{3,2,1,0:T(1,128)} %bitcast.39), calls=%async_computation.4 | async-start | bytes 1179648 | tf_op jit(solution)/shard_map/all_to_all | solution.py:193
  496.6 5.6 %collective-permute-start.27 = (f32[2,24,1,8]{1,3,2,0:T(8,128)S(1)}, f32[2,24,1,8]{1,3,2,0:T(8,128)S(1)}, u32[]{:S(2)}, u32[]{:S(2)}) collective-permute-start(f32[2,24,1,8]{1,3,2,0:T(8,128)S(1)} %get-tuple-element.52), channel_id=1, source_target_pairs={{0,32},{32,64},{64,96},{96,128},{128,160},{160,192},{192,224},{1,3... | collective-permute-start | bytes 4616 | tf_op jit(solution)/shard_map/ppermute | solution.py:30
  503.6 5.9 %collective-permute-start.28 = (f32[2,24,18,1]{1,3,2,0:T(1,128)S(1)}, f32[2,24,18,1]{1,3,2,0:T(1,128)S(1)}, u32[]{:S(2)}, u32[]{:S(2)}) collective-permute-start(f32[2,24,18,1]{1,3,2,0:T(1,128)S(1)} %get-tuple-element.44), channel_id=1, source_target_pairs={{1,0},{2,1},{3,2},{4,3},{5,4},{6,5},{7,6},{8,7},{9,8},{10,9},{11,1... | collective-permute-start | bytes 10376 | tf_op jit(solution)/shard_map/ppermute | solution.py:32
  505.7 5.7 %collective-permute-start.29 = (f32[2,24,18,1]{1,3,2,0:T(1,128)S(1)}, f32[2,24,18,1]{1,3,2,0:T(1,128)S(1)}, u32[]{:S(2)}, u32[]{:S(2)}) collective-permute-start(f32[2,24,18,1]{1,3,2,0:T(1,128)S(1)} %get-tuple-element.45), channel_id=1, source_target_pairs={{0,1},{1,2},{2,3},{3,4},{4,5},{5,6},{6,7},{7,8},{8,9},{9,10},{10,1... | collective-permute-start | bytes 10376 | tf_op jit(solution)/shard_map/ppermute | solution.py:30
  (37 other events, 925.9 us)
Sparse Core Ops, SparseCore 0:
  210.1 217.3 reduce-scatter.1
where the time goes:
time: 537 us; the launch traced here: 531 us
  waiting for transfers between devices  250 us (47%)
  starting transfers between devices  128 us (24%)
  local copies, waits for them, and re-layouts  65.1 us (12%)
  other arithmetic  58.1 us (11%)
  between operations  15.3 us (3%)
  matrix products  13.3 us (2%)
    reduce_scatter x1, waiting for transfers between devices, body(): lax.psum_scatter(partial_value, 'freq', scatter_dimension=3, tiled=True)  203 us
    ppermute x15, starting transfers between devices, padded_2(): lax.ppermute(tail, axis, [(i, (i + 1) % count) for i in range(ends)])  47.1 us
    ppermute x15, starting transfers between devices, padded_2(): lax.ppermute(head, axis, [((i + 1) % count, i) for i in range(ends)])  35.2 us
    add x16, other arithmetic, transport(): return upwind + limiter * (wendroff - upwind)  34 us
    all_to_all x2, waiting for transfers between devices, body(): lax.all_to_all(grouped, 'freq', split_axis=2, concat_axis=0, tiled=True)  18.7 us
    all_to_all x2, starting transfers between devices, body(): lax.all_to_all(grouped, 'freq', split_axis=2, concat_axis=0, tiled=True)  17.7 us
    all_to_all x2, starting transfers between devices, body(): lax.all_to_all(whole, 'freq', split_axis=0, concat_axis=2, tiled=True)  16.9 us
    unnamed x73, local copies, waits for them, and re-layouts  16.6 us
  transfers between devices with their start and end apart: 36, of which 18 were waited for; matrix products, arithmetic and copies ran while one was open for 22% of the time, Pallas kernels for 0%

commit v1 on v0

--- a/solution.py
+++ b/solution.py
@@ -176,20 +176,16 @@
             field_now = substep(
                 extended, current_ext, flag_rows, sea_rows, rate_now, cos_table, sin_table
             )
-        if cycle_index == 0:
-            own_deposit = lax.dynamic_slice_in_dim(deposit_all, freq_index * F_DEV, F_DEV, 0)
-            own_numbers = wavenumber(own_freqs, freq_total)
-            partial_value = stokes_profile(field_now, own_numbers, own_deposit)
-            drift_tile = lax.psum_scatter(partial_value, "freq", scatter_dimension=3, tiled=True)
         grouped = field_now.reshape(F_DEV, DIR, local_rows, freq_count, tile_cols)
         grouped = jnp.transpose(grouped, (0, 1, 3, 2, 4)).reshape(
             F_DEV, DIR, freq_count, local_rows * tile_cols
         )
-        whole = source(
-            lax.all_to_all(grouped, "freq", split_axis=2, concat_axis=0, tiled=True),
-            gain_matrix,
-            quad_matrix,
-        )
+        cells = lax.all_to_all(grouped, "freq", split_axis=2, concat_axis=0, tiled=True)
+        if cycle_index == 0:
+            numbers = wavenumber(jnp.arange(freq_total, dtype=jnp.int32), freq_total)
+            drift_tile = stokes_profile(cells, numbers, deposit_all)
+            drift_tile = drift_tile.reshape(2, LAYERS, local_rows, tile_cols)
+        whole = source(cells, gain_matrix, quad_matrix)
         moved = lax.all_to_all(whole, "freq", split_axis=0, concat_axis=2, tiled=True)
         moved = moved.reshape(F_DEV, DIR, freq_count, local_rows, tile_cols)
         field_now = jnp.transpose(moved, (0, 1, 3, 2, 4)).reshape(F_DEV, DIR, local_rows, grid_cols)

time: 537 us -> 319 us (0.59)
  the two profiles are of different devices: /device:TPU:34 before, /device:TPU:25 now
where the time goes in v1:
time: 319 us; the launch traced here: 316 us
  starting transfers between devices  122 us (38%)
  waiting for transfers between devices  68 us (21%)
  local copies, waits for them, and re-layouts  59.1 us (19%)
  other arithmetic  55.4 us (17%)
  matrix products  8.95 us (3%)
    ppermute x15, starting transfers between devices, padded_2(): lax.ppermute(tail, axis, [(i, (i + 1) % count) for i in range(ends)])  39.9 us
    ppermute x15, starting transfers between devices, padded_2(): lax.ppermute(head, axis, [((i + 1) % count, i) for i in range(ends)])  39.7 us
    ppermute x15, waiting for transfers between devices, padded_2(): lax.ppermute(head, axis, [((i + 1) % count, i) for i in range(ends)])  38.1 us
    add x16, other arithmetic, transport(): return upwind + limiter * (wendroff - upwind)  31.4 us
    all_to_all x2, starting transfers between devices, body(): lax.all_to_all(grouped, 'freq', split_axis=2, concat_axis=0, tiled=True)  16.2 us
    all_to_all x2, starting transfers between devices, body(): lax.all_to_all(whole, 'freq', split_axis=0, concat_axis=2, tiled=True)  15.7 us
    all_to_all x2, waiting for transfers between devices, body(): lax.all_to_all(grouped, 'freq', split_axis=2, concat_axis=0, tiled=True)  14.5 us
    unnamed x69, local copies, waits for them, and re-layouts  12.8 us
  transfers between devices with their start and end apart: 35, of which 17 were waited for; matrix products, arithmetic and copies ran while one was open for 34% of the time, Pallas kernels for 0%

profile of v1, /device:TPU:25, one launch (start us, length us, event | category | flops | bytes accessed | tf_op | source)
XLA Modules:
  0.0 315.8 jit_solution(5259480364146558789)
XLA Ops:
  4.7 3.0 collective-permute-start.19
  9.8 11.0 %all-to-all-start = ((f32[32,1,256]{2,1,0:T(1,128)}), f32[32,1,256]{2,1,0:T(1,128)S(1)}, u32[]{:S(2)}, u32[]{:S(2)}) async-start(f32[32,1,256]{2,1,0:T(1,128)} %reshape.1834), calls=%async_computation | async-start | bytes 65536 | tf_op jit(solution)/shard_map/all_to_all | solution.py:159
  20.8 3.0 copy.288
  49.4 3.9 %fusion.79 = f32[1,36,17,256]{1,3,2,0:T(8,128)S(1)} fusion(f32[1,36,1,256]{1,3,2,0:T(8,128)S(1)} %collective-permute-done.3, f32[1,36,16,256]{1,3,2,0:T(8,128)} %copy.288, f32[1,36,1,256]{1,3,2,0:T(8,128)} %collective-permute-done.2, f32[17,256]{1,0:T(8,128)S(1)} %slice_bitcast_fusion.7, f32[17,256]{1,0:T(8,128)S(1)} %bitcast.169, f32[36]{0:T(128)} %fusion.239), kind=kLoop, calls=%fused_computation.91 | loop fusion | flops 2820096 | bytes 1325200 | tf_op jit(solution)/shard_map/add | solution.py:62
  61.6 3.1 collective-permute-done.5
  74.3 3.1 collective-permute-done.7
  86.2 3.8 %collective-permute-done.9 = f32[1,36,1,256]{1,3,2,0:T(8,128)S(1)} collective-permute-done((f32[1,36,1,256]{1,3,2,0:T(8,128)S(1)}, f32[1,36,1,256]{1,3,2,0:T(8,128)S(1)}, u32[]{:S(2)}, u32[]{:S(2)}) %collective-permute-start.9) | collective-permute-done | bytes 36896 | tf_op jit(solution)/shard_map/ppermute | solution.py:32
  95.4 3.5 %copy.290 = f32[1,36,32,128]{3,0,1,2:T(1,128)} copy(f32[1,36,32,128]{1,3,2,0:T(8,128)} %copy_bitcast_fusion.3) | data formatting | bytes 1179648 | tf_op jit(solution)/shard_map/reshape | solution.py:180
  98.9 9.2 %all-to-all-start.1 = ((f32[1,36,32,128]{3,0,1,2:T(1,128)}), f32[1,36,32,128]{3,0,1,2:T(1,128)S(1)}, u32[]{:S(2)}, u32[]{:S(2)}) async-start(f32[1,36,32,128]{3,0,1,2:T(1,128)} %copy.290), calls=%async_computation.1 | async-start | bytes 1179648 | tf_op jit(solution)/shard_map/all_to_all | solution.py:183
  109.0 14.5 %all-to-all-done.1 = f32[1,36,32,128]{3,0,1,2:T(1,128)S(1)} async-done(((f32[1,36,32,128]{3,0,1,2:T(1,128)}), f32[1,36,32,128]{3,0,1,2:T(1,128)S(1)}, u32[]{:S(2)}, u32[]{:S(2)}) %all-to-all-start.1) | async-done | bytes 589856 | tf_op jit(solution)/shard_map/all_to_all | solution.py:183
  135.0 6.8 %all-to-all-start.2 = ((f32[32,36,1,128]{3,2,1,0:T(1,128)}), f32[32,36,1,128]{3,2,1,0:T(1,128)}, u32[]{:S(2)}, u32[]{:S(2)}) async-start(f32[32,36,1,128]{3,2,1,0:T(1,128)} %bitcast.158), calls=%async_computation.2 | async-start | bytes 1179648 | tf_op jit(solution)/shard_map/all_to_all | solution.py:189
  148.0 9.7 %all-to-all-done.2 = f32[32,36,1,128]{3,2,1,0:T(1,128)} async-done(((f32[32,36,1,128]{3,2,1,0:T(1,128)}), f32[32,36,1,128]{3,2,1,0:T(1,128)}, u32[]{:S(2)}, u32[]{:S(2)}) %all-to-all-start.2) | async-done | bytes 589856 | tf_op jit(solution)/shard_map/all_to_all | solution.py:189
  157.7 3.5 %copy.296 = f32[32,36,1,128]{1,3,0,2:T(8,128)} copy(f32[32,36,1,128]{3,2,1,0:T(1,128)} %all-to-all-done.2) | data formatting | bytes 1179648 | tf_op jit(solution)/shard_map/all_to_all | solution.py:189
  163.0 6.1 %collective-permute-start.10 = (f32[1,36,1,256]{1,3,2,0:T(8,128)S(1)}, f32[1,36,1,256]{1,3,2,0:T(8,128)S(1)}, u32[]{:S(2)}, u32[]{:S(2)}) collective-permute-start(f32[1,36,1,256]{1,3,2,0:T(8,128)S(1)} %get-tuple-element.22), channel_id=1, source_target_pairs={{0,32},{32,64},{64,96},{96,128},{128,160},{160,192},{192,224},{1,3... | collective-permute-start | bytes 110600 | tf_op jit(solution)/shard_map/ppermute | solution.py:30
  171.5 3.8 %collective-permute-done.11 = f32[1,36,1,256]{1,3,2,0:T(8,128)S(1)} collective-permute-done((f32[1,36,1,256]{1,3,2,0:T(8,128)S(1)}, f32[1,36,1,256]{1,3,2,0:T(8,128)S(1)}, u32[]{:S(2)}, u32[]{:S(2)}) %collective-permute-start.11) | collective-permute-done | bytes 36896 | tf_op jit(solution)/shard_map/ppermute | solution.py:32
  184.7 3.8 %collective-permute-done.13 = f32[1,36,1,256]{1,3,2,0:T(8,128)S(1)} collective-permute-done((f32[1,36,1,256]{1,3,2,0:T(8,128)S(1)}, f32[1,36,1,256]{1,3,2,0:T(8,128)S(1)}, u32[]{:S(2)}, u32[]{:S(2)}) %collective-permute-start.13) | collective-permute-done | bytes 36896 | tf_op jit(solution)/shard_map/ppermute | solution.py:32
  199.3 3.6 %collective-permute-done.15 = f32[1,36,1,256]{1,3,2,0:T(8,128)S(1)} collective-permute-done((f32[1,36,1,256]{1,3,2,0:T(8,128)S(1)}, f32[1,36,1,256]{1,3,2,0:T(8,128)S(1)}, u32[]{:S(2)}, u32[]{:S(2)}) %collective-permute-start.15) | collective-permute-done | bytes 36896 | tf_op jit(solution)/shard_map/ppermute | solution.py:32
  202.9 3.8 %fusion.103 = f32[1,36,17,256]{1,3,2,0:T(8,128)S(1)} fusion(f32[1,36,1,256]{1,3,2,0:T(8,128)S(1)} %collective-permute-done.15, f32[1,36,16,256]{1,3,2,0:T(8,128)} %copy-done.2, f32[1,36,1,256]{1,3,2,0:T(8,128)S(1)} %collective-permute-done.14, f32[17,256]{1,0:T(8,128)S(1)} %slice_bitcast_fusion.1, f32[17,256]{1,0:T(8,128)S(1)} %bitcast.175, f32[36]{0:T(128)S(1)} %copy-done.28), kind=kLoop, calls=%fused_computation.115 | loop fusion | flops 2820096 | bytes 1325200 | tf_op jit(solution)/shard_map/add | solution.py:62
  215.0 3.2 collective-permute-done.17
  224.1 3.5 %copy.299 = f32[1,36,32,128]{3,0,1,2:T(1,128)} copy(f32[1,36,32,128]{1,3,2,0:T(8,128)} %copy_bitcast_fusion.1) | data formatting | bytes 1179648 | tf_op jit(solution)/shard_map/reshape | solution.py:180
  227.6 7.0 %all-to-all-start.3 = ((f32[1,36,32,128]{3,0,1,2:T(1,128)}), f32[1,36,32,128]{3,0,1,2:T(1,128)S(1)}, u32[]{:S(2)}, u32[]{:S(2)}) async-start(f32[1,36,32,128]{3,0,1,2:T(1,128)} %copy.299), calls=%async_computation.3 | async-start | bytes 1179648 | tf_op jit(solution)/shard_map/all_to_all | solution.py:183
  236.9 4.6 %collective-permute-start.20 = (f32[2,24,18,1]{1,3,2,0:T(1,128)S(1)}, f32[2,24,18,1]{1,3,2,0:T(1,128)S(1)}, u32[]{:S(2)}, u32[]{:S(2)}) collective-permute-start(f32[2,24,18,1]{1,3,2,0:T(1,128)S(1)} %get-tuple-element.46), channel_id=1, source_target_pairs={{1,0},{2,1},{3,2},{4,3},{5,4},{6,5},{7,6},{8,7},{9,8},{10,9},{11,1... | collective-permute-start | bytes 10376 | tf_op jit(solution)/shard_map/ppermute | solution.py:32
  244.3 3.8 %collective-permute-done.20 = f32[2,24,18,1]{1,3,2,0:T(1,128)S(1)} collective-permute-done((f32[2,24,18,1]{1,3,2,0:T(1,128)S(1)}, f32[2,24,18,1]{1,3,2,0:T(1,128)S(1)}, u32[]{:S(2)}, u32[]{:S(2)}) %collective-permute-start.20) | collective-permute-done | bytes 3488 | tf_op jit(solution)/shard_map/ppermute | solution.py:32
  250.5 4.8 %collective-permute-start.23 = (f32[2,24,1,8]{1,3,2,0:T(8,128)S(1)}, f32[2,24,1,8]{1,3,2,0:T(8,128)S(1)}, u32[]{:S(2)}, u32[]{:S(2)}) collective-permute-start(f32[2,24,1,8]{1,3,2,0:T(8,128)S(1)} %get-tuple-element.52), channel_id=1, source_target_pairs={{0,32},{32,64},{64,96},{96,128},{128,160},{160,192},{192,224},{1,3... | collective-permute-start | bytes 4616 | tf_op jit(solution)/shard_map/ppermute | solution.py:30
  260.9 3.1 collective-permute-start.24
  275.5 8.9 %all-to-all-start.4 = ((f32[32,36,1,128]{3,2,1,0:T(1,128)}), f32[32,36,1,128]{3,2,1,0:T(1,128)S(1)}, u32[]{:S(2)}, u32[]{:S(2)}) async-start(f32[32,36,1,128]{3,2,1,0:T(1,128)} %bitcast.39), calls=%async_computation.4 | async-start | bytes 1179648 | tf_op jit(solution)/shard_map/all_to_all | solution.py:189
  286.3 3.1 collective-permute-start.27
  291.3 3.3 %collective-permute-done.26 = f32[2,24,1,8]{1,3,2,0:T(8,128)S(1)} collective-permute-done((f32[2,24,1,8]{1,3,2,0:T(8,128)S(1)}, f32[2,24,1,8]{1,3,2,0:T(8,128)S(1)}, u32[]{:S(2)}, u32[]{:S(2)}) %collective-permute-start.26) | collective-permute-done | bytes 1568 | tf_op jit(solution)/shard_map/ppermute | solution.py:32
  294.7 4.6 %collective-permute-start.28 = (f32[2,24,18,1]{1,3,2,0:T(1,128)S(1)}, f32[2,24,18,1]{1,3,2,0:T(1,128)S(1)}, u32[]{:S(2)}, u32[]{:S(2)}) collective-permute-start(f32[2,24,18,1]{1,3,2,0:T(1,128)S(1)} %get-tuple-element.42), channel_id=1, source_target_pairs={{1,0},{2,1},{3,2},{4,3},{5,4},{6,5},{7,6},{8,7},{9,8},{10,9},{11,1... | collective-permute-start | bytes 10376 | tf_op jit(solution)/shard_map/ppermute | solution.py:32
  301.2 4.7 %collective-permute-done.29 = f32[2,24,18,1]{1,3,2,0:T(1,128)S(1)} collective-permute-done((f32[2,24,18,1]{1,3,2,0:T(1,128)S(1)}, f32[2,24,18,1]{1,3,2,0:T(1,128)S(1)}, u32[]{:S(2)}, u32[]{:S(2)}) %collective-permute-start.29) | collective-permute-done | bytes 3488 | tf_op jit(solution)/shard_map/ppermute | solution.py:30
  309.5 3.2 %copy_bitcast_fusion = f32[1,36,16,256]{1,3,2,0:T(8,128)} fusion(f32[32,36,1,128]{1,3,0,2:T(8,128)} %copy.305), kind=kLoop, calls=%fused_computation.226 | loop fusion | bytes 1179648 | tf_op jit(solution)/shard_map/reshape | solution.py:191
  312.7 3.1 copy.309
  (239 shorter events, 154.1 us)
Async XLA Ops:
  2.1 232.4 %collective-permute-start.18 = (f32[2,24,1,8]{1,3,2,0:T(8,128)}, f32[2,24,1,8]{1,3,2,0:T(8,128)}, u32[]{:S(2)}, u32[]{:S(2)}) collective-permute-start(f32[2,24,1,8]{1,3,2,0:T(8,128)} %get-tuple-element.56), channel_id=1, source_target_pairs={{32,0},{64,32},{96,64},{128,96},{160,128},{192,160},{224,192},{33,... | collective-permute-start | bytes 4616 | tf_op jit(solution)/shard_map/ppermute | solution.py:32
  4.7 141.5 %collective-permute-start.19 = (f32[2,24,1,8]{1,3,2,0:T(8,128)}, f32[2,24,1,8]{1,3,2,0:T(8,128)}, u32[]{:S(2)}, u32[]{:S(2)}) collective-permute-start(f32[2,24,1,8]{1,3,2,0:T(8,128)} %get-tuple-element.57), channel_id=1, source_target_pairs={{0,32},{32,64},{64,96},{96,128},{128,160},{160,192},{192,224},{1,3... | collective-permute-start | bytes 4616 | tf_op jit(solution)/shard_map/ppermute | solution.py:30
  9.8 24.1 %all-to-all-start = ((f32[32,1,256]{2,1,0:T(1,128)}), f32[32,1,256]{2,1,0:T(1,128)S(1)}, u32[]{:S(2)}, u32[]{:S(2)}) async-start(f32[32,1,256]{2,1,0:T(1,128)} %reshape.1834), calls=%async_computation | async-start | bytes 65536 | tf_op jit(solution)/shard_map/all_to_all | solution.py:159
  25.5 21.4 %collective-permute-start.2 = (f32[1,36,1,256]{1,3,2,0:T(8,128)}, f32[1,36,1,256]{1,3,2,0:T(8,128)}, u32[]{:S(2)}, u32[]{:S(2)}) collective-permute-start(f32[1,36,1,256]{1,3,2,0:T(8,128)} %get-tuple-element.30), channel_id=1, source_target_pairs={{0,32},{32,64},{64,96},{96,128},{128,160},{160,192},{192,224},{1,3... | collective-permute-start | bytes 110600 | tf_op jit(solution)/shard_map/ppermute | solution.py:30
  36.1 6.1 %collective-permute-start = (f32[1,2,1,256]{2,3,1,0:T(8,128)}, f32[1,2,1,256]{2,3,1,0:T(8,128)}, u32[]{:S(2)}, u32[]{:S(2)}) collective-permute-start(f32[1,2,1,256]{2,3,1,0:T(8,128)} %get-tuple-element.40), channel_id=1, source_target_pairs={{0,32},{32,64},{64,96},{96,128},{128,160},{160,192},{192,224},{1,3... | collective-permute-start | bytes 6152 | tf_op jit(solution)/shard_map/ppermute | solution.py:30
  38.6 7.9 %collective-permute-start.1 = (f32[1,2,1,256]{2,3,1,0:T(8,128)}, f32[1,2,1,256]{2,3,1,0:T(8,128)S(1)}, u32[]{:S(2)}, u32[]{:S(2)}) collective-permute-start(f32[1,2,1,256]{2,3,1,0:T(8,128)} %get-tuple-element.41), channel_id=1, source_target_pairs={{32,0},{64,32},{96,64},{128,96},{160,128},{192,160},{224,192},{33,... | collective-permute-start | bytes 6152 | tf_op jit(solution)/shard_map/ppermute | solution.py:32
  42.2 7.2 %collective-permute-start.3 = (f32[1,36,1,256]{1,3,2,0:T(8,128)}, f32[1,36,1,256]{1,3,2,0:T(8,128)S(1)}, u32[]{:S(2)}, u32[]{:S(2)}) collective-permute-start(f32[1,36,1,256]{1,3,2,0:T(8,128)} %get-tuple-element.31), channel_id=1, source_target_pairs={{32,0},{64,32},{96,64},{128,96},{160,128},{192,160},{224,192},{33,... | collective-permute-start | bytes 110600 | tf_op jit(solution)/shard_map/ppermute | solution.py:32
  56.4 5.1 %collective-permute-start.4 = (f32[1,36,1,256]{1,3,2,0:T(8,128)S(1)}, f32[1,36,1,256]{1,3,2,0:T(8,128)S(1)}, u32[]{:S(2)}, u32[]{:S(2)}) collective-permute-start(f32[1,36,1,256]{1,3,2,0:T(8,128)S(1)} %get-tuple-element.28), channel_id=1, source_target_pairs={{0,32},{32,64},{64,96},{96,128},{128,160},{160,192},{192,224},{1,3... | collective-permute-start | bytes 110600 | tf_op jit(solution)/shard_map/ppermute | solution.py:30
  58.4 6.3 %collective-permute-start.5 = (f32[1,36,1,256]{1,3,2,0:T(8,128)S(1)}, f32[1,36,1,256]{1,3,2,0:T(8,128)S(1)}, u32[]{:S(2)}, u32[]{:S(2)}) collective-permute-start(f32[1,36,1,256]{1,3,2,0:T(8,128)S(1)} %get-tuple-element.29), channel_id=1, source_target_pairs={{32,0},{64,32},{96,64},{128,96},{160,128},{192,160},{224,192},{33,... | collective-permute-start | bytes 110600 | tf_op jit(solution)/shard_map/ppermute | solution.py:32
  69.1 5.1 %collective-permute-start.6 = (f32[1,36,1,256]{1,3,2,0:T(8,128)S(1)}, f32[1,36,1,256]{1,3,2,0:T(8,128)S(1)}, u32[]{:S(2)}, u32[]{:S(2)}) collective-permute-start(f32[1,36,1,256]{1,3,2,0:T(8,128)S(1)} %get-tuple-element.26), channel_id=1, source_target_pairs={{0,32},{32,64},{64,96},{96,128},{128,160},{160,192},{192,224},{1,3... | collective-permute-start | bytes 110600 | tf_op jit(solution)/shard_map/ppermute | solution.py:30
  71.0 6.3 %collective-permute-start.7 = (f32[1,36,1,256]{1,3,2,0:T(8,128)S(1)}, f32[1,36,1,256]{1,3,2,0:T(8,128)S(1)}, u32[]{:S(2)}, u32[]{:S(2)}) collective-permute-start(f32[1,36,1,256]{1,3,2,0:T(8,128)S(1)} %get-tuple-element.27), channel_id=1, source_target_pairs={{32,0},{64,32},{96,64},{128,96},{160,128},{192,160},{224,192},{33,... | collective-permute-start | bytes 110600 | tf_op jit(solution)/shard_map/ppermute | solution.py:32
  83.7 6.3 %collective-permute-start.9 = (f32[1,36,1,256]{1,3,2,0:T(8,128)S(1)}, f32[1,36,1,256]{1,3,2,0:T(8,128)S(1)}, u32[]{:S(2)}, u32[]{:S(2)}) collective-permute-start(f32[1,36,1,256]{1,3,2,0:T(8,128)S(1)} %get-tuple-element.25), channel_id=1, source_target_pairs={{32,0},{64,32},{96,64},{128,96},{160,128},{192,160},{224,192},{33,... | collective-permute-start | bytes 110600 | tf_op jit(solution)/shard_map/ppermute | solution.py:32
  98.9 24.6 %all-to-all-start.1 = ((f32[1,36,32,128]{3,0,1,2:T(1,128)}), f32[1,36,32,128]{3,0,1,2:T(1,128)S(1)}, u32[]{:S(2)}, u32[]{:S(2)}) async-start(f32[1,36,32,128]{3,0,1,2:T(1,128)} %copy.290), calls=%async_computation.1 | async-start | bytes 1179648 | tf_op jit(solution)/shard_map/all_to_all | solution.py:183
  135.0 22.7 %all-to-all-start.2 = ((f32[32,36,1,128]{3,2,1,0:T(1,128)}), f32[32,36,1,128]{3,2,1,0:T(1,128)}, u32[]{:S(2)}, u32[]{:S(2)}) async-start(f32[32,36,1,128]{3,2,1,0:T(1,128)} %bitcast.158), calls=%async_computation.2 | async-start | bytes 1179648 | tf_op jit(solution)/shard_map/all_to_all | solution.py:189
  163.0 8.5 %collective-permute-start.10 = (f32[1,36,1,256]{1,3,2,0:T(8,128)S(1)}, f32[1,36,1,256]{1,3,2,0:T(8,128)S(1)}, u32[]{:S(2)}, u32[]{:S(2)}) collective-permute-start(f32[1,36,1,256]{1,3,2,0:T(8,128)S(1)} %get-tuple-element.22), channel_id=1, source_target_pairs={{0,32},{32,64},{64,96},{96,128},{128,160},{160,192},{192,224},{1,3... | collective-permute-start | bytes 110600 | tf_op jit(solution)/shard_map/ppermute | solution.py:30
  169.1 6.3 %collective-permute-start.11 = (f32[1,36,1,256]{1,3,2,0:T(8,128)S(1)}, f32[1,36,1,256]{1,3,2,0:T(8,128)S(1)}, u32[]{:S(2)}, u32[]{:S(2)}) collective-permute-start(f32[1,36,1,256]{1,3,2,0:T(8,128)S(1)} %get-tuple-element.23), channel_id=1, source_target_pairs={{32,0},{64,32},{96,64},{128,96},{160,128},{192,160},{224,192},{33,... | collective-permute-start | bytes 110600 | tf_op jit(solution)/shard_map/ppermute | solution.py:32
  182.2 6.3 %collective-permute-start.13 = (f32[1,36,1,256]{1,3,2,0:T(8,128)S(1)}, f32[1,36,1,256]{1,3,2,0:T(8,128)S(1)}, u32[]{:S(2)}, u32[]{:S(2)}) collective-permute-start(f32[1,36,1,256]{1,3,2,0:T(8,128)S(1)} %get-tuple-element.21), channel_id=1, source_target_pairs={{32,0},{64,32},{96,64},{128,96},{160,128},{192,160},{224,192},{33,... | collective-permute-start | bytes 110600 | tf_op jit(solution)/shard_map/ppermute | solution.py:32
  196.6 6.3 %collective-permute-start.15 = (f32[1,36,1,256]{1,3,2,0:T(8,128)S(1)}, f32[1,36,1,256]{1,3,2,0:T(8,128)S(1)}, u32[]{:S(2)}, u32[]{:S(2)}) collective-permute-start(f32[1,36,1,256]{1,3,2,0:T(8,128)S(1)} %get-tuple-element.19), channel_id=1, source_target_pairs={{32,0},{64,32},{96,64},{128,96},{160,128},{192,160},{224,192},{33,... | collective-permute-start | bytes 110600 | tf_op jit(solution)/shard_map/ppermute | solution.py:32
  210.0 5.1 %collective-permute-start.16 = (f32[1,36,1,256]{1,3,2,0:T(8,128)S(1)}, f32[1,36,1,256]{1,3,2,0:T(8,128)S(1)}, u32[]{:S(2)}, u32[]{:S(2)}) collective-permute-start(f32[1,36,1,256]{1,3,2,0:T(8,128)S(1)} %get-tuple-element.16), channel_id=1, source_target_pairs={{0,32},{32,64},{64,96},{96,128},{128,160},{160,192},{192,224},{1,3... | collective-permute-start | bytes 110600 | tf_op jit(solution)/shard_map/ppermute | solution.py:30
  211.9 6.3 %collective-permute-start.17 = (f32[1,36,1,256]{1,3,2,0:T(8,128)S(1)}, f32[1,36,1,256]{1,3,2,0:T(8,128)S(1)}, u32[]{:S(2)}, u32[]{:S(2)}) collective-permute-start(f32[1,36,1,256]{1,3,2,0:T(8,128)S(1)} %get-tuple-element.17), channel_id=1, source_target_pairs={{32,0},{64,32},{96,64},{128,96},{160,128},{192,160},{224,192},{33,... | collective-permute-start | bytes 110600 | tf_op jit(solution)/shard_map/ppermute | solution.py:32
  227.6 38.6 %all-to-all-start.3 = ((f32[1,36,32,128]{3,0,1,2:T(1,128)}), f32[1,36,32,128]{3,0,1,2:T(1,128)S(1)}, u32[]{:S(2)}, u32[]{:S(2)}) async-start(f32[1,36,32,128]{3,0,1,2:T(1,128)} %copy.299), calls=%async_computation.3 | async-start | bytes 1179648 | tf_op jit(solution)/shard_map/all_to_all | solution.py:183
  236.9 11.2 %collective-permute-start.20 = (f32[2,24,18,1]{1,3,2,0:T(1,128)S(1)}, f32[2,24,18,1]{1,3,2,0:T(1,128)S(1)}, u32[]{:S(2)}, u32[]{:S(2)}) collective-permute-start(f32[2,24,18,1]{1,3,2,0:T(1,128)S(1)} %get-tuple-element.46), channel_id=1, source_target_pairs={{1,0},{2,1},{3,2},{4,3},{5,4},{6,5},{7,6},{8,7},{9,8},{10,9},{11,1... | collective-permute-start | bytes 10376 | tf_op jit(solution)/shard_map/ppermute | solution.py:32
  241.5 7.2 %collective-permute-start.21 = (f32[2,24,18,1]{1,3,2,0:T(1,128)S(1)}, f32[2,24,18,1]{1,3,2,0:T(1,128)S(1)}, u32[]{:S(2)}, u32[]{:S(2)}) collective-permute-start(f32[2,24,18,1]{1,3,2,0:T(1,128)S(1)} %get-tuple-element.47), channel_id=1, source_target_pairs={{0,1},{1,2},{2,3},{3,4},{4,5},{5,6},{6,7},{7,8},{8,9},{9,10},{10,1... | collective-permute-start | bytes 10376 | tf_op jit(solution)/shard_map/ppermute | solution.py:30
  250.5 7.0 %collective-permute-start.23 = (f32[2,24,1,8]{1,3,2,0:T(8,128)S(1)}, f32[2,24,1,8]{1,3,2,0:T(8,128)S(1)}, u32[]{:S(2)}, u32[]{:S(2)}) collective-permute-start(f32[2,24,1,8]{1,3,2,0:T(8,128)S(1)} %get-tuple-element.52), channel_id=1, source_target_pairs={{0,32},{32,64},{64,96},{96,128},{128,160},{160,192},{192,224},{1,3... | collective-permute-start | bytes 4616 | tf_op jit(solution)/shard_map/ppermute | solution.py:30
  255.3 5.0 %collective-permute-start.22 = (f32[2,24,1,8]{1,3,2,0:T(8,128)S(1)}, f32[2,24,1,8]{1,3,2,0:T(8,128)S(1)}, u32[]{:S(2)}, u32[]{:S(2)}) collective-permute-start(f32[2,24,1,8]{1,3,2,0:T(8,128)S(1)} %get-tuple-element.53), channel_id=1, source_target_pairs={{32,0},{64,32},{96,64},{128,96},{160,128},{192,160},{224,192},{33,... | collective-permute-start | bytes 4616 | tf_op jit(solution)/shard_map/ppermute | solution.py:32
  260.9 24.4 %collective-permute-start.24 = (f32[2,24,18,1]{1,3,2,0:T(1,128)}, f32[2,24,18,1]{1,3,2,0:T(1,128)S(1)}, u32[]{:S(2)}, u32[]{:S(2)}) collective-permute-start(f32[2,24,18,1]{1,3,2,0:T(1,128)} %get-tuple-element.44), channel_id=1, source_target_pairs={{1,0},{2,1},{3,2},{4,3},{5,4},{6,5},{7,6},{8,7},{9,8},{10,9},{11,1... | collective-permute-start | bytes 10376 | tf_op jit(solution)/shard_map/ppermute | solution.py:32
  264.0 21.4 %collective-permute-start.25 = (f32[2,24,18,1]{1,3,2,0:T(1,128)}, f32[2,24,18,1]{1,3,2,0:T(1,128)}, u32[]{:S(2)}, u32[]{:S(2)}) collective-permute-start(f32[2,24,18,1]{1,3,2,0:T(1,128)} %get-tuple-element.45), channel_id=1, source_target_pairs={{0,1},{1,2},{2,3},{3,4},{4,5},{5,6},{6,7},{7,8},{8,9},{9,10},{10,1... | collective-permute-start | bytes 10376 | tf_op jit(solution)/shard_map/ppermute | solution.py:30
  275.5 31.2 %all-to-all-start.4 = ((f32[32,36,1,128]{3,2,1,0:T(1,128)}), f32[32,36,1,128]{3,2,1,0:T(1,128)S(1)}, u32[]{:S(2)}, u32[]{:S(2)}) async-start(f32[32,36,1,128]{3,2,1,0:T(1,128)} %bitcast.39), calls=%async_computation.4 | async-start | bytes 1179648 | tf_op jit(solution)/shard_map/all_to_all | solution.py:189
  286.3 5.0 %collective-permute-start.27 = (f32[2,24,1,8]{1,3,2,0:T(8,128)S(1)}, f32[2,24,1,8]{1,3,2,0:T(8,128)S(1)}, u32[]{:S(2)}, u32[]{:S(2)}) collective-permute-start(f32[2,24,1,8]{1,3,2,0:T(8,128)S(1)} %get-tuple-element.50), channel_id=1, source_target_pairs={{0,32},{32,64},{64,96},{96,128},{128,160},{160,192},{192,224},{1,3... | collective-permute-start | bytes 4616 | tf_op jit(solution)/shard_map/ppermute | solution.py:30
  289.4 5.3 %collective-permute-start.26 = (f32[2,24,1,8]{1,3,2,0:T(8,128)S(1)}, f32[2,24,1,8]{1,3,2,0:T(8,128)S(1)}, u32[]{:S(2)}, u32[]{:S(2)}) collective-permute-start(f32[2,24,1,8]{1,3,2,0:T(8,128)S(1)} %get-tuple-element.51), channel_id=1, source_target_pairs={{32,0},{64,32},{96,64},{128,96},{160,128},{192,160},{224,192},{33,... | collective-permute-start | bytes 4616 | tf_op jit(solution)/shard_map/ppermute | solution.py:32
  294.7 6.5 %collective-permute-start.28 = (f32[2,24,18,1]{1,3,2,0:T(1,128)S(1)}, f32[2,24,18,1]{1,3,2,0:T(1,128)S(1)}, u32[]{:S(2)}, u32[]{:S(2)}) collective-permute-start(f32[2,24,18,1]{1,3,2,0:T(1,128)S(1)} %get-tuple-element.42), channel_id=1, source_target_pairs={{1,0},{2,1},{3,2},{4,3},{5,4},{6,5},{7,6},{8,7},{9,8},{10,9},{11,1... | collective-permute-start | bytes 10376 | tf_op jit(solution)/shard_map/ppermute | solution.py:32
  299.3 6.6 %collective-permute-start.29 = (f32[2,24,18,1]{1,3,2,0:T(1,128)S(1)}, f32[2,24,18,1]{1,3,2,0:T(1,128)S(1)}, u32[]{:S(2)}, u32[]{:S(2)}) collective-permute-start(f32[2,24,18,1]{1,3,2,0:T(1,128)S(1)} %get-tuple-element.43), channel_id=1, source_target_pairs={{0,1},{1,2},{2,3},{3,4},{4,5},{5,6},{6,7},{7,8},{8,9},{9,10},{10,1... | collective-permute-start | bytes 10376 | tf_op jit(solution)/shard_map/ppermute | solution.py:30
  (34 other events, 317.0 us)

commit v2 on v1

v2 whole, which is shorter than its diff:
```python
import jax
import jax.numpy as jnp
from jax import lax
from jax.experimental import pallas as pl
from jax.experimental.pallas import tpu as pltpu
from jax.sharding import PartitionSpec as P

DIR = 36
FREQS = 32
COMP = 1152
LAYERS = 24
SUB = 4
CYCLES = 2
OSTEPS = 3
BANDS = 8
ROWS = 16
COLS = 8
HALO = 4
EXT_R = 24
EXT_C = 16
LANES = 128
GROUPS = 9

precise = lax.Precision.HIGHEST
ocean_dt = 0.2
viscous = 0.5
mixing = 0.5
friction = 0.1

SIDES = ((0, 1), (0, -1), (1, 0), (-1, 0), (1, 1), (1, -1), (-1, 1), (-1, -1))
f32 = jnp.float32


def directions(how_many):
    angles = (jnp.arange(how_many, dtype=f32) + 0.5) * (2.0 * jnp.pi / how_many)
    return (jnp.cos(angles), jnp.sin(angles))


def speed_of(position, total_count):
    return 0.5 + 0.3 * (position.astype(f32) + 0.5) / total_count


def wavenumber(position, total_count):
    return 0.5 + 1.5 * (position.astype(f32) + 0.5) / total_count


def deposit_table(stokes_route):
    layer_ids = jnp.arange(LAYERS, dtype=jnp.int32)
    weights = 1.0 / (1.0 + jnp.arange(stokes_route.shape[1], dtype=f32))
    hits = (stokes_route[:, :, None] == layer_ids[None, None, :]).astype(f32)
    return jnp.sum(hits * weights[None, :, None], axis=1)


def sent_rows(side):
    return {0: (0, ROWS), 1: (0, HALO), -1: (ROWS - HALO, ROWS)}[side]


def sent_cols(side):
    return {0: (0, COLS), 1: (0, HALO), -1: (COLS - HALO, COLS)}[side]


def kept_rows(side):
    return {0: HALO, 1: HALO + ROWS, -1: 0}[side]


def kept_cols(side):
    return {0: (0, COLS), 1: (COLS, COLS + HALO), -1: (COLS + HALO, EXT_C)}[side]


def message_shape(side, lanes):
    return (ROWS if side[0] == 0 else HALO, COLS if side[1] == 0 else HALO, lanes)


def exchange(messages):
    received = []
    for (db, dt), message in zip(SIDES, messages):
        pairs = [
            ((b + db) * FREQS + t + dt, b * FREQS + t)
            for b in range(BANDS)
            for t in range(FREQS)
            if 0 <= b + db < BANDS and 0 <= t + dt < FREQS
        ]
        received.append(lax.ppermute(message, ("band", "freq"), pairs))
    return received


def swap_blocks(tiles):
    block = lax.broadcasted_iota(jnp.int32, tiles[0].shape, 1) // 8
    for bit in (1, 2, 4, 8):
        upper = (block & bit) != 0
        fresh = list(tiles)
        for low in range(16):
            if low & bit:
                continue
            high = low | bit
            fresh[low] = jnp.where(upper, pltpu.roll(tiles[high], bit * 8, 1), tiles[low])
            fresh[high] = jnp.where(upper, tiles[high], pltpu.roll(tiles[low], LANES - bit * 8, 1))
        tiles = fresh
    return tiles


def spread_kernel(x_ref, o_ref, half_ref):
    for half in range(2):
        half_ref[half] = x_ref[:, half * LANES : (half + 1) * LANES]
        for first in range(0, DIR, 8):
            count = min(8, DIR - first)
            tiles = [half_ref[half, pl.ds(first * ROWS + r, count, stride=ROWS), :] for r in range(16)]
            for i, tile in enumerate(swap_blocks(tiles)):
                o_ref[half * 16 + i, pl.ds(first, count), :] = tile


def gather_kernel(x_ref, o_ref, half_ref):
    for half in range(2):
        for first in range(0, DIR, 8):
            count = min(8, DIR - first)
            tiles = [x_ref[half * 16 + i, pl.ds(first, count), :] for i in range(16)]
            for r, tile in enumerate(swap_blocks(tiles)):
                half_ref[half, pl.ds(first * ROWS + r, count, stride=ROWS), :] = tile
        o_ref[:, half * LANES : (half + 1) * LANES] = half_ref[half]


def put_messages(value, message_refs, lanes):
    for side, ref in zip(SIDES, message_refs):
        r0, r1 = sent_rows(side[0])
        c0, c1 = sent_cols(side[1])
        ref[:, :, lanes] = value[r0:r1, c0:c1, :]


def unpack_kernel(x_ref, c_ref, *rest):
    message_refs, flat_ref = rest[:-1], rest[-1]
    for g in range(FREQS):
        flat_ref[pl.ds(g * DIR, DIR), :] = x_ref[g]
    for k in range(GROUPS):
        lanes = pl.ds(k * LANES, LANES)
        tile = jnp.transpose(flat_ref[lanes, :]).reshape(ROWS, COLS, LANES)
        c_ref[:, :, lanes] = tile
        put_messages(tile, message_refs, lanes)


def face_flux(lower, upper, half_courant, second):
    q = jnp.where(second, (half_courant + half_courant) * half_courant, jnp.abs(half_courant))
    return lower * (half_courant + q) + upper * (half_courant - q)


def cycle_kernel(first, *refs):
    refs = list(refs)
    take = lambda n: [refs.pop(0) for _ in range(n)]
    (c_ref,) = take(1)
    message_refs = take(8)
    north_ref, east_ref, flag_ref, sea_ref, gain_hbm, quad_hbm = take(6)
    if first:
        weight_hi, weight_lo, out_ref, stokes_ref = take(4)
        out_refs = take(8)
    else:
        (out_ref,) = take(1)
    tile_ref, energy_ref, gain_ref, quad_ref, sems = take(5)
    copies = [
        pltpu.make_async_copy(gain_hbm, gain_ref, sems.at[0]),
        pltpu.make_async_copy(quad_hbm, quad_ref, sems.at[1]),
    ]
    for copy in copies:
        copy.start()

    def advect(k, carry):
        lanes = pl.ds(pl.multiple_of(k * LANES, LANES), LANES)
        tile_ref[HALO : HALO + ROWS, 0:COLS, :] = c_ref[:, :, lanes]
        for side, ref in zip(SIDES, message_refs):
            r0 = kept_rows(side[0])
            c0, c1 = kept_cols(side[1])
            tile_ref[r0 : r0 + ref.shape[0], c0:c1, :] = ref[:, :, lanes]
        for s in range(SUB):
            here = tile_ref[s]
            above = tile_ref[s + 1]
            flag = flag_ref[s, s + 1] != 0.0
            flux_below = face_flux(here, above, north_ref[s, :, lanes], flag)
            for r in range(s + 1, EXT_R - 1 - s):
                here = above
                above = tile_ref[r + 1]
                flag_above = flag_ref[s, r + 1] != 0.0
                flux_above = face_flux(here, above, north_ref[r, :, lanes], flag_above)
                shifted = here - (flux_above - flux_below)
                flux_east = face_flux(
                    pltpu.roll(shifted, 1, 0), shifted, east_ref[r, :, lanes], flag
                )
                result = shifted - (pltpu.roll(flux_east, EXT_C - 1, 0) - flux_east)
                result = result * sea_ref[r]
                if s == SUB - 1:
                    energy_ref[r - HALO, :, lanes] = result[0:COLS]
                else:
                    tile_ref[r] = result
                flux_below = flux_above
                flag = flag_above
        return carry

    lax.fori_loop(0, GROUPS, advect, 0)
    cells = ROWS * COLS
    energy = energy_ref[...].reshape(cells, COMP)
    rounded = energy.astype(jnp.bfloat16)
    squared = (energy * energy).astype(jnp.bfloat16)
    if first:
        rest = (energy - rounded.astype(f32)).astype(jnp.bfloat16)
        mm = lambda a, b: jnp.dot(a, b, preferred_element_type=f32)
        stokes = mm(rounded, weight_hi[...]) + (mm(rest, weight_hi[...]) + mm(rounded, weight_lo[...]))
        stokes = stokes.reshape(ROWS, COLS, LANES)
        stokes_ref[...] = stokes
        put_messages(stokes, out_refs, pl.ds(COMP, LANES))
    for copy in copies:
        copy.wait()
    nt = (((1,), (1,)), ((), ()))
    for k in range(GROUPS):
        lanes = pl.ds(k * LANES, LANES)
        gain = lax.dot_general(rounded, gain_ref[lanes, :], nt, preferred_element_type=f32)
        quartic = lax.dot_general(squared, quad_ref[lanes, :], nt, preferred_element_type=f32)
        before = energy_ref[:, :, lanes].reshape(cells, LANES)
        updated = before * (1.0 + 0.5 * jnp.tanh(gain) - 0.25 * jnp.tanh(quartic))
        if first:
            updated = updated.reshape(ROWS, COLS, LANES)
            out_ref[:, :, lanes] = updated
            put_messages(updated, out_refs, lanes)
        else:
            flat = jnp.transpose(updated)
            start = k * LANES
            while start < (k + 1) * LANES:
                g, d = divmod(start, DIR)
                count = min(DIR - d, (k + 1) * LANES - start)
                at = start - k * LANES
                out_ref[g, d : d + count, :] = flat[at : at + count, :]
                start += count


def ocean_kernel(u_ref, stokes_ref, *refs):
    message_refs, (sea_ref, o_ref, now_ref, drift_ref) = refs[:8], refs[8:]
    now_ref[...] = u_ref[...]
    drift_ref[HALO : HALO + ROWS, 0:COLS, :] = stokes_ref[...]
    for side, ref in zip(SIDES, message_refs):
        r0 = kept_rows(side[0])
        c0, c1 = kept_cols(side[1])
        drift_ref[r0 : r0 + ref.shape[0], c0:c1, :] = ref[...]
    lane = lax.broadcasted_iota(jnp.int32, (EXT_C, LANES), 1)
    used = lane < 2 * LAYERS
    east = lane < LAYERS
    top = (lane == LAYERS - 1) | (lane == 2 * LAYERS - 1)
    bottom = (lane == 0) | (lane == LAYERS)
    for s in range(OSTEPS):
        low = 2 + s
        below = now_ref[low - 1]
        here = now_ref[low]
        for r in range(low, EXT_R - low):
            above = now_ref[r + 1]
            laplace = above + below + pltpu.roll(here, EXT_C - 1, 0) + pltpu.roll(here, 1, 0) - 4.0 * here
            moving = here + drift_ref[r]
            turning = jnp.where(
                east, pltpu.roll(moving, LANES - LAYERS, 1), -pltpu.roll(moving, LAYERS, 1)
            )
            over = jnp.where(top, 0.0, pltpu.roll(here, LANES - 1, 1))
            under = jnp.where(bottom, 0.0, pltpu.roll(here, 1, 1))
            tendency = (
                viscous * laplace + turning + mixing * (over + under - 2.0 * here) - friction * here
            )
            result = jnp.where(used, (here + ocean_dt * tendency) * sea_ref[r], 0.0)
            if s == OSTEPS - 1:
                o_ref[r - HALO] = result[0:COLS]
            else:
                now_ref[r] = result
            below, here = here, above


def shape_of(*dims, dtype=f32):
    return jax.ShapeDtypeStruct(dims, dtype)


vmem = pl.BlockSpec(memory_space=pltpu.VMEM)
hbm = pl.BlockSpec(memory_space=pl.ANY)
big = pltpu.CompilerParams(vmem_limit_bytes=40 * 2**20)


def spread(x):
    return pl.pallas_call(
        spread_kernel,
        out_shape=shape_of(FREQS, DIR, LANES),
        in_specs=[vmem],
        out_specs=vmem,
        scratch_shapes=[pltpu.VMEM((2, DIR * ROWS, LANES), f32)],
        name="spread",
    )(x.reshape(DIR * ROWS, 2 * LANES))


def collect(x):
    return pl.pallas_call(
        gather_kernel,
        out_shape=shape_of(DIR * ROWS, 2 * LANES),
        in_specs=[vmem],
        out_specs=vmem,
        scratch_shapes=[pltpu.VMEM((2, DIR * ROWS, LANES), f32)],
        name="collect",
    )(x).reshape(1, DIR, ROWS, 2 * LANES)


def unpack(x):
    out = pl.pallas_call(
        unpack_kernel,
        out_shape=[shape_of(ROWS, COLS, COMP)] + [shape_of(*message_shape(s, COMP)) for s in SIDES],
        in_specs=[vmem],
        out_specs=[vmem] * 9,
        scratch_shapes=[pltpu.VMEM((COMP, LANES), f32)],
        name="unpack",
    )(x)
    return out[0], out[1:]


def run_cycle(first, cells, halos, north, east, flags, sea, gain, quad, weights):
    operands = [cells, *halos, north, east, flags, sea, gain, quad]
    if first:
        operands += weights
        out_shape = [shape_of(ROWS, COLS, COMP), shape_of(ROWS, COLS, LANES)]
        out_shape += [shape_of(*message_shape(s, COMP + LANES)) for s in SIDES]
    else:
        out_shape = [shape_of(FREQS, DIR, LANES)]
    specs = [vmem] * len(operands)
    specs[13] = hbm
    specs[14] = hbm
    return pl.pallas_call(
        lambda *refs: cycle_kernel(first, *refs),
        out_shape=out_shape,
        in_specs=specs,
        out_specs=[vmem] * len(out_shape),
        scratch_shapes=[
            pltpu.VMEM((EXT_R, EXT_C, LANES), f32),
            pltpu.VMEM((ROWS, COLS, COMP), f32),
            pltpu.VMEM((COMP, COMP), jnp.bfloat16),
            pltpu.VMEM((COMP, COMP), jnp.bfloat16),
            pltpu.SemaphoreType.DMA((2,)),
        ],
        compiler_params=big,
        name="cycle_first" if first else "cycle_last",
    )(*operands)


def ocean(velocity_ext, stokes, halos, sea):
    operands = [velocity_ext, stokes, *halos, sea]
    return pl.pallas_call(
        ocean_kernel,
        out_shape=shape_of(ROWS, COLS, LANES),
        in_specs=[vmem] * len(operands),
        out_specs=vmem,
        scratch_shapes=[pltpu.VMEM((EXT_R, EXT_C, LANES), f32)] * 2,
        name="ocean",
    )(*operands)


def line(count, shift):
    return [(i, i - shift) for i in range(count) if 0 <= i - shift < count]


def body(
    spectrum,
    velocity,
    gain_matrix,
    quad_matrix,
    limiter_flags,
    sea_mask,
    current_route,
    stokes_route,
):
    band_index = lax.axis_index("band")
    freq_index = lax.axis_index("freq")
    chunks = lax.all_to_all(spread(spectrum), "freq", split_axis=0, concat_axis=0, tiled=True)

    tile = jnp.transpose(velocity, (2, 3, 0, 1)).reshape(ROWS, COLS, 2 * LAYERS)
    from_next = lax.ppermute(tile[:, :HALO], "freq", line(FREQS, 1))
    from_last = lax.ppermute(tile[:, HALO:], "freq", line(FREQS, -1))
    wide = jnp.concatenate([tile, from_next, from_last], axis=1)
    from_up = lax.ppermute(wide[:HALO], "band", line(BANDS, 1))
    from_down = lax.ppermute(wide[-HALO:], "band", line(BANDS, -1))
    velocity_ext = jnp.concatenate([from_down, wide, from_up], axis=0)

    drift = 0.15 * jnp.tanh(velocity_ext)
    drift_east = drift[..., :LAYERS]
    drift_north = drift[..., LAYERS:]
    half_east = 0.25 * (drift_east + jnp.roll(drift_east, 1, axis=1))
    half_north = 0.25 * (drift_north + jnp.roll(drift_north, -1, axis=0))
    layer_ids = jnp.arange(LAYERS, dtype=jnp.int32)
    routes = jnp.repeat(current_route, DIR)
    picker = (layer_ids[:, None] == routes[None, :]).astype(f32)
    cos_table, sin_table = directions(DIR)
    speeds = speed_of(jnp.arange(FREQS, dtype=jnp.int32), FREQS)
    half_cos = 0.5 * (speeds[:, None] * cos_table[None, :]).reshape(COMP)
    half_sin = 0.5 * (speeds[:, None] * sin_table[None, :]).reshape(COMP)
    pick = lambda x: jnp.einsum("rcl,lk->rck", x, picker, precision=precise)
    north = half_sin + pick(half_north)
    east = half_cos + pick(half_east)

    def window(grid):
        padded = jnp.pad(grid, ((0, 0), (HALO, HALO), (HALO, HALO))).astype(f32)
        part = lax.dynamic_slice(
            padded,
            (0, band_index * ROWS, freq_index * COLS),
            (grid.shape[0], EXT_R, EXT_C),
        )
        part = jnp.concatenate([part[:, :, HALO:], part[:, :, :HALO]], axis=2)
        return jnp.broadcast_to(part[..., None], part.shape + (LANES,))

    flags = window(limiter_flags)
    sea = window(sea_mask[None])[0]

    numbers = wavenumber(jnp.arange(FREQS, dtype=jnp.int32), FREQS) * DIR ** (-0.5)
    deposit = deposit_table(stokes_route) * numbers[:, None]
    both = jnp.stack([cos_table, sin_table])
    weight = (both.T[None, :, :, None] * deposit[:, None, None, :]).reshape(COMP, 2 * LAYERS)
    weight = jnp.pad(weight, ((0, 0), (0, LANES - 2 * LAYERS)))
    weight_hi = lax.reduce_precision(weight, 8, 7)
    weight_lo = (weight - weight_hi).astype(jnp.bfloat16)
    weights = [weight_hi.astype(jnp.bfloat16), weight_lo]

    cells, messages = unpack(chunks)
    halos = exchange(messages)
    results = run_cycle(
        True, cells, halos, north, east, flags[:SUB], sea, gain_matrix, quad_matrix, weights
    )
    cells, stokes, messages = results[0], results[1], results[2:]
    halos = exchange(messages)
    (chunks,) = run_cycle(
        False, cells, halos, north, east, flags[SUB:], sea, gain_matrix, quad_matrix, None
    )
    chunks = lax.all_to_all(chunks, "freq", split_axis=0, concat_axis=0, tiled=True)
    velocity_wide = jnp.pad(velocity_ext, ((0, 0), (0, 0), (0, LANES - 2 * LAYERS)))
    ocean_out = ocean(velocity_wide, stokes, [h[:, :, COMP:] for h in halos], sea)
    ocean_out = ocean_out[:, :, : 2 * LAYERS].reshape(ROWS, COLS, 2, LAYERS)
    velocity_out = jnp.transpose(ocean_out, (2, 3, 0, 1))
    return (collect(chunks), velocity_out)


def solution(mesh):
    return jax.shard_map(
        body,
        mesh=mesh,
        in_specs=(
            P("freq", None, "band", None),
            P(None, None, "band", "freq"),
            P(),
            P(),
            P(),
            P(),
            P(),
            P(),
        ),
        out_specs=(P("freq", None, "band", None), P(None, None, "band", "freq")),
        check_vma=False,
    )
```

time: 319 us -> 162 us (0.51)
  the two profiles are of different devices: /device:TPU:25 before, /device:TPU:34 now
where the time goes in v2:
time: 162 us; the launch traced here: 161 us
  starting transfers between devices  86.7 us (54%)
  Pallas kernels  29 us (18%)
  waiting for transfers between devices  27.3 us (17%)
  local copies, waits for them, and re-layouts  13.8 us (9%)
  matrix products  1.75 us (1%)
    ppermute x16, starting transfers between devices, exchange(): received.append(lax.ppermute(message, ('band', 'freq'), pairs))  48.7 us
    pallas_call x2, Pallas kernels, run_cycle(): pl.pallas_call(lambda *refs: cycle_kernel(first, *refs), out_shape=out_sh...  16.7 us
    all_to_all x1, starting transfers between devices, body(): lax.all_to_all(chunks, 'freq', split_axis=0, concat_axis=0, tiled=True)  14.5 us
    all_to_all x1, starting transfers between devices, body(): lax.all_to_all(spread(spectrum), 'freq', split_axis=0, concat_axis=0, til...  12.1 us
    all_to_all x1, waiting for transfers between devices, body(): lax.all_to_all(chunks, 'freq', split_axis=0, concat_axis=0, tiled=True)  11.6 us
    all_to_all x1, waiting for transfers between devices, body(): lax.all_to_all(spread(spectrum), 'freq', split_axis=0, concat_axis=0, til...  10.7 us
    slice x8, local copies, waits for them, and re-layouts, body(): h[:, :, COMP:]  4.8 us
    ppermute x16, waiting for transfers between devices, exchange(): received.append(lax.ppermute(message, ('band', 'freq'), pairs))  3.94 us
  transfers between devices with their start and end apart: 22, of which 6 were waited for; matrix products, arithmetic and copies ran while one was open for 7% of the time, Pallas kernels for 4%

profile of v2, /device:TPU:34, one launch (start us, length us, event | category | flops | bytes accessed | tf_op | source)
XLA Modules:
  0.0 160.7 jit_solution(6975730483097162610)
XLA Ops:
  1.9 2.0 %collective-permute-start.8 = (f32[16,4,48]{2,1,0:T(4,128)S(1)}, f32[16,4,48]{2,1,0:T(4,128)S(1)}, u32[]{:S(2)}, u32[]{:S(2)}) collective-permute-start(f32[16,4,48]{2,1,0:T(4,128)S(1)} %get-tuple-element.48), channel_id=1, source_target_pairs={{1,0},{2,1},{3,2},{4,3},{5,4},{6,5},{7,6},{8,7},{9,8},{10,9},{11,1... | collective-permute-start | bytes 36872 | tf_op jit(solution)/shard_map/ppermute | solution.py:370
  3.9 3.8 %collective-permute-start.9 = (f32[16,4,48]{2,1,0:T(4,128)S(1)}, f32[16,4,48]{2,1,0:T(4,128)S(1)}, u32[]{:S(2)}, u32[]{:S(2)}) collective-permute-start(f32[16,4,48]{2,1,0:T(4,128)S(1)} %get-tuple-element.49), channel_id=1, source_target_pairs={{0,1},{1,2},{2,3},{3,4},{4,5},{5,6},{6,7},{7,8},{8,9},{9,10},{10,1... | collective-permute-start | bytes 36872 | tf_op jit(solution)/shard_map/ppermute | solution.py:371
  7.8 3.7 %spread.1 = f32[32,36,128]{2,1,0:T(8,128)} custom-call(f32[576,256]{1,0:T(8,128)} %bitcast.25), custom_call_target="tpu_custom_call" | custom-call | tf_op jit(solution)/shard_map/spread/pallas_call | solution.py:278
  11.5 12.1 %all-to-all-start = ((f32[32,36,128]{2,1,0:T(8,128)}), f32[32,36,128]{2,1,0:T(8,128)S(1)}, u32[]{:S(2)}, u32[]{:S(2)}) async-start(f32[32,36,128]{2,1,0:T(8,128)} %spread.1), calls=%async_computation | async-start | bytes 1310720 | tf_op jit(solution)/shard_map/all_to_all | solution.py:367
  25.5 1.9 %collective-permute-start.10 = (f32[4,16,48]{2,1,0:T(8,128)S(1)}, f32[4,16,48]{2,1,0:T(8,128)S(1)}, u32[]{:S(2)}, u32[]{:S(2)}) collective-permute-start(f32[4,16,48]{2,1,0:T(8,128)S(1)} %get-tuple-element.46), channel_id=1, source_target_pairs={{0,32},{32,64},{64,96},{96,128},{128,160},{160,192},{192,224},{1,3... | collective-permute-start | bytes 36872 | tf_op jit(solution)/shard_map/ppermute | solution.py:374
  27.4 3.6 %collective-permute-start.11 = (f32[4,16,48]{2,1,0:T(8,128)S(1)}, f32[4,16,48]{2,1,0:T(8,128)S(1)}, u32[]{:S(2)}, u32[]{:S(2)}) collective-permute-start(f32[4,16,48]{2,1,0:T(8,128)S(1)} %get-tuple-element.47), channel_id=1, source_target_pairs={{32,0},{64,32},{96,64},{128,96},{160,128},{192,160},{224,192},{33,... | collective-permute-start | bytes 36872 | tf_op jit(solution)/shard_map/ppermute | solution.py:373
  31.5 1.1 collective-permute-done.11
  32.7 10.7 %all-to-all-done.x_ref = f32[32,36,128]{2,1,0:T(8,128)S(1)} async-done(((f32[32,36,128]{2,1,0:T(8,128)}), f32[32,36,128]{2,1,0:T(8,128)S(1)}, u32[]{:S(2)}, u32[]{:S(2)}) %all-to-all-start) | async-done | bytes 589856 | tf_op jit(solution)/shard_map/all_to_all | solution.py:367
  44.2 2.5 %unpack.1 = (f32[16,8,1152]{2,1,0:T(8,128)}, f32[16,4,1152]{2,1,0:T(4,128)}, f32[16,4,1152]{2,1,0:T(4,128)}, f32[4,8,1152]{2,1,0:T(8,128)}, f32[4,8,1152]{2,1,0:...) custom-call(f32[32,36,128]{2,1,0:T(8,128)} %copy-done.5), custom_call_target="tpu_custom_call" | custom-call | tf_op jit(solution)/shard_map/unpack/pallas_call | solution.py:300
  46.7 2.6 %collective-permute-start = (f32[16,4,1152]{2,1,0:T(4,128)}, f32[16,4,1152]{2,1,0:T(4,128)S(1)}, u32[]{:S(2)}, u32[]{:S(2)}) collective-permute-start(f32[16,4,1152]{2,1,0:T(4,128)} %get-tuple-element.22), channel_id=1, source_target_pairs={{1,0},{2,1},{3,2},{4,3},{5,4},{6,5},{7,6},{8,7},{9,8},{10,9},{11,1... | collective-permute-start | bytes 884744 | tf_op jit(solution)/shard_map/ppermute | solution.py:83
  49.3 3.4 %collective-permute-start.1 = (f32[16,4,1152]{2,1,0:T(4,128)}, f32[16,4,1152]{2,1,0:T(4,128)S(1)}, u32[]{:S(2)}, u32[]{:S(2)}) collective-permute-start(f32[16,4,1152]{2,1,0:T(4,128)} %get-tuple-element.23), channel_id=1, source_target_pairs={{0,1},{1,2},{2,3},{3,4},{4,5},{5,6},{6,7},{7,8},{8,9},{9,10},{10,1... | collective-permute-start | bytes 884744 | tf_op jit(solution)/shard_map/ppermute | solution.py:83
  52.7 1.9 %collective-permute-start.4 = (f32[4,4,1152]{2,1,0:T(4,128)}, f32[4,4,1152]{2,1,0:T(4,128)S(1)}, u32[]{:S(2)}, u32[]{:S(2)}) collective-permute-start(f32[4,4,1152]{2,1,0:T(4,128)} %get-tuple-element.26), channel_id=1, source_target_pairs={{33,0},{34,1},{35,2},{36,3},{37,4},{38,5},{39,6},{40,7},{41,8},{42... | collective-permute-start | bytes 221192 | tf_op jit(solution)/shard_map/ppermute | solution.py:83
  54.7 3.6 %collective-permute-start.5 = (f32[4,4,1152]{2,1,0:T(4,128)}, f32[4,4,1152]{2,1,0:T(4,128)S(1)}, u32[]{:S(2)}, u32[]{:S(2)}) collective-permute-start(f32[4,4,1152]{2,1,0:T(4,128)} %get-tuple-element.27), channel_id=1, source_target_pairs={{32,1},{33,2},{34,3},{35,4},{36,5},{37,6},{38,7},{39,8},{40,9},{41... | collective-permute-start | bytes 221192 | tf_op jit(solution)/shard_map/ppermute | solution.py:83
  58.3 1.9 %collective-permute-start.6 = (f32[4,4,1152]{2,1,0:T(4,128)}, f32[4,4,1152]{2,1,0:T(4,128)S(1)}, u32[]{:S(2)}, u32[]{:S(2)}) collective-permute-start(f32[4,4,1152]{2,1,0:T(4,128)} %get-tuple-element.28), channel_id=1, source_target_pairs={{1,32},{2,33},{3,34},{4,35},{5,36},{6,37},{7,38},{8,39},{9,40},{10... | collective-permute-start | bytes 221192 | tf_op jit(solution)/shard_map/ppermute | solution.py:83
  61.3 3.7 %collective-permute-start.2 = (f32[4,8,1152]{2,1,0:T(8,128)S(1)}, f32[4,8,1152]{2,1,0:T(8,128)S(1)}, u32[]{:S(2)}, u32[]{:S(2)}) collective-permute-start(f32[4,8,1152]{2,1,0:T(8,128)S(1)} %copy-done.12), channel_id=1, source_target_pairs={{32,0},{33,1},{34,2},{35,3},{36,4},{37,5},{38,6},{39,7},{40,8},{41... | collective-permute-start | bytes 442376 | tf_op jit(solution)/shard_map/ppermute | solution.py:83
  65.1 1.9 %collective-permute-start.3 = (f32[4,8,1152]{2,1,0:T(8,128)S(1)}, f32[4,8,1152]{2,1,0:T(8,128)S(1)}, u32[]{:S(2)}, u32[]{:S(2)}) collective-permute-start(f32[4,8,1152]{2,1,0:T(8,128)S(1)} %copy-done.11), channel_id=1, source_target_pairs={{0,32},{1,33},{2,34},{3,35},{4,36},{5,37},{6,38},{7,39},{8,40},{9,... | collective-permute-start | bytes 442376 | tf_op jit(solution)/shard_map/ppermute | solution.py:83
  67.0 4.6 %collective-permute-start.7 = (f32[4,4,1152]{2,1,0:T(4,128)S(1)}, f32[4,4,1152]{2,1,0:T(4,128)S(1)}, u32[]{:S(2)}, u32[]{:S(2)}) collective-permute-start(f32[4,4,1152]{2,1,0:T(4,128)S(1)} %copy-done.13), channel_id=1, source_target_pairs={{0,33},{1,34},{2,35},{3,36},{4,37},{5,38},{6,39},{7,40},{8,41},{9,... | collective-permute-start | bytes 221192 | tf_op jit(solution)/shard_map/ppermute | solution.py:83
  75.1 8.0 %cycle_first.1 = (f32[16,8,1152]{2,1,0:T(8,128)S(1)}, f32[16,8,128]{2,1,0:T(8,128)S(1)}, f32[16,4,1280]{2,1,0:T(4,128)S(1)}, f32[16,4,1280]{2,1,0:T(4,128)S(1)},...) custom-call(f32[16,8,1152]{2,1,0:T(8,128)S(1)} %copy-done.3, ...), custom_call_target="tpu_custom_call" | custom-call | tf_op jit(solution)/shard_map/cycle_first/pallas_call | solution.py:322
  83.8 2.4 %collective-permute-start.12 = (f32[16,4,1280]{2,1,0:T(4,128)S(1)}, f32[16,4,1280]{2,1,0:T(4,128)S(1)}, u32[]{:S(2)}, u32[]{:S(2)}) collective-permute-start(f32[16,4,1280]{2,1,0:T(4,128)S(1)} %get-tuple-element.31), channel_id=1, source_target_pairs={{1,0},{2,1},{3,2},{4,3},{5,4},{6,5},{7,6},{8,7},{9,8},{10,9},{11,1... | collective-permute-start | bytes 983048 | tf_op jit(solution)/shard_map/ppermute | solution.py:83
  86.2 3.4 %collective-permute-start.13 = (f32[16,4,1280]{2,1,0:T(4,128)S(1)}, f32[16,4,1280]{2,1,0:T(4,128)S(1)}, u32[]{:S(2)}, u32[]{:S(2)}) collective-permute-start(f32[16,4,1280]{2,1,0:T(4,128)S(1)} %get-tuple-element.32), channel_id=1, source_target_pairs={{0,1},{1,2},{2,3},{3,4},{4,5},{5,6},{6,7},{7,8},{8,9},{9,10},{10,1... | collective-permute-start | bytes 983048 | tf_op jit(solution)/shard_map/ppermute | solution.py:83
  89.6 1.9 %collective-permute-start.16 = (f32[4,4,1280]{2,1,0:T(4,128)S(1)}, f32[4,4,1280]{2,1,0:T(4,128)S(1)}, u32[]{:S(2)}, u32[]{:S(2)}) collective-permute-start(f32[4,4,1280]{2,1,0:T(4,128)S(1)} %get-tuple-element.35), channel_id=1, source_target_pairs={{33,0},{34,1},{35,2},{36,3},{37,4},{38,5},{39,6},{40,7},{41,8},{42... | collective-permute-start | bytes 245768 | tf_op jit(solution)/shard_map/ppermute | solution.py:83
  91.5 3.8 %collective-permute-start.17 = (f32[4,4,1280]{2,1,0:T(4,128)S(1)}, f32[4,4,1280]{2,1,0:T(4,128)S(1)}, u32[]{:S(2)}, u32[]{:S(2)}) collective-permute-start(f32[4,4,1280]{2,1,0:T(4,128)S(1)} %get-tuple-element.36), channel_id=1, source_target_pairs={{32,1},{33,2},{34,3},{35,4},{36,5},{37,6},{38,7},{39,8},{40,9},{41... | collective-permute-start | bytes 245768 | tf_op jit(solution)/shard_map/ppermute | solution.py:83
  95.4 1.9 %collective-permute-start.18 = (f32[4,4,1280]{2,1,0:T(4,128)S(1)}, f32[4,4,1280]{2,1,0:T(4,128)S(1)}, u32[]{:S(2)}, u32[]{:S(2)}) collective-permute-start(f32[4,4,1280]{2,1,0:T(4,128)S(1)} %get-tuple-element.37), channel_id=1, source_target_pairs={{1,32},{2,33},{3,34},{4,35},{5,36},{6,37},{7,38},{8,39},{9,40},{10... | collective-permute-start | bytes 245768 | tf_op jit(solution)/shard_map/ppermute | solution.py:83
  97.3 3.4 %collective-permute-start.14 = (f32[4,8,1280]{2,1,0:T(8,128)S(1)}, f32[4,8,1280]{2,1,0:T(8,128)S(1)}, u32[]{:S(2)}, u32[]{:S(2)}) collective-permute-start(f32[4,8,1280]{2,1,0:T(8,128)S(1)} %get-tuple-element.33), channel_id=1, source_target_pairs={{32,0},{33,1},{34,2},{35,3},{36,4},{37,5},{38,6},{39,7},{40,8},{41... | collective-permute-start | bytes 491528 | tf_op jit(solution)/shard_map/ppermute | solution.py:83
  100.7 2.0 %collective-permute-start.15 = (f32[4,8,1280]{2,1,0:T(8,128)S(1)}, f32[4,8,1280]{2,1,0:T(8,128)S(1)}, u32[]{:S(2)}, u32[]{:S(2)}) collective-permute-start(f32[4,8,1280]{2,1,0:T(8,128)S(1)} %get-tuple-element.34), channel_id=1, source_target_pairs={{0,32},{1,33},{2,34},{3,35},{4,36},{5,37},{6,38},{7,39},{8,40},{9,... | collective-permute-start | bytes 491528 | tf_op jit(solution)/shard_map/ppermute | solution.py:83
  103.1 6.1 %collective-permute-start.19 = (f32[4,4,1280]{2,1,0:T(4,128)S(1)}, f32[4,4,1280]{2,1,0:T(4,128)S(1)}, u32[]{:S(2)}, u32[]{:S(2)}) collective-permute-start(f32[4,4,1280]{2,1,0:T(4,128)S(1)} %get-tuple-element.38), channel_id=1, source_target_pairs={{0,33},{1,34},{2,35},{3,36},{4,37},{5,38},{6,39},{7,40},{8,41},{9,... | collective-permute-start | bytes 245768 | tf_op jit(solution)/shard_map/ppermute | solution.py:83
  109.2 2.4 %collective-permute-done.19.refs_8_ = f32[4,4,1280]{2,1,0:T(4,128)S(1)} collective-permute-done((f32[4,4,1280]{2,1,0:T(4,128)S(1)}, f32[4,4,1280]{2,1,0:T(4,128)S(1)}, u32[]{:S(2)}, u32[]{:S(2)}) %collective-permute-start.19) | collective-permute-done | bytes 81952 | tf_op jit(solution)/shard_map/ppermute | solution.py:83
  112.0 8.7 %cycle_last.1 = f32[32,36,128]{2,1,0:T(8,128)} custom-call(f32[16,8,1152]{2,1,0:T(8,128)S(1)} %get-tuple-element.30.refs_0_, f32[16,4,1280]{2,1,0:T(4,128)S(1)} %collective-permute-done.12.refs_1_, f32[16,4,1280]{2,1,0:T(4,128)S(1)} %collective-permute-done.13.refs_2_, f32[4,8,1280]{2,1,0:T(8,128)S(1)} %collective-permute-done.14.refs_3_, ...), custom_call_target="tpu_custom_call" | custom-call | tf_op jit(solution)/shard_map/cycle_last/pallas_call | solution.py:322
  120.7 14.5 %all-to-all-start.1 = ((f32[32,36,128]{2,1,0:T(8,128)}), f32[32,36,128]{2,1,0:T(8,128)S(1)}, u32[]{:S(2)}, u32[]{:S(2)}) async-start(f32[32,36,128]{2,1,0:T(8,128)} %cycle_last.1), calls=%async_computation.1 | async-start | bytes 1310720 | tf_op jit(solution)/shard_map/all_to_all | solution.py:425
  140.7 2.3 %ocean.1 = f32[16,8,128]{2,1,0:T(8,128)} custom-call(f32[24,16,128]{2,1,0:T(8,128)} %pad.19.u_ref, f32[16,8,128]{2,1,0:T(8,128)} %copy-done.4, f32[16,4,128]{2,1,0:T(4,128)} %slice.125.refs_0_, f32[16,4,128]{2,1,0:T(4,128)} %slice.126.refs_1_, f32[4,8,128]{2,1,0:T(8,128)} %slice.127.refs_2_, f32[4,8,128]{2,1,0:T(8,128)} %slice.128.refs_3_, ...), custom_call_target="tpu_custom_call" | custom-call | tf_op jit(solution)/shard_map/ocean/pallas_call | solution.py:341
  144.5 11.6 %all-to-all-done.1.x_ref = f32[32,36,128]{2,1,0:T(8,128)S(1)} async-done(((f32[32,36,128]{2,1,0:T(8,128)}), f32[32,36,128]{2,1,0:T(8,128)S(1)}, u32[]{:S(2)}, u32[]{:S(2)}) %all-to-all-start.1) | async-done | bytes 589856 | tf_op jit(solution)/shard_map/all_to_all | solution.py:425
  157.0 3.8 %collect.1 = f32[576,256]{1,0:T(8,128)} custom-call(f32[32,36,128]{2,1,0:T(8,128)} %copy-done.6), custom_call_target="tpu_custom_call" | custom-call | tf_op jit(solution)/shard_map/collect/pallas_call | solution.py:289
  (93 shorter events, 18.0 us)
Async XLA Ops:
  0.6 23.1 %copy-start.7 = (s32[8,128,256]{2,1,0:T(8,128)S(1)}, s32[8,128,256]{2,1,0:T(8,128)}, u32[]{:S(2)}) copy-start(s32[8,128,256]{2,1,0:T(8,128)} %param.12) | copy-start | bytes 3145732
  1.9 23.6 %collective-permute-start.8 = (f32[16,4,48]{2,1,0:T(4,128)S(1)}, f32[16,4,48]{2,1,0:T(4,128)S(1)}, u32[]{:S(2)}, u32[]{:S(2)}) collective-permute-start(f32[16,4,48]{2,1,0:T(4,128)S(1)} %get-tuple-element.48), channel_id=1, source_target_pairs={{1,0},{2,1},{3,2},{4,3},{5,4},{6,5},{7,6},{8,7},{9,8},{10,9},{11,1... | collective-permute-start | bytes 36872 | tf_op jit(solution)/shard_map/ppermute | solution.py:370
  3.9 21.5 %collective-permute-start.9 = (f32[16,4,48]{2,1,0:T(4,128)S(1)}, f32[16,4,48]{2,1,0:T(4,128)S(1)}, u32[]{:S(2)}, u32[]{:S(2)}) collective-permute-start(f32[16,4,48]{2,1,0:T(4,128)S(1)} %get-tuple-element.49), channel_id=1, source_target_pairs={{0,1},{1,2},{2,3},{3,4},{4,5},{5,6},{6,7},{7,8},{8,9},{9,10},{10,1... | collective-permute-start | bytes 36872 | tf_op jit(solution)/shard_map/ppermute | solution.py:371
  7.7 16.3 %copy-start.9 = (s32[32,4]{0,1:T(4,128)S(1)}, s32[32,4]{0,1:T(4,128)}, u32[]{:S(2)}) copy-start(s32[32,4]{0,1:T(4,128)} %param.15) | copy-start | bytes 1540
  11.5 31.9 %all-to-all-start = ((f32[32,36,128]{2,1,0:T(8,128)}), f32[32,36,128]{2,1,0:T(8,128)S(1)}, u32[]{:S(2)}, u32[]{:S(2)}) async-start(f32[32,36,128]{2,1,0:T(8,128)} %spread.1), calls=%async_computation | async-start | bytes 1310720 | tf_op jit(solution)/shard_map/all_to_all | solution.py:367
  24.3 6.9 %copy-start.10 = (s32[32]{0:T(128)S(1)}, s32[32]{0:T(128)}, u32[]{:S(2)}) copy-start(s32[32]{0:T(128)} %param.14) | copy-start | bytes 388
  25.5 6.1 %collective-permute-start.10 = (f32[4,16,48]{2,1,0:T(8,128)S(1)}, f32[4,16,48]{2,1,0:T(8,128)S(1)}, u32[]{:S(2)}, u32[]{:S(2)}) collective-permute-start(f32[4,16,48]{2,1,0:T(8,128)S(1)} %get-tuple-element.46), channel_id=1, source_target_pairs={{0,32},{32,64},{64,96},{96,128},{128,160},{160,192},{192,224},{1,3... | collective-permute-start | bytes 36872 | tf_op jit(solution)/shard_map/ppermute | solution.py:374
  27.4 5.2 %collective-permute-start.11 = (f32[4,16,48]{2,1,0:T(8,128)S(1)}, f32[4,16,48]{2,1,0:T(8,128)S(1)}, u32[]{:S(2)}, u32[]{:S(2)}) collective-permute-start(f32[4,16,48]{2,1,0:T(8,128)S(1)} %get-tuple-element.47), channel_id=1, source_target_pairs={{32,0},{64,32},{96,64},{128,96},{160,128},{192,160},{224,192},{33,... | collective-permute-start | bytes 36872 | tf_op jit(solution)/shard_map/ppermute | solution.py:373
  46.7 14.6 %copy-start.12 = (f32[4,8,1152]{2,1,0:T(8,128)S(1)}, f32[4,8,1152]{2,1,0:T(8,128)}, u32[]{:S(2)}) copy-start(f32[4,8,1152]{2,1,0:T(8,128)} %get-tuple-element.24) | copy-start | bytes 442372
  46.7 18.3 %copy-start.11 = (f32[4,8,1152]{2,1,0:T(8,128)S(1)}, f32[4,8,1152]{2,1,0:T(8,128)}, u32[]{:S(2)}) copy-start(f32[4,8,1152]{2,1,0:T(8,128)} %get-tuple-element.25) | copy-start | bytes 442372
  46.7 20.3 %copy-start.13 = (f32[4,4,1152]{2,1,0:T(4,128)S(1)}, f32[4,4,1152]{2,1,0:T(4,128)}, u32[]{:S(2)}) copy-start(f32[4,4,1152]{2,1,0:T(4,128)} %get-tuple-element.29) | copy-start | bytes 221188
  46.7 26.9 %collective-permute-start = (f32[16,4,1152]{2,1,0:T(4,128)}, f32[16,4,1152]{2,1,0:T(4,128)S(1)}, u32[]{:S(2)}, u32[]{:S(2)}) collective-permute-start(f32[16,4,1152]{2,1,0:T(4,128)} %get-tuple-element.22), channel_id=1, source_target_pairs={{1,0},{2,1},{3,2},{4,3},{5,4},{6,5},{7,6},{8,7},{9,8},{10,9},{11,1... | collective-permute-start | bytes 884744 | tf_op jit(solution)/shard_map/ppermute | solution.py:83
  49.3 24.3 %collective-permute-start.1 = (f32[16,4,1152]{2,1,0:T(4,128)}, f32[16,4,1152]{2,1,0:T(4,128)S(1)}, u32[]{:S(2)}, u32[]{:S(2)}) collective-permute-start(f32[16,4,1152]{2,1,0:T(4,128)} %get-tuple-element.23), channel_id=1, source_target_pairs={{0,1},{1,2},{2,3},{3,4},{4,5},{5,6},{6,7},{7,8},{8,9},{9,10},{10,1... | collective-permute-start | bytes 884744 | tf_op jit(solution)/shard_map/ppermute | solution.py:83
  52.7 8.6 %collective-permute-start.4 = (f32[4,4,1152]{2,1,0:T(4,128)}, f32[4,4,1152]{2,1,0:T(4,128)S(1)}, u32[]{:S(2)}, u32[]{:S(2)}) collective-permute-start(f32[4,4,1152]{2,1,0:T(4,128)} %get-tuple-element.26), channel_id=1, source_target_pairs={{33,0},{34,1},{35,2},{36,3},{37,4},{38,5},{39,6},{40,7},{41,8},{42... | collective-permute-start | bytes 221192 | tf_op jit(solution)/shard_map/ppermute | solution.py:83
  54.7 10.4 %collective-permute-start.5 = (f32[4,4,1152]{2,1,0:T(4,128)}, f32[4,4,1152]{2,1,0:T(4,128)S(1)}, u32[]{:S(2)}, u32[]{:S(2)}) collective-permute-start(f32[4,4,1152]{2,1,0:T(4,128)} %get-tuple-element.27), channel_id=1, source_target_pairs={{32,1},{33,2},{34,3},{35,4},{36,5},{37,6},{38,7},{39,8},{40,9},{41... | collective-permute-start | bytes 221192 | tf_op jit(solution)/shard_map/ppermute | solution.py:83
  58.3 8.7 %collective-permute-start.6 = (f32[4,4,1152]{2,1,0:T(4,128)}, f32[4,4,1152]{2,1,0:T(4,128)S(1)}, u32[]{:S(2)}, u32[]{:S(2)}) collective-permute-start(f32[4,4,1152]{2,1,0:T(4,128)} %get-tuple-element.28), channel_id=1, source_target_pairs={{1,32},{2,33},{3,34},{4,35},{5,36},{6,37},{7,38},{8,39},{9,40},{10... | collective-permute-start | bytes 221192 | tf_op jit(solution)/shard_map/ppermute | solution.py:83
  60.2 13.8 %copy-start.1 = (bf16[1152,1152]{1,0:T(8,128)(2,1)S(1)}, bf16[1152,1152]{1,0:T(8,128)(2,1)}, u32[]{:S(2)}) copy-start(bf16[1152,1152]{1,0:T(8,128)(2,1)} %refs_14_.3) | copy-start | bytes 7962628
  61.1 12.9 %copy-start = (bf16[1152,1152]{1,0:T(8,128)(2,1)S(1)}, bf16[1152,1152]{1,0:T(8,128)(2,1)}, u32[]{:S(2)}) copy-start(bf16[1152,1152]{1,0:T(8,128)(2,1)} %refs_13_.3) | copy-start | bytes 7962628
  61.3 12.3 %collective-permute-start.2 = (f32[4,8,1152]{2,1,0:T(8,128)S(1)}, f32[4,8,1152]{2,1,0:T(8,128)S(1)}, u32[]{:S(2)}, u32[]{:S(2)}) collective-permute-start(f32[4,8,1152]{2,1,0:T(8,128)S(1)} %copy-done.12), channel_id=1, source_target_pairs={{32,0},{33,1},{34,2},{35,3},{36,4},{37,5},{38,6},{39,7},{40,8},{41... | collective-permute-start | bytes 442376 | tf_op jit(solution)/shard_map/ppermute | solution.py:83
  65.1 8.5 %collective-permute-start.3 = (f32[4,8,1152]{2,1,0:T(8,128)S(1)}, f32[4,8,1152]{2,1,0:T(8,128)S(1)}, u32[]{:S(2)}, u32[]{:S(2)}) collective-permute-start(f32[4,8,1152]{2,1,0:T(8,128)S(1)} %copy-done.11), channel_id=1, source_target_pairs={{0,32},{1,33},{2,34},{3,35},{4,36},{5,37},{6,38},{7,39},{8,40},{9,... | collective-permute-start | bytes 442376 | tf_op jit(solution)/shard_map/ppermute | solution.py:83
  67.0 6.6 %collective-permute-start.7 = (f32[4,4,1152]{2,1,0:T(4,128)S(1)}, f32[4,4,1152]{2,1,0:T(4,128)S(1)}, u32[]{:S(2)}, u32[]{:S(2)}) collective-permute-start(f32[4,4,1152]{2,1,0:T(4,128)S(1)} %copy-done.13), channel_id=1, source_target_pairs={{0,33},{1,34},{2,35},{3,36},{4,37},{5,38},{6,39},{7,40},{8,41},{9,... | collective-permute-start | bytes 221192 | tf_op jit(solution)/shard_map/ppermute | solution.py:83
  73.7 38.2 %copy-start.2 = (f32[24,16,128]{2,1,0:T(8,128)}, f32[24,16,128]{2,1,0:T(8,128)S(1)}, u32[]{:S(2)}) copy-start(f32[24,16,128]{2,1,0:T(8,128)S(1)} %squeeze.3.refs_12_.refs_8_) | copy-start | bytes 589828
  74.0 1.1 copy-start.3
  83.8 27.9 %collective-permute-start.12 = (f32[16,4,1280]{2,1,0:T(4,128)S(1)}, f32[16,4,1280]{2,1,0:T(4,128)S(1)}, u32[]{:S(2)}, u32[]{:S(2)}) collective-permute-start(f32[16,4,1280]{2,1,0:T(4,128)S(1)} %get-tuple-element.31), channel_id=1, source_target_pairs={{1,0},{2,1},{3,2},{4,3},{5,4},{6,5},{7,6},{8,7},{9,8},{10,9},{11,1... | collective-permute-start | bytes 983048 | tf_op jit(solution)/shard_map/ppermute | solution.py:83
  86.2 25.5 %collective-permute-start.13 = (f32[16,4,1280]{2,1,0:T(4,128)S(1)}, f32[16,4,1280]{2,1,0:T(4,128)S(1)}, u32[]{:S(2)}, u32[]{:S(2)}) collective-permute-start(f32[16,4,1280]{2,1,0:T(4,128)S(1)} %get-tuple-element.32), channel_id=1, source_target_pairs={{0,1},{1,2},{2,3},{3,4},{4,5},{5,6},{6,7},{7,8},{8,9},{9,10},{10,1... | collective-permute-start | bytes 983048 | tf_op jit(solution)/shard_map/ppermute | solution.py:83
  89.6 7.7 %collective-permute-start.16 = (f32[4,4,1280]{2,1,0:T(4,128)S(1)}, f32[4,4,1280]{2,1,0:T(4,128)S(1)}, u32[]{:S(2)}, u32[]{:S(2)}) collective-permute-start(f32[4,4,1280]{2,1,0:T(4,128)S(1)} %get-tuple-element.35), channel_id=1, source_target_pairs={{33,0},{34,1},{35,2},{36,3},{37,4},{38,5},{39,6},{40,7},{41,8},{42... | collective-permute-start | bytes 245768 | tf_op jit(solution)/shard_map/ppermute | solution.py:83
  91.5 9.2 %collective-permute-start.17 = (f32[4,4,1280]{2,1,0:T(4,128)S(1)}, f32[4,4,1280]{2,1,0:T(4,128)S(1)}, u32[]{:S(2)}, u32[]{:S(2)}) collective-permute-start(f32[4,4,1280]{2,1,0:T(4,128)S(1)} %get-tuple-element.36), channel_id=1, source_target_pairs={{32,1},{33,2},{34,3},{35,4},{36,5},{37,6},{38,7},{39,8},{40,9},{41... | collective-permute-start | bytes 245768 | tf_op jit(solution)/shard_map/ppermute | solution.py:83
  95.4 7.7 %collective-permute-start.18 = (f32[4,4,1280]{2,1,0:T(4,128)S(1)}, f32[4,4,1280]{2,1,0:T(4,128)S(1)}, u32[]{:S(2)}, u32[]{:S(2)}) collective-permute-start(f32[4,4,1280]{2,1,0:T(4,128)S(1)} %get-tuple-element.37), channel_id=1, source_target_pairs={{1,32},{2,33},{3,34},{4,35},{5,36},{6,37},{7,38},{8,39},{9,40},{10... | collective-permute-start | bytes 245768 | tf_op jit(solution)/shard_map/ppermute | solution.py:83
  97.3 14.4 %collective-permute-start.14 = (f32[4,8,1280]{2,1,0:T(8,128)S(1)}, f32[4,8,1280]{2,1,0:T(8,128)S(1)}, u32[]{:S(2)}, u32[]{:S(2)}) collective-permute-start(f32[4,8,1280]{2,1,0:T(8,128)S(1)} %get-tuple-element.33), channel_id=1, source_target_pairs={{32,0},{33,1},{34,2},{35,3},{36,4},{37,5},{38,6},{39,7},{40,8},{41... | collective-permute-start | bytes 491528 | tf_op jit(solution)/shard_map/ppermute | solution.py:83
  100.7 10.9 %collective-permute-start.15 = (f32[4,8,1280]{2,1,0:T(8,128)S(1)}, f32[4,8,1280]{2,1,0:T(8,128)S(1)}, u32[]{:S(2)}, u32[]{:S(2)}) collective-permute-start(f32[4,8,1280]{2,1,0:T(8,128)S(1)} %get-tuple-element.34), channel_id=1, source_target_pairs={{0,32},{1,33},{2,34},{3,35},{4,36},{5,37},{6,38},{7,39},{8,40},{9,... | collective-permute-start | bytes 491528 | tf_op jit(solution)/shard_map/ppermute | solution.py:83
  103.1 8.5 %collective-permute-start.19 = (f32[4,4,1280]{2,1,0:T(4,128)S(1)}, f32[4,4,1280]{2,1,0:T(4,128)S(1)}, u32[]{:S(2)}, u32[]{:S(2)}) collective-permute-start(f32[4,4,1280]{2,1,0:T(4,128)S(1)} %get-tuple-element.38), channel_id=1, source_target_pairs={{0,33},{1,34},{2,35},{3,36},{4,37},{5,38},{6,39},{7,40},{8,41},{9,... | collective-permute-start | bytes 245768 | tf_op jit(solution)/shard_map/ppermute | solution.py:83
  120.7 35.5 %all-to-all-start.1 = ((f32[32,36,128]{2,1,0:T(8,128)}), f32[32,36,128]{2,1,0:T(8,128)S(1)}, u32[]{:S(2)}, u32[]{:S(2)}) async-start(f32[32,36,128]{2,1,0:T(8,128)} %cycle_last.1), calls=%async_computation.1 | async-start | bytes 1310720 | tf_op jit(solution)/shard_map/all_to_all | solution.py:425
  (4 other events, 3.3 us)

commit v3 on v2

v3 whole, which is shorter than its diff:
```python
import jax
import jax.numpy as jnp
from jax import lax
from jax.experimental import pallas as pl
from jax.experimental.pallas import tpu as pltpu
from jax.sharding import PartitionSpec as P

DIR = 36
FREQS = 32
COMP = 1152
LAYERS = 24
SUB = 4
CYCLES = 2
OSTEPS = 3
BANDS = 8
ROWS = 16
COLS = 8
HALO = 4
EXT_R = 24
EXT_C = 16
LANES = 128
GROUPS = 9
WIDE = COMP + LANES

precise = lax.Precision.HIGHEST
ocean_dt = 0.2
viscous = 0.5
mixing = 0.5
friction = 0.1

f32 = jnp.float32


def directions(how_many):
    angles = (jnp.arange(how_many, dtype=f32) + 0.5) * (2.0 * jnp.pi / how_many)
    return (jnp.cos(angles), jnp.sin(angles))


def speed_of(position, total_count):
    return 0.5 + 0.3 * (position.astype(f32) + 0.5) / total_count


def wavenumber(position, total_count):
    return 0.5 + 1.5 * (position.astype(f32) + 0.5) / total_count


def deposit_table(stokes_route):
    layer_ids = jnp.arange(LAYERS, dtype=jnp.int32)
    weights = 1.0 / (1.0 + jnp.arange(stokes_route.shape[1], dtype=f32))
    hits = (stokes_route[:, :, None] == layer_ids[None, None, :]).astype(f32)
    return jnp.sum(hits * weights[None, :, None], axis=1)


def line(count, shift):
    return [(i, i - shift) for i in range(count) if 0 <= i - shift < count]


def widen(own, to_last, to_next):
    from_next = lax.ppermute(to_last, "freq", line(FREQS, 1))
    from_last = lax.ppermute(to_next, "freq", line(FREQS, -1))
    first, last = ends(own, from_next, from_last)
    from_up = lax.ppermute(first, "band", line(BANDS, 1))
    from_down = lax.ppermute(last, "band", line(BANDS, -1))
    return [own, from_next, from_last, from_up, from_down]


def fill(ext_ref, pieces, lanes):
    own, from_next, from_last, from_up, from_down = pieces
    middle = slice(HALO, HALO + ROWS)
    ext_ref[middle, 0:COLS, :] = own[:, :, lanes]
    ext_ref[middle, COLS : COLS + HALO, :] = from_next[:, :, lanes]
    ext_ref[middle, COLS + HALO : EXT_C, :] = from_last[:, :, lanes]
    ext_ref[HALO + ROWS : EXT_R] = from_up[:, :, lanes]
    ext_ref[0:HALO] = from_down[:, :, lanes]


def swap_blocks(tiles):
    block = lax.broadcasted_iota(jnp.int32, tiles[0].shape, 1) // 8
    for bit in (1, 2, 4, 8):
        upper = (block & bit) != 0
        fresh = list(tiles)
        for low in range(16):
            if low & bit:
                continue
            high = low | bit
            fresh[low] = jnp.where(upper, pltpu.roll(tiles[high], bit * 8, 1), tiles[low])
            fresh[high] = jnp.where(upper, tiles[high], pltpu.roll(tiles[low], LANES - bit * 8, 1))
        tiles = fresh
    return tiles


def spread_kernel(x_ref, o_ref, half_ref):
    for half in range(2):
        half_ref[half] = x_ref[:, half * LANES : (half + 1) * LANES]
        tiles = [half_ref[half, pl.ds(r, 8, stride=ROWS), :] for r in range(ROWS)]
        for i, tile in enumerate(swap_blocks(tiles)):
            o_ref[half * ROWS + i] = tile


def collect_kernel(x_ref, o_ref, half_ref):
    for half in range(2):
        tiles = [x_ref[half * ROWS + i] for i in range(ROWS)]
        for r, tile in enumerate(swap_blocks(tiles)):
            half_ref[half, pl.ds(r, 8, stride=ROWS), :] = tile
        o_ref[:, half * LANES : (half + 1) * LANES] = half_ref[half]


def ends_kernel(own, from_next, from_last, first_ref, last_ref):
    for ref, rows in ((first_ref, slice(0, HALO)), (last_ref, slice(ROWS - HALO, ROWS))):
        ref[:, 0:COLS, :] = own[rows]
        ref[:, COLS : COLS + HALO, :] = from_next[rows]
        ref[:, COLS + HALO : EXT_C, :] = from_last[rows]


def put(value, refs, lanes):
    refs[0][:, :, lanes] = value
    refs[1][:, :, lanes] = value[:, :HALO, :]
    refs[2][:, :, lanes] = value[:, HALO:, :]


def unpack_kernel(x_ref, u_ref, *rest):
    out_refs, flat_ref = rest[:-1], rest[-1]
    for g in range(FREQS):
        flat_ref[pl.ds(g * DIR, DIR), :] = x_ref[g]
    for k in range(GROUPS):
        lanes = slice(k * LANES, (k + 1) * LANES)
        put(jnp.transpose(flat_ref[lanes, :]).reshape(ROWS, COLS, LANES), out_refs, lanes)
    put(u_ref[...], out_refs, slice(COMP, WIDE))


def face_flux(lower, upper, half_courant, second):
    q = jnp.where(second, (half_courant + half_courant) * half_courant, jnp.abs(half_courant))
    return lower * (half_courant + q) + upper * (half_courant - q)


def courants(ext_ref, lane_ref, pick_ref, north_ref, east_ref):
    lane = lax.broadcasted_iota(jnp.int32, (EXT_C, LANES), 1)
    quarter = (0.25 * 0.15) * jnp.tanh(ext_ref[...])
    faces = []
    for r in range(EXT_R):
        along_rows = quarter[r] + quarter[min(r + 1, EXT_R - 1)]
        along_cols = quarter[r] + pltpu.roll(quarter[r], 1, 0)
        faces.append(jnp.where(lane < LAYERS, along_cols, along_rows))
    faces = jnp.concatenate(faces, axis=0)
    high = faces.astype(jnp.bfloat16)
    rest = faces - high.astype(f32)
    middle = rest.astype(jnp.bfloat16)
    low = (rest - middle.astype(f32)).astype(jnp.bfloat16)
    parts = jnp.concatenate([high, middle, low], axis=1)
    for index, ref in ((0, east_ref), (1, north_ref)):
        picked = jnp.dot(parts, pick_ref[index], preferred_element_type=f32)
        ref[...] = (lane_ref[index] + picked).reshape(EXT_R, EXT_C, COMP)


def cycle_kernel(first, *refs):
    refs = list(refs)
    take = lambda n: [refs.pop(0) for _ in range(n)]
    pieces = take(5)
    flag_ref, sea_ref, gain_ref, quad_ref = take(4)
    if first:
        lane_ref, pick_ref, weight_hi, weight_lo = take(4)
        out_refs = take(3)
        ext_ref, north_ref, east_ref = take(3)
    else:
        north_ref, east_ref = take(2)
        out_ref, ext_ref = take(2)
    tile_ref, energy_ref = take(2)
    fill(ext_ref, pieces, slice(COMP, WIDE))
    if first:
        courants(ext_ref, lane_ref, pick_ref, north_ref, east_ref)

    def advect(k, carry):
        lanes = pl.ds(pl.multiple_of(k * LANES, LANES), LANES)
        fill(tile_ref, pieces, lanes)
        for s in range(SUB):
            here = tile_ref[s]
            above = tile_ref[s + 1]
            flag = flag_ref[s, s + 1] != 0.0
            flux_below = face_flux(here, above, north_ref[s, :, lanes], flag)
            for r in range(s + 1, EXT_R - 1 - s):
                here = above
                above = tile_ref[r + 1]
                flag_above = flag_ref[s, r + 1] != 0.0
                flux_above = face_flux(here, above, north_ref[r, :, lanes], flag_above)
                shifted = here - (flux_above - flux_below)
                flux_east = face_flux(
                    pltpu.roll(shifted, 1, 0), shifted, east_ref[r, :, lanes], flag
                )
                result = shifted - (pltpu.roll(flux_east, EXT_C - 1, 0) - flux_east)
                result = result * sea_ref[r]
                if s == SUB - 1:
                    energy_ref[r - HALO, :, lanes] = result[0:COLS]
                else:
                    tile_ref[r] = result
                flux_below = flux_above
                flag = flag_above
        return carry

    lax.fori_loop(0, GROUPS, advect, 0)
    cells = ROWS * COLS
    energy = energy_ref[...].reshape(cells, COMP)
    rounded = energy.astype(jnp.bfloat16)
    squared = (energy * energy).astype(jnp.bfloat16)
    if first:
        rest = (energy - rounded.astype(f32)).astype(jnp.bfloat16)
        mm = lambda a, b: jnp.dot(a, b, preferred_element_type=f32)
        stokes = mm(rounded, weight_hi[...]) + (mm(rest, weight_hi[...]) + mm(rounded, weight_lo[...]))
        stokes = stokes.reshape(ROWS, COLS, LANES)
        put(stokes, out_refs, pl.ds(COMP, LANES))
    nt = (((1,), (1,)), ((), ()))
    for k in range(GROUPS):
        lanes = pl.ds(k * LANES, LANES)
        gain = lax.dot_general(rounded, gain_ref[lanes, :], nt, preferred_element_type=f32)
        quartic = lax.dot_general(squared, quad_ref[lanes, :], nt, preferred_element_type=f32)
        before = energy_ref[:, :, lanes].reshape(cells, LANES)
        updated = before * (1.0 + 0.5 * jnp.tanh(gain) - 0.25 * jnp.tanh(quartic))
        if first:
            put(updated.reshape(ROWS, COLS, LANES), out_refs, lanes)
        else:
            flat = jnp.transpose(updated)
            start = k * LANES
            while start < (k + 1) * LANES:
                g, d = divmod(start, DIR)
                count = min(DIR - d, (k + 1) * LANES - start)
                at = start - k * LANES
                out_ref[g, d : d + count, :] = flat[at : at + count, :]
                start += count


def ocean_kernel(u_ref, drift_ref, sea_ref, o_ref, now_ref):
    now_ref[...] = u_ref[...]
    lane = lax.broadcasted_iota(jnp.int32, (EXT_C, LANES), 1)
    used = lane < 2 * LAYERS
    east = lane < LAYERS
    top = (lane == LAYERS - 1) | (lane == 2 * LAYERS - 1)
    bottom = (lane == 0) | (lane == LAYERS)
    for s in range(OSTEPS):
        low = 2 + s
        below = now_ref[low - 1]
        here = now_ref[low]
        for r in range(low, EXT_R - low):
            above = now_ref[r + 1]
            laplace = above + below + pltpu.roll(here, EXT_C - 1, 0) + pltpu.roll(here, 1, 0) - 4.0 * here
            moving = here + drift_ref[r]
            turning = jnp.where(
                east, pltpu.roll(moving, LANES - LAYERS, 1), -pltpu.roll(moving, LAYERS, 1)
            )
            over = jnp.where(top, 0.0, pltpu.roll(here, LANES - 1, 1))
            under = jnp.where(bottom, 0.0, pltpu.roll(here, 1, 1))
            tendency = (
                viscous * laplace + turning + mixing * (over + under - 2.0 * here) - friction * here
            )
            result = jnp.where(used, (here + ocean_dt * tendency) * sea_ref[r], 0.0)
            if s == OSTEPS - 1:
                o_ref[r - HALO] = result[0:COLS]
            else:
                now_ref[r] = result
            below, here = here, above


def shape_of(*dims, dtype=f32):
    return jax.ShapeDtypeStruct(dims, dtype)


vmem = pl.BlockSpec(memory_space=pltpu.VMEM)


def call(kernel, name, operands, out_shape, scratch, mebibytes):
    return pl.pallas_call(
        kernel,
        out_shape=out_shape,
        in_specs=[vmem] * len(operands),
        out_specs=jax.tree.map(lambda _: vmem, out_shape),
        scratch_shapes=[pltpu.VMEM(shape, f32) for shape in scratch],
        compiler_params=pltpu.CompilerParams(vmem_limit_bytes=mebibytes * 2**20),
        name=name,
    )(*operands)


by_rows = pl.BlockSpec((8 * ROWS, 2 * LANES), lambda i: (i, 0))
by_chunks = pl.BlockSpec((FREQS, 8, LANES), lambda i: (0, i, 0))


def relayout(kernel, name, x, in_spec, out_spec, out_shape):
    return pl.pallas_call(
        kernel,
        grid=(pl.cdiv(DIR, 8),),
        out_shape=out_shape,
        in_specs=[in_spec],
        out_specs=out_spec,
        scratch_shapes=[pltpu.VMEM((2, 8 * ROWS, LANES), f32)],
        compiler_params=pltpu.CompilerParams(vmem_limit_bytes=4 * 2**20),
        name=name,
    )(x)


def spread(x):
    x = x.reshape(DIR * ROWS, 2 * LANES)
    return relayout(spread_kernel, "spread", x, by_rows, by_chunks, shape_of(FREQS, DIR, LANES))


def collect(x):
    out_shape = shape_of(DIR * ROWS, 2 * LANES)
    out = relayout(collect_kernel, "collect", x, by_chunks, by_rows, out_shape)
    return out.reshape(1, DIR, ROWS, 2 * LANES)


tile_shapes = [shape_of(ROWS, COLS, WIDE)] + [shape_of(ROWS, HALO, WIDE)] * 2
ext_shape = shape_of(EXT_R, EXT_C, LANES)
face_shape = shape_of(EXT_R, EXT_C, COMP)


def unpack(x, velocity):
    return call(unpack_kernel, "unpack", [x, velocity], tile_shapes, [(COMP, LANES)], 8)


def ends(*pieces):
    return call(ends_kernel, "ends", pieces, [shape_of(HALO, EXT_C, WIDE)] * 2, [], 4)


def run_cycle(first, operands):
    if first:
        out_shape = tile_shapes + [ext_shape, face_shape, face_shape]
    else:
        out_shape = [shape_of(FREQS, DIR, LANES), ext_shape]
    return call(
        lambda *refs: cycle_kernel(first, *refs),
        "cycle_first" if first else "cycle_last",
        operands,
        out_shape,
        [(EXT_R, EXT_C, LANES), (ROWS, COLS, COMP)],
        24,
    )


def ocean(velocity, stokes, sea):
    out_shape = shape_of(ROWS, COLS, LANES)
    return call(ocean_kernel, "ocean", [velocity, stokes, sea], out_shape, [(EXT_R, EXT_C, LANES)], 4)


def body(
    spectrum,
    velocity,
    gain_matrix,
    quad_matrix,
    limiter_flags,
    sea_mask,
    current_route,
    stokes_route,
):
    band_index = lax.axis_index("band")
    freq_index = lax.axis_index("freq")
    chunks = lax.all_to_all(spread(spectrum), "freq", split_axis=0, concat_axis=0, tiled=True)

    tile = jnp.transpose(velocity, (2, 3, 0, 1)).reshape(ROWS, COLS, 2 * LAYERS)
    tile = jnp.pad(tile, ((0, 0), (0, 0), (0, LANES - 2 * LAYERS)))

    cos_table, sin_table = directions(DIR)
    speeds = speed_of(jnp.arange(FREQS, dtype=jnp.int32), FREQS)
    waves = 0.5 * speeds[None, :, None] * jnp.stack([cos_table, sin_table])[:, None, :]
    waves = waves.reshape(2, 1, COMP)
    lane_ids = jnp.arange(LANES, dtype=jnp.int32)[None, :, None]
    routes = jnp.repeat(current_route, DIR)[None, None, :]
    starts = jnp.array([0, LAYERS], jnp.int32)[:, None, None]
    picker = (lane_ids == routes + starts).astype(jnp.bfloat16)
    picker = jnp.concatenate([picker] * 3, axis=1)

    def window(grid):
        padded = jnp.pad(grid, ((0, 0), (HALO, HALO), (HALO, HALO))).astype(f32)
        part = lax.dynamic_slice(
            padded,
            (0, band_index * ROWS, freq_index * COLS),
            (grid.shape[0], EXT_R, EXT_C),
        )
        part = jnp.concatenate([part[:, :, HALO:], part[:, :, :HALO]], axis=2)
        return jnp.broadcast_to(part[..., None], part.shape + (LANES,))

    flags = window(limiter_flags)
    sea = window(sea_mask[None])[0]

    numbers = wavenumber(jnp.arange(FREQS, dtype=jnp.int32), FREQS) * DIR ** (-0.5)
    deposit = deposit_table(stokes_route) * numbers[:, None]
    both = jnp.stack([cos_table, sin_table])
    weight = (both.T[None, :, :, None] * deposit[:, None, None, :]).reshape(COMP, 2 * LAYERS)
    weight = jnp.pad(weight, ((0, 0), (0, LANES - 2 * LAYERS)))
    weight_hi = lax.reduce_precision(weight, 8, 7)
    weight_lo = (weight - weight_hi).astype(jnp.bfloat16)
    weights = [weight_hi.astype(jnp.bfloat16), weight_lo]

    pieces = widen(*unpack(chunks, tile))
    results = run_cycle(
        True, [*pieces, flags[:SUB], sea, gain_matrix, quad_matrix, waves, picker, *weights]
    )
    velocity_ext, north, east = results[3:]
    pieces = widen(*results[:3])
    chunks, stokes_ext = run_cycle(
        False, [*pieces, flags[SUB:], sea, gain_matrix, quad_matrix, north, east]
    )
    chunks = lax.all_to_all(chunks, "freq", split_axis=0, concat_axis=0, tiled=True)
    ocean_out = ocean(velocity_ext, stokes_ext, sea)
    ocean_out = ocean_out[:, :, : 2 * LAYERS].reshape(ROWS, COLS, 2, LAYERS)
    velocity_out = jnp.transpose(ocean_out, (2, 3, 0, 1))
    return (collect(chunks), velocity_out)


def solution(mesh):
    return jax.shard_map(
        body,
        mesh=mesh,
        in_specs=(
            P("freq", None, "band", None),
            P(None, None, "band", "freq"),
            P(),
            P(),
            P(),
            P(),
            P(),
            P(),
        ),
        out_specs=(P("freq", None, "band", None), P(None, None, "band", "freq")),
        check_vma=False,
    )
```

time: 162 us -> 133 us (0.82)
  starting transfers between devices: 86.7 us -> 43 us
  waiting for transfers between devices: 27.3 us -> 59.4 us
  local copies, waits for them, and re-layouts: 13.8 us -> 4.03 us
  Pallas kernels: 29 us -> 23.7 us
  matrix products: 1.75 us -> 0 us
    ppermute x20 -> x8, starting transfers between devices: 60.1 us -> 20.6 us  [the longest x2 7.44 us: widen(): from_last = lax.ppermute(to_next, 'freq', line(FREQS, -1))]
    ppermute x20 -> x8, waiting for transfers between devices: 5.05 us -> 23.6 us  [the longest x2 7.72 us: widen(): from_next = lax.ppermute(to_last, 'freq', line(FREQS, 1))]
    all_to_all x1, waiting for transfers between devices: 10.7 us -> 17.8 us  [body(): lax.all_to_all(spread(spectrum), 'freq', split_axis=0, concat_axis=0, til...]
    all_to_all x1, waiting for transfers between devices: 11.6 us -> 18 us  [body(): lax.all_to_all(chunks, 'freq', split_axis=0, concat_axis=0, tiled=True)]
    pallas_call x6 -> x8, Pallas kernels: 29 us -> 23.7 us  [the longest x6 17.6 us: call(): pl.pallas_call(kernel, out_shape=out_shape, in_specs=[vmem] * len(operand...]
    slice x12 -> x0, local copies, waits for them, and re-layouts: 5 us -> none  [the longest x8 4.8 us: body(): h[:, :, COMP:]]
    all_to_all x1, starting transfers between devices: 14.5 us -> 10.9 us  [body(): lax.all_to_all(chunks, 'freq', split_axis=0, concat_axis=0, tiled=True)]
    unnamed x28 -> x16, local copies, waits for them, and re-layouts: 3.4 us -> 1.09 us
  transfers between devices with their start and end apart: 22 -> 10, of which waited for: 6 -> 10; matrix products, arithmetic and copies ran while one was open for 7% -> 3% of each run, Pallas kernels for 4% -> 0%
where the time goes in v3:
time: 133 us; the launch traced here: 132 us
  waiting for transfers between devices  59.4 us (45%)
  starting transfers between devices  43 us (32%)
  Pallas kernels  23.7 us (18%)
  local copies, waits for them, and re-layouts  4.03 us (3%)
    all_to_all x1, waiting for transfers between devices, body(): lax.all_to_all(chunks, 'freq', split_axis=0, concat_axis=0, tiled=True)  18 us
    all_to_all x1, waiting for transfers between devices, body(): lax.all_to_all(spread(spectrum), 'freq', split_axis=0, concat_axis=0, til...  17.8 us
    pallas_call x6, Pallas kernels, call(): pl.pallas_call(kernel, out_shape=out_shape, in_specs=[vmem] * len(operand...  17.6 us
    all_to_all x1, starting transfers between devices, body(): lax.all_to_all(spread(spectrum), 'freq', split_axis=0, concat_axis=0, til...  11.5 us
    all_to_all x1, starting transfers between devices, body(): lax.all_to_all(chunks, 'freq', split_axis=0, concat_axis=0, tiled=True)  10.9 us
    ppermute x2, waiting for transfers between devices, widen(): from_next = lax.ppermute(to_last, 'freq', line(FREQS, 1))  7.72 us
    ppermute x2, waiting for transfers between devices, widen(): from_down = lax.ppermute(last, 'band', line(BANDS, -1))  7.64 us
    ppermute x2, starting transfers between devices, widen(): from_last = lax.ppermute(to_next, 'freq', line(FREQS, -1))  7.44 us
  transfers between devices with their start and end apart: 10, of which 10 were waited for; matrix products, arithmetic and copies ran while one was open for 3% of the time, Pallas kernels for 0%

profile of v3, /device:TPU:34, one launch (start us, length us, event | category | flops | bytes accessed | tf_op | source)
XLA Modules:
  0.0 132.3 jit_solution(1409392156164606061)
XLA Ops:
  0.6 1.1 copy-done.2
  1.7 3.0 %spread.1 = f32[32,36,128]{2,1,0:T(8,128)} custom-call(f32[576,256]{1,0:T(8,128)S(1)} %bitcast.18), custom_call_target="tpu_custom_call" | custom-call | tf_op jit(solution)/shard_map/spread/pallas_call | solution.py:285
  4.7 11.5 %all-to-all-start = ((f32[32,36,128]{2,1,0:T(8,128)}), f32[32,36,128]{2,1,0:T(8,128)S(1)}, u32[]{:S(2)}, u32[]{:S(2)}) async-start(f32[32,36,128]{2,1,0:T(8,128)} %spread.1), calls=%async_computation | async-start | bytes 1310720 | tf_op jit(solution)/shard_map/all_to_all | solution.py:353
  17.3 0.4 mul.135
  17.7 0.2 copy.20
  18.7 17.8 %all-to-all-done.x_ref = f32[32,36,128]{2,1,0:T(8,128)S(1)} async-done(((f32[32,36,128]{2,1,0:T(8,128)}), f32[32,36,128]{2,1,0:T(8,128)S(1)}, u32[]{:S(2)}, u32[]{:S(2)}) %all-to-all-start) | async-done | bytes 589856 | tf_op jit(solution)/shard_map/all_to_all | solution.py:353
  36.5 0.2 unpack.1
  36.7 2.3 %collective-permute-start = (f32[16,4,1280]{2,1,0:T(4,128)S(1)}, f32[16,4,1280]{2,1,0:T(4,128)S(1)}, u32[]{:S(2)}, u32[]{:S(2)}) collective-permute-start(f32[16,4,1280]{2,1,0:T(4,128)S(1)} %get-tuple-element.18), channel_id=1, source_target_pairs={{1,0},{2,1},{3,2},{4,3},{5,4},{6,5},{7,6},{8,7},{9,8},{10,9},{11,1... | collective-permute-start | bytes 983048 | tf_op jit(solution)/shard_map/ppermute | solution.py:59
  39.1 3.5 %collective-permute-start.1 = (f32[16,4,1280]{2,1,0:T(4,128)S(1)}, f32[16,4,1280]{2,1,0:T(4,128)S(1)}, u32[]{:S(2)}, u32[]{:S(2)}) collective-permute-start(f32[16,4,1280]{2,1,0:T(4,128)S(1)} %get-tuple-element.19), channel_id=1, source_target_pairs={{0,1},{1,2},{2,3},{3,4},{4,5},{5,6},{6,7},{7,8},{8,9},{9,10},{10,1... | collective-permute-start | bytes 983048 | tf_op jit(solution)/shard_map/ppermute | solution.py:60
  42.8 2.9 %collective-permute-done.from_next.refs_1_ = f32[16,4,1280]{2,1,0:T(4,128)S(1)} collective-permute-done((f32[16,4,1280]{2,1,0:T(4,128)S(1)}, f32[16,4,1280]{2,1,0:T(4,128)S(1)}, u32[]{:S(2)}, u32[]{:S(2)}) %collective-permute-start) | collective-permute-done | bytes 327712 | tf_op jit(solution)/shard_map/ppermute | solution.py:59
  45.7 2.3 %collective-permute-done.1.from_last.refs_2_ = f32[16,4,1280]{2,1,0:T(4,128)S(1)} collective-permute-done((f32[16,4,1280]{2,1,0:T(4,128)S(1)}, f32[16,4,1280]{2,1,0:T(4,128)S(1)}, u32[]{:S(2)}, u32[]{:S(2)}) %collective-permute-start.1) | collective-permute-done | bytes 327712 | tf_op jit(solution)/shard_map/ppermute | solution.py:60
  48.1 2.2 %collective-permute-start.2 = (f32[4,16,1280]{2,1,0:T(8,128)S(1)}, f32[4,16,1280]{2,1,0:T(8,128)S(1)}, u32[]{:S(2)}, u32[]{:S(2)}) collective-permute-start(f32[4,16,1280]{2,1,0:T(8,128)S(1)} %get-tuple-element.20), channel_id=1, source_target_pairs={{32,0},{64,32},{96,64},{128,96},{160,128},{192,160},{224,192},{33,... | collective-permute-start | bytes 983048 | tf_op jit(solution)/shard_map/ppermute | solution.py:62
  50.3 2.4 %collective-permute-start.3 = (f32[4,16,1280]{2,1,0:T(8,128)S(1)}, f32[4,16,1280]{2,1,0:T(8,128)S(1)}, u32[]{:S(2)}, u32[]{:S(2)}) collective-permute-start(f32[4,16,1280]{2,1,0:T(8,128)S(1)} %get-tuple-element.21), channel_id=1, source_target_pairs={{0,32},{32,64},{64,96},{96,128},{128,160},{160,192},{192,224},{1,3... | collective-permute-start | bytes 983048 | tf_op jit(solution)/shard_map/ppermute | solution.py:63
  53.0 1.9 %collective-permute-done.2.refs_3_ = f32[4,16,1280]{2,1,0:T(8,128)S(1)} collective-permute-done((f32[4,16,1280]{2,1,0:T(8,128)S(1)}, f32[4,16,1280]{2,1,0:T(8,128)S(1)}, u32[]{:S(2)}, u32[]{:S(2)}) %collective-permute-start.2) | collective-permute-done | bytes 327712 | tf_op jit(solution)/shard_map/ppermute | solution.py:62
  54.9 3.8 %collective-permute-done.3.refs_4_ = f32[4,16,1280]{2,1,0:T(8,128)S(1)} collective-permute-done((f32[4,16,1280]{2,1,0:T(8,128)S(1)}, f32[4,16,1280]{2,1,0:T(8,128)S(1)}, u32[]{:S(2)}, u32[]{:S(2)}) %collective-permute-start.3) | collective-permute-done | bytes 327712 | tf_op jit(solution)/shard_map/ppermute | solution.py:63
  58.8 0.3 broadcast_in_dim.10.refs_5_
  59.1 8.7 %cycle_first.1 = (f32[16,8,1280]{2,1,0:T(8,128)S(1)}, f32[16,4,1280]{2,1,0:T(4,128)S(1)}, f32[16,4,1280]{2,1,0:T(4,128)S(1)}, f32[24,16,128]{2,1,0:T(8,128)S(1)}...) custom-call(f32[16,8,1280]{2,1,0:T(8,128)S(1)} %get-tuple-element.17.own.refs_0_, ...), custom_call_target="tpu_custom_call" | custom-call | tf_op jit(solution)/shard_map/cycle_first/pallas_call | solution.py:269
  67.8 1.9 %collective-permute-start.4 = (f32[16,4,1280]{2,1,0:T(4,128)S(1)}, f32[16,4,1280]{2,1,0:T(4,128)S(1)}, u32[]{:S(2)}, u32[]{:S(2)}) collective-permute-start(f32[16,4,1280]{2,1,0:T(4,128)S(1)} %get-tuple-element.23), channel_id=1, source_target_pairs={{1,0},{2,1},{3,2},{4,3},{5,4},{6,5},{7,6},{8,7},{9,8},{10,9},{11,1... | collective-permute-start | bytes 983048 | tf_op jit(solution)/shard_map/ppermute | solution.py:59
  69.7 3.9 %collective-permute-start.5 = (f32[16,4,1280]{2,1,0:T(4,128)S(1)}, f32[16,4,1280]{2,1,0:T(4,128)S(1)}, u32[]{:S(2)}, u32[]{:S(2)}) collective-permute-start(f32[16,4,1280]{2,1,0:T(4,128)S(1)} %get-tuple-element.24), channel_id=1, source_target_pairs={{0,1},{1,2},{2,3},{3,4},{4,5},{5,6},{6,7},{7,8},{8,9},{9,10},{10,1... | collective-permute-start | bytes 983048 | tf_op jit(solution)/shard_map/ppermute | solution.py:60
  73.7 4.8 %collective-permute-done.4.from_next.refs_1_ = f32[16,4,1280]{2,1,0:T(4,128)S(1)} collective-permute-done((f32[16,4,1280]{2,1,0:T(4,128)S(1)}, f32[16,4,1280]{2,1,0:T(4,128)S(1)}, u32[]{:S(2)}, u32[]{:S(2)}) %collective-permute-start.4) | collective-permute-done | bytes 327712 | tf_op jit(solution)/shard_map/ppermute | solution.py:59
  78.4 1.9 %collective-permute-done.5.from_last.refs_2_ = f32[16,4,1280]{2,1,0:T(4,128)S(1)} collective-permute-done((f32[16,4,1280]{2,1,0:T(4,128)S(1)}, f32[16,4,1280]{2,1,0:T(4,128)S(1)}, u32[]{:S(2)}, u32[]{:S(2)}) %collective-permute-start.5) | collective-permute-done | bytes 327712 | tf_op jit(solution)/shard_map/ppermute | solution.py:60
  80.4 1.9 %collective-permute-start.6 = (f32[4,16,1280]{2,1,0:T(8,128)S(1)}, f32[4,16,1280]{2,1,0:T(8,128)S(1)}, u32[]{:S(2)}, u32[]{:S(2)}) collective-permute-start(f32[4,16,1280]{2,1,0:T(8,128)S(1)} %get-tuple-element.25), channel_id=1, source_target_pairs={{32,0},{64,32},{96,64},{128,96},{160,128},{192,160},{224,192},{33,... | collective-permute-start | bytes 983048 | tf_op jit(solution)/shard_map/ppermute | solution.py:62
  82.4 2.4 %collective-permute-start.7 = (f32[4,16,1280]{2,1,0:T(8,128)S(1)}, f32[4,16,1280]{2,1,0:T(8,128)S(1)}, u32[]{:S(2)}, u32[]{:S(2)}) collective-permute-start(f32[4,16,1280]{2,1,0:T(8,128)S(1)} %get-tuple-element.26), channel_id=1, source_target_pairs={{0,32},{32,64},{64,96},{96,128},{128,160},{160,192},{192,224},{1,3... | collective-permute-start | bytes 983048 | tf_op jit(solution)/shard_map/ppermute | solution.py:63
  84.8 2.2 %collective-permute-done.6.refs_3_ = f32[4,16,1280]{2,1,0:T(8,128)S(1)} collective-permute-done((f32[4,16,1280]{2,1,0:T(8,128)S(1)}, f32[4,16,1280]{2,1,0:T(8,128)S(1)}, u32[]{:S(2)}, u32[]{:S(2)}) %collective-permute-start.6) | collective-permute-done | bytes 327712 | tf_op jit(solution)/shard_map/ppermute | solution.py:62
  86.9 3.8 %collective-permute-done.7.refs_4_ = f32[4,16,1280]{2,1,0:T(8,128)S(1)} collective-permute-done((f32[4,16,1280]{2,1,0:T(8,128)S(1)}, f32[4,16,1280]{2,1,0:T(8,128)S(1)}, u32[]{:S(2)}, u32[]{:S(2)}) %collective-permute-start.7) | collective-permute-done | bytes 327712 | tf_op jit(solution)/shard_map/ppermute | solution.py:63
  90.8 0.3 broadcast_in_dim.14.refs_5_
  91.0 8.1 %cycle_last.1 = (f32[32,36,128]{2,1,0:T(8,128)}, f32[24,16,128]{2,1,0:T(8,128)S(1)}) custom-call(f32[16,8,1280]{2,1,0:T(8,128)S(1)} %get-tuple-element.22.own.refs_0_, f32[16,4,1280]{2,1,0:T(4,128)S(1)} %collective-permute-done.4.from_next.refs_1_, f32[16,4,1280]{2,1,0:T(4,128)S(1)} %collective-permute-done.5.from_last.refs_2_, ...), custom_call_target="tpu_custom_call" | custom-call | tf_op jit(solution)/shard_map/cycle_last/pallas_call | solution.py:269
  99.1 10.9 %all-to-all-start.1 = ((f32[32,36,128]{2,1,0:T(8,128)}), f32[32,36,128]{2,1,0:T(8,128)S(1)}, u32[]{:S(2)}, u32[]{:S(2)}) async-start(f32[32,36,128]{2,1,0:T(8,128)} %get-tuple-element.29), calls=%async_computation.1 | async-start | bytes 1310720 | tf_op jit(solution)/shard_map/all_to_all | solution.py:399
  110.0 0.5 ocean.1
  110.7 0.7 copy.23
  111.3 18.0 %all-to-all-done.1.x_ref = f32[32,36,128]{2,1,0:T(8,128)S(1)} async-done(((f32[32,36,128]{2,1,0:T(8,128)}), f32[32,36,128]{2,1,0:T(8,128)S(1)}, u32[]{:S(2)}, u32[]{:S(2)}) %all-to-all-start.1) | async-done | bytes 589856 | tf_op jit(solution)/shard_map/all_to_all | solution.py:399
  129.3 3.0 %collect.1 = f32[576,256]{1,0:T(8,128)} custom-call(f32[32,36,128]{2,1,0:T(8,128)S(1)} %all-to-all-done.1.x_ref), custom_call_target="tpu_custom_call" | custom-call | tf_op jit(solution)/shard_map/collect/pallas_call | solution.py:285
  (48 shorter events, 2.5 us)
Async XLA Ops:
  0.6 1.1 copy-start.2
  1.7 14.6 %copy-start.4 = (s32[128,256]{1,0:T(8,128)S(1)}, s32[128,256]{1,0:T(8,128)}, u32[]{:S(2)}) copy-start(s32[128,256]{1,0:T(8,128)} %param.14) | copy-start | bytes 393220
  1.7 14.8 %copy-start.3 = (s32[8,128,256]{2,1,0:T(8,128)S(1)}, s32[8,128,256]{2,1,0:T(8,128)}, u32[]{:S(2)}) copy-start(s32[8,128,256]{2,1,0:T(8,128)} %param.13) | copy-start | bytes 3145732
  1.7 15.0 %copy-start.5 = (f32[2,24,16,8]{1,3,2,0:T(8,128)S(1)}, f32[2,24,16,8]{1,3,2,0:T(8,128)}, u32[]{:S(2)}) copy-start(f32[2,24,16,8]{1,3,2,0:T(8,128)} %param.10) | copy-start | bytes 73732
  4.7 12.3 %copy-start.6 = (s32[32,4]{0,1:T(4,128)S(1)}, s32[32,4]{0,1:T(4,128)}, u32[]{:S(2)}) copy-start(s32[32,4]{0,1:T(4,128)} %param.16) | copy-start | bytes 1540
  4.7 31.8 %all-to-all-start = ((f32[32,36,128]{2,1,0:T(8,128)}), f32[32,36,128]{2,1,0:T(8,128)S(1)}, u32[]{:S(2)}, u32[]{:S(2)}) async-start(f32[32,36,128]{2,1,0:T(8,128)} %spread.1), calls=%async_computation | async-start | bytes 1310720 | tf_op jit(solution)/shard_map/all_to_all | solution.py:353
  16.6 1.6 %copy-start.7 = (s32[32]{0:T(128)S(1)}, s32[32]{0:T(128)}, u32[]{:S(2)}) copy-start(s32[32]{0:T(128)} %param.15) | copy-start | bytes 388
  36.7 9.0 %collective-permute-start = (f32[16,4,1280]{2,1,0:T(4,128)S(1)}, f32[16,4,1280]{2,1,0:T(4,128)S(1)}, u32[]{:S(2)}, u32[]{:S(2)}) collective-permute-start(f32[16,4,1280]{2,1,0:T(4,128)S(1)} %get-tuple-element.18), channel_id=1, source_target_pairs={{1,0},{2,1},{3,2},{4,3},{5,4},{6,5},{7,6},{8,7},{9,8},{10,9},{11,1... | collective-permute-start | bytes 983048 | tf_op jit(solution)/shard_map/ppermute | solution.py:59
  39.1 9.0 %collective-permute-start.1 = (f32[16,4,1280]{2,1,0:T(4,128)S(1)}, f32[16,4,1280]{2,1,0:T(4,128)S(1)}, u32[]{:S(2)}, u32[]{:S(2)}) collective-permute-start(f32[16,4,1280]{2,1,0:T(4,128)S(1)} %get-tuple-element.19), channel_id=1, source_target_pairs={{0,1},{1,2},{2,3},{3,4},{4,5},{5,6},{6,7},{7,8},{8,9},{9,10},{10,1... | collective-permute-start | bytes 983048 | tf_op jit(solution)/shard_map/ppermute | solution.py:60
  42.7 16.4 %copy-start.1 = (bf16[1152,1152]{1,0:T(8,128)(2,1)S(1)}, bf16[1152,1152]{1,0:T(8,128)(2,1)}, u32[]{:S(2)}) copy-start(bf16[1152,1152]{1,0:T(8,128)(2,1)} %refs_8_.3) | copy-start | bytes 7962628
  48.1 11.0 %copy-start = (bf16[1152,1152]{1,0:T(8,128)(2,1)S(1)}, bf16[1152,1152]{1,0:T(8,128)(2,1)}, u32[]{:S(2)}) copy-start(bf16[1152,1152]{1,0:T(8,128)(2,1)} %refs_7_.3) | copy-start | bytes 7962628
  48.1 6.8 %collective-permute-start.2 = (f32[4,16,1280]{2,1,0:T(8,128)S(1)}, f32[4,16,1280]{2,1,0:T(8,128)S(1)}, u32[]{:S(2)}, u32[]{:S(2)}) collective-permute-start(f32[4,16,1280]{2,1,0:T(8,128)S(1)} %get-tuple-element.20), channel_id=1, source_target_pairs={{32,0},{64,32},{96,64},{128,96},{160,128},{192,160},{224,192},{33,... | collective-permute-start | bytes 983048 | tf_op jit(solution)/shard_map/ppermute | solution.py:62
  50.3 8.4 %collective-permute-start.3 = (f32[4,16,1280]{2,1,0:T(8,128)S(1)}, f32[4,16,1280]{2,1,0:T(8,128)S(1)}, u32[]{:S(2)}, u32[]{:S(2)}) collective-permute-start(f32[4,16,1280]{2,1,0:T(8,128)S(1)} %get-tuple-element.21), channel_id=1, source_target_pairs={{0,32},{32,64},{64,96},{96,128},{128,160},{160,192},{192,224},{1,3... | collective-permute-start | bytes 983048 | tf_op jit(solution)/shard_map/ppermute | solution.py:63
  67.8 10.6 %collective-permute-start.4 = (f32[16,4,1280]{2,1,0:T(4,128)S(1)}, f32[16,4,1280]{2,1,0:T(4,128)S(1)}, u32[]{:S(2)}, u32[]{:S(2)}) collective-permute-start(f32[16,4,1280]{2,1,0:T(4,128)S(1)} %get-tuple-element.23), channel_id=1, source_target_pairs={{1,0},{2,1},{3,2},{4,3},{5,4},{6,5},{7,6},{8,7},{9,8},{10,9},{11,1... | collective-permute-start | bytes 983048 | tf_op jit(solution)/shard_map/ppermute | solution.py:59
  69.7 10.6 %collective-permute-start.5 = (f32[16,4,1280]{2,1,0:T(4,128)S(1)}, f32[16,4,1280]{2,1,0:T(4,128)S(1)}, u32[]{:S(2)}, u32[]{:S(2)}) collective-permute-start(f32[16,4,1280]{2,1,0:T(4,128)S(1)} %get-tuple-element.24), channel_id=1, source_target_pairs={{0,1},{1,2},{2,3},{3,4},{4,5},{5,6},{6,7},{7,8},{8,9},{9,10},{10,1... | collective-permute-start | bytes 983048 | tf_op jit(solution)/shard_map/ppermute | solution.py:60
  80.4 6.5 %collective-permute-start.6 = (f32[4,16,1280]{2,1,0:T(8,128)S(1)}, f32[4,16,1280]{2,1,0:T(8,128)S(1)}, u32[]{:S(2)}, u32[]{:S(2)}) collective-permute-start(f32[4,16,1280]{2,1,0:T(8,128)S(1)} %get-tuple-element.25), channel_id=1, source_target_pairs={{32,0},{64,32},{96,64},{128,96},{160,128},{192,160},{224,192},{33,... | collective-permute-start | bytes 983048 | tf_op jit(solution)/shard_map/ppermute | solution.py:62
  82.4 8.4 %collective-permute-start.7 = (f32[4,16,1280]{2,1,0:T(8,128)S(1)}, f32[4,16,1280]{2,1,0:T(8,128)S(1)}, u32[]{:S(2)}, u32[]{:S(2)}) collective-permute-start(f32[4,16,1280]{2,1,0:T(8,128)S(1)} %get-tuple-element.26), channel_id=1, source_target_pairs={{0,32},{32,64},{64,96},{96,128},{128,160},{160,192},{192,224},{1,3... | collective-permute-start | bytes 983048 | tf_op jit(solution)/shard_map/ppermute | solution.py:63
  99.1 30.2 %all-to-all-start.1 = ((f32[32,36,128]{2,1,0:T(8,128)}), f32[32,36,128]{2,1,0:T(8,128)S(1)}, u32[]{:S(2)}, u32[]{:S(2)}) async-start(f32[32,36,128]{2,1,0:T(8,128)} %get-tuple-element.29), calls=%async_computation.1 | async-start | bytes 1310720 | tf_op jit(solution)/shard_map/all_to_all | solution.py:399

commit v4 on v3

--- a/solution.py
+++ b/solution.py
@@ -21,6 +21,7 @@
 LANES = 128
 GROUPS = 9
 WIDE = COMP + LANES
+QUADS = COMP // 4
 
 precise = lax.Precision.HIGHEST
 ocean_dt = 0.2
@@ -89,20 +90,56 @@
     return tiles
 
 
-def spread_kernel(x_ref, o_ref, half_ref):
-    for half in range(2):
-        half_ref[half] = x_ref[:, half * LANES : (half + 1) * LANES]
-        tiles = [half_ref[half, pl.ds(r, 8, stride=ROWS), :] for r in range(ROWS)]
+def direction_groups():
+    for index in range(5):
+        count = min(8, DIR - 8 * index)
+        for half in range(2):
+            yield index, count, half, 2 * index + half
+
+
+def rows_copy(hbm_ref, vmem_ref, sems, group, outward):
+    index, count, half, slot = group
+    far = hbm_ref.at[pl.ds(index * 8 * ROWS, count * ROWS), pl.ds(half * LANES, LANES)]
+    near = vmem_ref.at[slot, pl.ds(0, count * ROWS)]
+    pair = (near, far) if outward else (far, near)
+    return pltpu.make_async_copy(*pair, sems.at[slot])
+
+
+def spread_kernel(x_hbm, o_hbm, half_ref, chunk_ref, in_sems, out_sems):
+    copies = [rows_copy(x_hbm, half_ref, in_sems, group, False) for group in direction_groups()]
+    for copy in copies:
+        copy.start()
+    sent = []
+    for index, count, half, slot in direction_groups():
+        copies[slot].wait()
+        tiles = [half_ref[slot, pl.ds(r, count, stride=ROWS), :] for r in range(ROWS)]
         for i, tile in enumerate(swap_blocks(tiles)):
-            o_ref[half * ROWS + i] = tile
-
-
-def collect_kernel(x_ref, o_ref, half_ref):
-    for half in range(2):
-        tiles = [x_ref[half * ROWS + i] for i in range(ROWS)]
+            for j in range(count // 4):
+                chunk_ref[half * ROWS + i, 2 * index + j] = tile[4 * j : 4 * j + 4]
+        if half:
+            part = pl.ds(2 * index, count // 4)
+            sent.append(
+                pltpu.make_async_copy(chunk_ref.at[:, part], o_hbm.at[:, part], out_sems.at[index])
+            )
+            sent[-1].start()
+    for copy in sent:
+        copy.wait()
+
+
+def collect_kernel(x_ref, o_hbm, half_ref, sems):
+    copies = []
+    for group in direction_groups():
+        index, count, half, slot = group
+        tiles = []
+        for i in range(ROWS):
+            quads = [x_ref[half * ROWS + i, 2 * index + j] for j in range(count // 4)]
+            tiles.append(jnp.concatenate(quads, axis=0))
         for r, tile in enumerate(swap_blocks(tiles)):
-            half_ref[half, pl.ds(r, 8, stride=ROWS), :] = tile
-        o_ref[:, half * LANES : (half + 1) * LANES] = half_ref[half]
+            half_ref[slot, pl.ds(r, count, stride=ROWS), :] = tile
+        copies.append(rows_copy(o_hbm, half_ref, sems, group, True))
+        copies[-1].start()
+    for copy in copies:
+        copy.wait()
 
 
 def ends_kernel(own, from_next, from_last, first_ref, last_ref):
@@ -120,20 +157,20 @@
 
 def unpack_kernel(x_ref, u_ref, *rest):
     out_refs, flat_ref = rest[:-1], rest[-1]
-    for g in range(FREQS):
-        flat_ref[pl.ds(g * DIR, DIR), :] = x_ref[g]
+    for q in range(QUADS):
+        flat_ref[4 * q : 4 * q + 4, :] = x_ref[q]
     for k in range(GROUPS):
         lanes = slice(k * LANES, (k + 1) * LANES)
         put(jnp.transpose(flat_ref[lanes, :]).reshape(ROWS, COLS, LANES), out_refs, lanes)
     put(u_ref[...], out_refs, slice(COMP, WIDE))
 
 
-def face_flux(lower, upper, half_courant, second):
-    q = jnp.where(second, (half_courant + half_courant) * half_courant, jnp.abs(half_courant))
+def face_flux(lower, upper, half_courant, half_square, second):
+    q = jnp.where(second, half_square, jnp.abs(half_courant))
     return lower * (half_courant + q) + upper * (half_courant - q)
 
 
-def courants(ext_ref, lane_ref, pick_ref, north_ref, east_ref):
+def courants(ext_ref, lane_ref, pick_ref, face_refs):
     lane = lax.broadcasted_iota(jnp.int32, (EXT_C, LANES), 1)
     quarter = (0.25 * 0.15) * jnp.tanh(ext_ref[...])
     faces = []
@@ -142,14 +179,16 @@
         along_cols = quarter[r] + pltpu.roll(quarter[r], 1, 0)
         faces.append(jnp.where(lane < LAYERS, along_cols, along_rows))
     faces = jnp.concatenate(faces, axis=0)
-    high = faces.astype(jnp.bfloat16)
-    rest = faces - high.astype(f32)
-    middle = rest.astype(jnp.bfloat16)
-    low = (rest - middle.astype(f32)).astype(jnp.bfloat16)
-    parts = jnp.concatenate([high, middle, low], axis=1)
-    for index, ref in ((0, east_ref), (1, north_ref)):
+    high = faces.astype(jnp.bfloat16).astype(f32)
+    rest = faces - high
+    middle = rest.astype(jnp.bfloat16).astype(f32)
+    parts = jnp.concatenate([high + pltpu.roll(middle, LANES // 2, 1), rest - middle], axis=1)
+    parts = parts.astype(jnp.bfloat16)
+    for index in range(2):
         picked = jnp.dot(parts, pick_ref[index], preferred_element_type=f32)
-        ref[...] = (lane_ref[index] + picked).reshape(EXT_R, EXT_C, COMP)
+        half_courant = (lane_ref[index] + picked).reshape(EXT_R, EXT_C, COMP)
+        face_refs[2 * index][...] = half_courant
+        face_refs[2 * index + 1][...] = (half_courant + half_courant) * half_courant
 
 
 def cycle_kernel(first, *refs):
@@ -157,17 +196,23 @@
     take = lambda n: [refs.pop(0) for _ in range(n)]
     pieces = take(5)
     flag_ref, sea_ref, gain_ref, quad_ref = take(4)
+    flag_base = 0 if first else SUB
     if first:
         lane_ref, pick_ref, weight_hi, weight_lo = take(4)
         out_refs = take(3)
-        ext_ref, north_ref, east_ref = take(3)
+        (ext_ref,) = take(1)
+        face_refs = take(4)
     else:
-        north_ref, east_ref = take(2)
-        out_ref, ext_ref = take(2)
+        face_refs = take(4)
+        out_hbm, ext_ref = take(2)
     tile_ref, energy_ref = take(2)
+    if not first:
+        chunk_ref, sems = take(2)
     fill(ext_ref, pieces, slice(COMP, WIDE))
     if first:
-        courants(ext_ref, lane_ref, pick_ref, north_ref, east_ref)
+        courants(ext_ref, lane_ref, pick_ref, face_refs)
+    east, east_square, north, north_square = face_refs
+    copies = []
 
     def advect(k, carry):
         lanes = pl.ds(pl.multiple_of(k * LANES, LANES), LANES)
@@ -175,16 +220,22 @@
         for s in range(SUB):
             here = tile_ref[s]
             above = tile_ref[s + 1]
-            flag = flag_ref[s, s + 1] != 0.0
-            flux_below = face_flux(here, above, north_ref[s, :, lanes], flag)
+            flag = flag_ref[flag_base + s, s + 1] != 0.0
+            flux_below = face_flux(here, above, north[s, :, lanes], north_square[s, :, lanes], flag)
             for r in range(s + 1, EXT_R - 1 - s):
                 here = above
                 above = tile_ref[r + 1]
-                flag_above = flag_ref[s, r + 1] != 0.0
-                flux_above = face_flux(here, above, north_ref[r, :, lanes], flag_above)
+                flag_above = flag_ref[flag_base + s, r + 1] != 0.0
+                flux_above = face_flux(
+                    here, above, north[r, :, lanes], north_square[r, :, lanes], flag_above
+                )
                 shifted = here - (flux_above - flux_below)
                 flux_east = face_flux(
-                    pltpu.roll(shifted, 1, 0), shifted, east_ref[r, :, lanes], flag
+                    pltpu.roll(shifted, 1, 0),
+                    shifted,
+                    east[r, :, lanes],
+                    east_square[r, :, lanes],
+                    flag,
                 )
                 result = shifted - (pltpu.roll(flux_east, EXT_C - 1, 0) - flux_east)
                 result = result * sea_ref[r]
@@ -218,13 +269,13 @@
             put(updated.reshape(ROWS, COLS, LANES), out_refs, lanes)
         else:
             flat = jnp.transpose(updated)
-            start = k * LANES
-            while start < (k + 1) * LANES:
-                g, d = divmod(start, DIR)
-                count = min(DIR - d, (k + 1) * LANES - start)
-                at = start - k * LANES
-                out_ref[g, d : d + count, :] = flat[at : at + count, :]
-                start += count
+            for q in range(32):
+                chunk_ref[32 * k + q] = flat[4 * q : 4 * q + 4]
+            part = pl.ds(32 * k, 32)
+            copies.append(pltpu.make_async_copy(chunk_ref.at[part], out_hbm.at[part], sems.at[k]))
+            copies[-1].start()
+    for copy in copies:
+        copy.wait()
 
 
 def ocean_kernel(u_ref, drift_ref, sea_ref, o_ref, now_ref):
@@ -263,45 +314,38 @@
 
 
 vmem = pl.BlockSpec(memory_space=pltpu.VMEM)
-
-
-def call(kernel, name, operands, out_shape, scratch, mebibytes):
+hbm = pl.BlockSpec(memory_space=pltpu.HBM)
+
+
+def call(kernel, name, operands, out_shape, scratch, mebibytes, in_specs=None, out_specs=None):
     return pl.pallas_call(
         kernel,
         out_shape=out_shape,
-        in_specs=[vmem] * len(operands),
-        out_specs=jax.tree.map(lambda _: vmem, out_shape),
-        scratch_shapes=[pltpu.VMEM(shape, f32) for shape in scratch],
+        in_specs=in_specs or [vmem] * len(operands),
+        out_specs=out_specs or jax.tree.map(lambda _: vmem, out_shape),
+        scratch_shapes=[pltpu.VMEM(x, f32) if isinstance(x, tuple) else x for x in scratch],
         compiler_params=pltpu.CompilerParams(vmem_limit_bytes=mebibytes * 2**20),
         name=name,
     )(*operands)
 
 
-by_rows = pl.BlockSpec((8 * ROWS, 2 * LANES), lambda i: (i, 0))
-by_chunks = pl.BlockSpec((FREQS, 8, LANES), lambda i: (0, i, 0))
-
-
-def relayout(kernel, name, x, in_spec, out_spec, out_shape):
-    return pl.pallas_call(
-        kernel,
-        grid=(pl.cdiv(DIR, 8),),
-        out_shape=out_shape,
-        in_specs=[in_spec],
-        out_specs=out_spec,
-        scratch_shapes=[pltpu.VMEM((2, 8 * ROWS, LANES), f32)],
-        compiler_params=pltpu.CompilerParams(vmem_limit_bytes=4 * 2**20),
-        name=name,
-    )(x)
+halves = (10, 8 * ROWS, LANES)
+chunks_dims = (FREQS, DIR // 4, 4, LANES)
+sems = pltpu.SemaphoreType.DMA
 
 
 def spread(x):
     x = x.reshape(DIR * ROWS, 2 * LANES)
-    return relayout(spread_kernel, "spread", x, by_rows, by_chunks, shape_of(FREQS, DIR, LANES))
+    scratch = [halves, chunks_dims, sems((10,)), sems((5,))]
+    out = call(spread_kernel, "spread", [x], shape_of(*chunks_dims), scratch, 4, [hbm], hbm)
+    return out.reshape(QUADS, 4, LANES)
 
 
 def collect(x):
     out_shape = shape_of(DIR * ROWS, 2 * LANES)
-    out = relayout(collect_kernel, "collect", x, by_chunks, by_rows, out_shape)
+    scratch = [halves, sems((10,))]
+    x = x.reshape(chunks_dims)
+    out = call(collect_kernel, "collect", [x], out_shape, scratch, 4, [vmem], hbm)
     return out.reshape(1, DIR, ROWS, 2 * LANES)
 
 
@@ -319,18 +363,17 @@
 
 
 def run_cycle(first, operands):
+    scratch = [(EXT_R, EXT_C, LANES), (ROWS, COLS, COMP)]
     if first:
-        out_shape = tile_shapes + [ext_shape, face_shape, face_shape]
+        out_shape = tile_shapes + [ext_shape] + [face_shape] * 4
+        out_specs = [vmem] * 8
     else:
-        out_shape = [shape_of(FREQS, DIR, LANES), ext_shape]
-    return call(
-        lambda *refs: cycle_kernel(first, *refs),
-        "cycle_first" if first else "cycle_last",
-        operands,
-        out_shape,
-        [(EXT_R, EXT_C, LANES), (ROWS, COLS, COMP)],
-        24,
-    )
+        out_shape = [shape_of(QUADS, 4, LANES), ext_shape]
+        out_specs = [hbm, vmem]
+        scratch += [(QUADS, 4, LANES), sems((GROUPS,))]
+    kernel = lambda *refs: cycle_kernel(first, *refs)
+    name = "cycle_first" if first else "cycle_last"
+    return call(kernel, name, operands, out_shape, scratch, 24, None, out_specs)
 
 
 def ocean(velocity, stokes, sea):
@@ -362,8 +405,9 @@
     lane_ids = jnp.arange(LANES, dtype=jnp.int32)[None, :, None]
     routes = jnp.repeat(current_route, DIR)[None, None, :]
     starts = jnp.array([0, LAYERS], jnp.int32)[:, None, None]
-    picker = (lane_ids == routes + starts).astype(jnp.bfloat16)
-    picker = jnp.concatenate([picker] * 3, axis=1)
+    wanted = routes + starts
+    high = (lane_ids == wanted) | (lane_ids == wanted + LANES // 2)
+    picker = jnp.concatenate([high, lane_ids == wanted], axis=1).astype(jnp.bfloat16)
 
     def window(grid):
         padded = jnp.pad(grid, ((0, 0), (HALO, HALO), (HALO, HALO))).astype(f32)
@@ -387,15 +431,12 @@
     weight_lo = (weight - weight_hi).astype(jnp.bfloat16)
     weights = [weight_hi.astype(jnp.bfloat16), weight_lo]
 
+    fixed = [flags, sea, gain_matrix, quad_matrix]
     pieces = widen(*unpack(chunks, tile))
-    results = run_cycle(
-        True, [*pieces, flags[:SUB], sea, gain_matrix, quad_matrix, waves, picker, *weights]
-    )
-    velocity_ext, north, east = results[3:]
+    results = run_cycle(True, [*pieces, *fixed, waves, picker, *weights])
+    velocity_ext, faces = results[3], results[4:]
     pieces = widen(*results[:3])
-    chunks, stokes_ext = run_cycle(
-        False, [*pieces, flags[SUB:], sea, gain_matrix, quad_matrix, north, east]
-    )
+    chunks, stokes_ext = run_cycle(False, [*pieces, *fixed, *faces])
     chunks = lax.all_to_all(chunks, "freq", split_axis=0, concat_axis=0, tiled=True)
     ocean_out = ocean(velocity_ext, stokes_ext, sea)
     ocean_out = ocean_out[:, :, : 2 * LAYERS].reshape(ROWS, COLS, 2, LAYERS)

time: 133 us -> 129 us (0.970)
  waiting for transfers between devices: 59.4 us -> 56.3 us
    all_to_all x1, waiting for transfers between devices: 17.8 us -> 16.3 us  [body(): lax.all_to_all(spread(spectrum), 'freq', split_axis=0, concat_axis=0, til...]
where the time goes in v4:
time: 129 us; the launch traced here: 128 us
  waiting for transfers between devices  56.3 us (44%)
  starting transfers between devices  42.8 us (33%)
  Pallas kernels  22.8 us (18%)
  local copies, waits for them, and re-layouts  3.97 us (3%)
  other arithmetic  1.4 us (1%)
    pallas_call x8, Pallas kernels, call(): pl.pallas_call(kernel, out_shape=out_shape, in_specs=in_specs or [vmem] *...  22.8 us
    all_to_all x1, waiting for transfers between devices, body(): lax.all_to_all(chunks, 'freq', split_axis=0, concat_axis=0, tiled=True)  16.7 us
    all_to_all x1, waiting for transfers between devices, body(): lax.all_to_all(spread(spectrum), 'freq', split_axis=0, concat_axis=0, til...  16.3 us
    all_to_all x1, starting transfers between devices, body(): lax.all_to_all(spread(spectrum), 'freq', split_axis=0, concat_axis=0, til...  11.5 us
    all_to_all x1, starting transfers between devices, body(): lax.all_to_all(chunks, 'freq', split_axis=0, concat_axis=0, tiled=True)  11 us
    ppermute x2, waiting for transfers between devices, widen(): from_next = lax.ppermute(to_last, 'freq', line(FREQS, 1))  7.95 us
    ppermute x2, starting transfers between devices, widen(): from_last = lax.ppermute(to_next, 'freq', line(FREQS, -1))  7.85 us
    ppermute x2, waiting for transfers between devices, widen(): from_down = lax.ppermute(last, 'band', line(BANDS, -1))  7.64 us
  transfers between devices with their start and end apart: 10, of which 10 were waited for; matrix products, arithmetic and copies ran while one was open for 3% of the time, Pallas kernels for 0%

profile of v4, /device:TPU:34, one launch (start us, length us, event | category | flops | bytes accessed | tf_op | source)
XLA Modules:
  0.0 128.2 jit_solution(13483508018024745352)
XLA Ops:
  0.7 1.1 copy-done.2
  1.7 3.9 %spread.1 = f32[32,9,4,128]{3,2,1,0:T(4,128)} custom-call(f32[576,256]{1,0:T(8,128)S(1)} %bitcast.21), custom_call_target="tpu_custom_call" | custom-call | tf_op jit(solution)/shard_map/spread/pallas_call | solution.py:321
  5.6 11.5 %all-to-all-start = ((f32[288,4,128]{2,1,0:T(4,128)}), f32[288,4,128]{2,1,0:T(4,128)S(1)}, u32[]{:S(2)}, u32[]{:S(2)}) async-start(f32[288,4,128]{2,1,0:T(4,128)} %bitcast.1), calls=%async_computation | async-start | bytes 1179648 | tf_op jit(solution)/shard_map/all_to_all | solution.py:396
  18.7 0.4 mul.135
  19.1 0.2 copy.20
  19.5 0.3 fusion
  19.8 16.3 %all-to-all-done.x_ref = f32[288,4,128]{2,1,0:T(4,128)S(1)} async-done(((f32[288,4,128]{2,1,0:T(4,128)}), f32[288,4,128]{2,1,0:T(4,128)S(1)}, u32[]{:S(2)}, u32[]{:S(2)}) %all-to-all-start) | async-done | bytes 589856 | tf_op jit(solution)/shard_map/all_to_all | solution.py:396
  36.1 0.2 unpack.1
  36.4 1.9 %collective-permute-start = (f32[16,4,1280]{2,1,0:T(4,128)S(1)}, f32[16,4,1280]{2,1,0:T(4,128)S(1)}, u32[]{:S(2)}, u32[]{:S(2)}) collective-permute-start(f32[16,4,1280]{2,1,0:T(4,128)S(1)} %get-tuple-element.20), channel_id=1, source_target_pairs={{1,0},{2,1},{3,2},{4,3},{5,4},{6,5},{7,6},{8,7},{9,8},{10,9},{11,1... | collective-permute-start | bytes 983048 | tf_op jit(solution)/shard_map/ppermute | solution.py:60
  38.3 3.9 %collective-permute-start.1 = (f32[16,4,1280]{2,1,0:T(4,128)S(1)}, f32[16,4,1280]{2,1,0:T(4,128)S(1)}, u32[]{:S(2)}, u32[]{:S(2)}) collective-permute-start(f32[16,4,1280]{2,1,0:T(4,128)S(1)} %get-tuple-element.21), channel_id=1, source_target_pairs={{0,1},{1,2},{2,3},{3,4},{4,5},{5,6},{6,7},{7,8},{8,9},{9,10},{10,1... | collective-permute-start | bytes 983048 | tf_op jit(solution)/shard_map/ppermute | solution.py:61
  42.5 2.9 %collective-permute-done.from_next.refs_1_ = f32[16,4,1280]{2,1,0:T(4,128)S(1)} collective-permute-done((f32[16,4,1280]{2,1,0:T(4,128)S(1)}, f32[16,4,1280]{2,1,0:T(4,128)S(1)}, u32[]{:S(2)}, u32[]{:S(2)}) %collective-permute-start) | collective-permute-done | bytes 327712 | tf_op jit(solution)/shard_map/ppermute | solution.py:60
  45.4 1.9 %collective-permute-done.1.from_last.refs_2_ = f32[16,4,1280]{2,1,0:T(4,128)S(1)} collective-permute-done((f32[16,4,1280]{2,1,0:T(4,128)S(1)}, f32[16,4,1280]{2,1,0:T(4,128)S(1)}, u32[]{:S(2)}, u32[]{:S(2)}) %collective-permute-start.1) | collective-permute-done | bytes 327712 | tf_op jit(solution)/shard_map/ppermute | solution.py:61
  47.4 1.9 %collective-permute-start.2 = (f32[4,16,1280]{2,1,0:T(8,128)S(1)}, f32[4,16,1280]{2,1,0:T(8,128)S(1)}, u32[]{:S(2)}, u32[]{:S(2)}) collective-permute-start(f32[4,16,1280]{2,1,0:T(8,128)S(1)} %get-tuple-element.22), channel_id=1, source_target_pairs={{32,0},{64,32},{96,64},{128,96},{160,128},{192,160},{224,192},{33,... | collective-permute-start | bytes 983048 | tf_op jit(solution)/shard_map/ppermute | solution.py:63
  49.3 2.4 %collective-permute-start.3 = (f32[4,16,1280]{2,1,0:T(8,128)S(1)}, f32[4,16,1280]{2,1,0:T(8,128)S(1)}, u32[]{:S(2)}, u32[]{:S(2)}) collective-permute-start(f32[4,16,1280]{2,1,0:T(8,128)S(1)} %get-tuple-element.23), channel_id=1, source_target_pairs={{0,32},{32,64},{64,96},{96,128},{128,160},{160,192},{192,224},{1,3... | collective-permute-start | bytes 983048 | tf_op jit(solution)/shard_map/ppermute | solution.py:64
  51.9 1.9 %collective-permute-done.2.refs_3_ = f32[4,16,1280]{2,1,0:T(8,128)S(1)} collective-permute-done((f32[4,16,1280]{2,1,0:T(8,128)S(1)}, f32[4,16,1280]{2,1,0:T(8,128)S(1)}, u32[]{:S(2)}, u32[]{:S(2)}) %collective-permute-start.2) | collective-permute-done | bytes 327712 | tf_op jit(solution)/shard_map/ppermute | solution.py:63
  53.9 3.8 %collective-permute-done.3.refs_4_ = f32[4,16,1280]{2,1,0:T(8,128)S(1)} collective-permute-done((f32[4,16,1280]{2,1,0:T(8,128)S(1)}, f32[4,16,1280]{2,1,0:T(8,128)S(1)}, u32[]{:S(2)}, u32[]{:S(2)}) %collective-permute-start.3) | collective-permute-done | bytes 327712 | tf_op jit(solution)/shard_map/ppermute | solution.py:64
  57.8 0.5 broadcast_in_dim.8.refs_5_
  58.3 7.9 %cycle_first.1 = (f32[16,8,1280]{2,1,0:T(8,128)S(1)}, f32[16,4,1280]{2,1,0:T(4,128)S(1)}, f32[16,4,1280]{2,1,0:T(4,128)S(1)}, f32[24,16,128]{2,1,0:T(8,128)S(1)}...) custom-call(f32[16,8,1280]{2,1,0:T(8,128)S(1)} %get-tuple-element.19, ...), custom_call_target="tpu_custom_call" | custom-call | tf_op jit(solution)/shard_map/cycle_first/pallas_call | solution.py:321
  66.2 1.9 %collective-permute-start.4 = (f32[16,4,1280]{2,1,0:T(4,128)S(1)}, f32[16,4,1280]{2,1,0:T(4,128)S(1)}, u32[]{:S(2)}, u32[]{:S(2)}) collective-permute-start(f32[16,4,1280]{2,1,0:T(4,128)S(1)} %get-tuple-element.25), channel_id=1, source_target_pairs={{1,0},{2,1},{3,2},{4,3},{5,4},{6,5},{7,6},{8,7},{9,8},{10,9},{11,1... | collective-permute-start | bytes 983048 | tf_op jit(solution)/shard_map/ppermute | solution.py:60
  68.1 3.9 %collective-permute-start.5 = (f32[16,4,1280]{2,1,0:T(4,128)S(1)}, f32[16,4,1280]{2,1,0:T(4,128)S(1)}, u32[]{:S(2)}, u32[]{:S(2)}) collective-permute-start(f32[16,4,1280]{2,1,0:T(4,128)S(1)} %get-tuple-element.26), channel_id=1, source_target_pairs={{0,1},{1,2},{2,3},{3,4},{4,5},{5,6},{6,7},{7,8},{8,9},{9,10},{10,1... | collective-permute-start | bytes 983048 | tf_op jit(solution)/shard_map/ppermute | solution.py:61
  72.0 5.1 %collective-permute-done.4.from_next.refs_1_ = f32[16,4,1280]{2,1,0:T(4,128)S(1)} collective-permute-done((f32[16,4,1280]{2,1,0:T(4,128)S(1)}, f32[16,4,1280]{2,1,0:T(4,128)S(1)}, u32[]{:S(2)}, u32[]{:S(2)}) %collective-permute-start.4) | collective-permute-done | bytes 327712 | tf_op jit(solution)/shard_map/ppermute | solution.py:60
  77.1 1.6 %collective-permute-done.5.from_last.refs_2_ = f32[16,4,1280]{2,1,0:T(4,128)S(1)} collective-permute-done((f32[16,4,1280]{2,1,0:T(4,128)S(1)}, f32[16,4,1280]{2,1,0:T(4,128)S(1)}, u32[]{:S(2)}, u32[]{:S(2)}) %collective-permute-start.5) | collective-permute-done | bytes 327712 | tf_op jit(solution)/shard_map/ppermute | solution.py:61
  78.8 1.9 %collective-permute-start.6 = (f32[4,16,1280]{2,1,0:T(8,128)S(1)}, f32[4,16,1280]{2,1,0:T(8,128)S(1)}, u32[]{:S(2)}, u32[]{:S(2)}) collective-permute-start(f32[4,16,1280]{2,1,0:T(8,128)S(1)} %get-tuple-element.27), channel_id=1, source_target_pairs={{32,0},{64,32},{96,64},{128,96},{160,128},{192,160},{224,192},{33,... | collective-permute-start | bytes 983048 | tf_op jit(solution)/shard_map/ppermute | solution.py:63
  80.8 2.4 %collective-permute-start.7 = (f32[4,16,1280]{2,1,0:T(8,128)S(1)}, f32[4,16,1280]{2,1,0:T(8,128)S(1)}, u32[]{:S(2)}, u32[]{:S(2)}) collective-permute-start(f32[4,16,1280]{2,1,0:T(8,128)S(1)} %get-tuple-element.28), channel_id=1, source_target_pairs={{0,32},{32,64},{64,96},{96,128},{128,160},{160,192},{192,224},{1,3... | collective-permute-start | bytes 983048 | tf_op jit(solution)/shard_map/ppermute | solution.py:64
  83.2 2.2 %collective-permute-done.6.refs_3_ = f32[4,16,1280]{2,1,0:T(8,128)S(1)} collective-permute-done((f32[4,16,1280]{2,1,0:T(8,128)S(1)}, f32[4,16,1280]{2,1,0:T(8,128)S(1)}, u32[]{:S(2)}, u32[]{:S(2)}) %collective-permute-start.6) | collective-permute-done | bytes 327712 | tf_op jit(solution)/shard_map/ppermute | solution.py:63
  85.3 3.8 %collective-permute-done.7.refs_4_ = f32[4,16,1280]{2,1,0:T(8,128)S(1)} collective-permute-done((f32[4,16,1280]{2,1,0:T(8,128)S(1)}, f32[4,16,1280]{2,1,0:T(8,128)S(1)}, u32[]{:S(2)}, u32[]{:S(2)}) %collective-permute-start.7) | collective-permute-done | bytes 327712 | tf_op jit(solution)/shard_map/ppermute | solution.py:64
  89.1 7.6 %cycle_last.1 = (f32[288,4,128]{2,1,0:T(4,128)}, f32[24,16,128]{2,1,0:T(8,128)S(1)}) custom-call(f32[16,8,1280]{2,1,0:T(8,128)S(1)} %get-tuple-element.24.own.refs_0_, f32[16,4,1280]{2,1,0:T(4,128)S(1)} %collective-permute-done.4.from_next.refs_1_, f32[16,4,1280]{2,1,0:T(4,128)S(1)} %collective-permute-done.5.from_last.refs_2_, ...), custom_call_target="tpu_custom_call" | custom-call | tf_op jit(solution)/shard_map/cycle_last/pallas_call | solution.py:321
  96.8 11.0 %all-to-all-start.1 = ((f32[288,4,128]{2,1,0:T(4,128)}), f32[288,4,128]{2,1,0:T(4,128)S(1)}, u32[]{:S(2)}, u32[]{:S(2)}) async-start(f32[288,4,128]{2,1,0:T(4,128)} %get-tuple-element.33), calls=%async_computation.1 | async-start | bytes 1179648 | tf_op jit(solution)/shard_map/all_to_all | solution.py:440
  107.8 0.5 ocean.1
  108.4 0.7 copy.23
  109.1 16.7 %all-to-all-done.1 = f32[288,4,128]{2,1,0:T(4,128)S(1)} async-done(((f32[288,4,128]{2,1,0:T(4,128)}), f32[288,4,128]{2,1,0:T(4,128)S(1)}, u32[]{:S(2)}, u32[]{:S(2)}) %all-to-all-start.1) | async-done | bytes 589856 | tf_op jit(solution)/shard_map/all_to_all | solution.py:440
  125.7 2.5 %collect.1 = f32[576,256]{1,0:T(8,128)} custom-call(f32[32,9,4,128]{3,2,1,0:T(4,128)S(1)} %bitcast.20), custom_call_target="tpu_custom_call" | custom-call | tf_op jit(solution)/shard_map/collect/pallas_call | solution.py:321
  (47 shorter events, 2.3 us)
Async XLA Ops:
  0.6 17.0 %copy-start.7 = (s32[32]{0:T(128)S(1)}, s32[32]{0:T(128)}, u32[]{:S(2)}) copy-start(s32[32]{0:T(128)} %param.15) | copy-start | bytes 388
  0.6 1.1 copy-start.2
  1.7 15.5 %copy-start.4 = (s32[128,256]{1,0:T(8,128)S(1)}, s32[128,256]{1,0:T(8,128)}, u32[]{:S(2)}) copy-start(s32[128,256]{1,0:T(8,128)} %param.14) | copy-start | bytes 393220
  1.7 16.2 %copy-start.6 = (s32[32,4]{0,1:T(4,128)S(1)}, s32[32,4]{0,1:T(4,128)}, u32[]{:S(2)}) copy-start(s32[32,4]{0,1:T(4,128)} %param.16) | copy-start | bytes 1540
  1.7 16.5 %copy-start.3 = (s32[8,128,256]{2,1,0:T(8,128)S(1)}, s32[8,128,256]{2,1,0:T(8,128)}, u32[]{:S(2)}) copy-start(s32[8,128,256]{2,1,0:T(8,128)} %param.13) | copy-start | bytes 3145732
  5.6 12.8 %copy-start.5 = (f32[2,24,16,8]{1,3,2,0:T(8,128)S(1)}, f32[2,24,16,8]{1,3,2,0:T(8,128)}, u32[]{:S(2)}) copy-start(f32[2,24,16,8]{1,3,2,0:T(8,128)} %param.10) | copy-start | bytes 73732
  5.6 30.5 %all-to-all-start = ((f32[288,4,128]{2,1,0:T(4,128)}), f32[288,4,128]{2,1,0:T(4,128)S(1)}, u32[]{:S(2)}, u32[]{:S(2)}) async-start(f32[288,4,128]{2,1,0:T(4,128)} %bitcast.1), calls=%async_computation | async-start | bytes 1179648 | tf_op jit(solution)/shard_map/all_to_all | solution.py:396
  36.4 9.0 %collective-permute-start = (f32[16,4,1280]{2,1,0:T(4,128)S(1)}, f32[16,4,1280]{2,1,0:T(4,128)S(1)}, u32[]{:S(2)}, u32[]{:S(2)}) collective-permute-start(f32[16,4,1280]{2,1,0:T(4,128)S(1)} %get-tuple-element.20), channel_id=1, source_target_pairs={{1,0},{2,1},{3,2},{4,3},{5,4},{6,5},{7,6},{8,7},{9,8},{10,9},{11,1... | collective-permute-start | bytes 983048 | tf_op jit(solution)/shard_map/ppermute | solution.py:60
  38.3 9.0 %collective-permute-start.1 = (f32[16,4,1280]{2,1,0:T(4,128)S(1)}, f32[16,4,1280]{2,1,0:T(4,128)S(1)}, u32[]{:S(2)}, u32[]{:S(2)}) collective-permute-start(f32[16,4,1280]{2,1,0:T(4,128)S(1)} %get-tuple-element.21), channel_id=1, source_target_pairs={{0,1},{1,2},{2,3},{3,4},{4,5},{5,6},{6,7},{7,8},{8,9},{9,10},{10,1... | collective-permute-start | bytes 983048 | tf_op jit(solution)/shard_map/ppermute | solution.py:61
  42.3 15.9 %copy-start.1 = (bf16[1152,1152]{1,0:T(8,128)(2,1)S(1)}, bf16[1152,1152]{1,0:T(8,128)(2,1)}, u32[]{:S(2)}) copy-start(bf16[1152,1152]{1,0:T(8,128)(2,1)} %refs_8_.3) | copy-start | bytes 7962628
  47.4 6.5 %collective-permute-start.2 = (f32[4,16,1280]{2,1,0:T(8,128)S(1)}, f32[4,16,1280]{2,1,0:T(8,128)S(1)}, u32[]{:S(2)}, u32[]{:S(2)}) collective-permute-start(f32[4,16,1280]{2,1,0:T(8,128)S(1)} %get-tuple-element.22), channel_id=1, source_target_pairs={{32,0},{64,32},{96,64},{128,96},{160,128},{192,160},{224,192},{33,... | collective-permute-start | bytes 983048 | tf_op jit(solution)/shard_map/ppermute | solution.py:63
  49.3 8.4 %collective-permute-start.3 = (f32[4,16,1280]{2,1,0:T(8,128)S(1)}, f32[4,16,1280]{2,1,0:T(8,128)S(1)}, u32[]{:S(2)}, u32[]{:S(2)}) collective-permute-start(f32[4,16,1280]{2,1,0:T(8,128)S(1)} %get-tuple-element.23), channel_id=1, source_target_pairs={{0,32},{32,64},{64,96},{96,128},{128,160},{160,192},{192,224},{1,3... | collective-permute-start | bytes 983048 | tf_op jit(solution)/shard_map/ppermute | solution.py:64
  51.8 6.5 %copy-start = (bf16[1152,1152]{1,0:T(8,128)(2,1)S(1)}, bf16[1152,1152]{1,0:T(8,128)(2,1)}, u32[]{:S(2)}) copy-start(bf16[1152,1152]{1,0:T(8,128)(2,1)} %refs_7_.3) | copy-start | bytes 7962628
  66.2 10.9 %collective-permute-start.4 = (f32[16,4,1280]{2,1,0:T(4,128)S(1)}, f32[16,4,1280]{2,1,0:T(4,128)S(1)}, u32[]{:S(2)}, u32[]{:S(2)}) collective-permute-start(f32[16,4,1280]{2,1,0:T(4,128)S(1)} %get-tuple-element.25), channel_id=1, source_target_pairs={{1,0},{2,1},{3,2},{4,3},{5,4},{6,5},{7,6},{8,7},{9,8},{10,9},{11,1... | collective-permute-start | bytes 983048 | tf_op jit(solution)/shard_map/ppermute | solution.py:60
  68.1 10.6 %collective-permute-start.5 = (f32[16,4,1280]{2,1,0:T(4,128)S(1)}, f32[16,4,1280]{2,1,0:T(4,128)S(1)}, u32[]{:S(2)}, u32[]{:S(2)}) collective-permute-start(f32[16,4,1280]{2,1,0:T(4,128)S(1)} %get-tuple-element.26), channel_id=1, source_target_pairs={{0,1},{1,2},{2,3},{3,4},{4,5},{5,6},{6,7},{7,8},{8,9},{9,10},{10,1... | collective-permute-start | bytes 983048 | tf_op jit(solution)/shard_map/ppermute | solution.py:61
  78.8 6.5 %collective-permute-start.6 = (f32[4,16,1280]{2,1,0:T(8,128)S(1)}, f32[4,16,1280]{2,1,0:T(8,128)S(1)}, u32[]{:S(2)}, u32[]{:S(2)}) collective-permute-start(f32[4,16,1280]{2,1,0:T(8,128)S(1)} %get-tuple-element.27), channel_id=1, source_target_pairs={{32,0},{64,32},{96,64},{128,96},{160,128},{192,160},{224,192},{33,... | collective-permute-start | bytes 983048 | tf_op jit(solution)/shard_map/ppermute | solution.py:63
  80.8 8.4 %collective-permute-start.7 = (f32[4,16,1280]{2,1,0:T(8,128)S(1)}, f32[4,16,1280]{2,1,0:T(8,128)S(1)}, u32[]{:S(2)}, u32[]{:S(2)}) collective-permute-start(f32[4,16,1280]{2,1,0:T(8,128)S(1)} %get-tuple-element.28), channel_id=1, source_target_pairs={{0,32},{32,64},{64,96},{96,128},{128,160},{160,192},{192,224},{1,3... | collective-permute-start | bytes 983048 | tf_op jit(solution)/shard_map/ppermute | solution.py:64
  96.8 28.9 %all-to-all-start.1 = ((f32[288,4,128]{2,1,0:T(4,128)}), f32[288,4,128]{2,1,0:T(4,128)S(1)}, u32[]{:S(2)}, u32[]{:S(2)}) async-start(f32[288,4,128]{2,1,0:T(4,128)} %get-tuple-element.33), calls=%async_computation.1 | async-start | bytes 1179648 | tf_op jit(solution)/shard_map/all_to_all | solution.py:440

commit v5 on v4

--- a/solution.py
+++ b/solution.py
@@ -20,10 +20,11 @@
 EXT_C = 16
 LANES = 128
 GROUPS = 9
-WIDE = COMP + LANES
 QUADS = COMP // 4
-
-precise = lax.Precision.HIGHEST
+KEPT = 10
+MAIN = 8
+CELLS = EXT_R * EXT_C
+
 ocean_dt = 0.2
 viscous = 0.5
 mixing = 0.5
@@ -65,14 +66,39 @@
     return [own, from_next, from_last, from_up, from_down]
 
 
-def fill(ext_ref, pieces, lanes):
+def block(row, group, cols):
+    start = (row * KEPT + group) * cols
+    return slice(start, start + cols)
+
+
+def fill(ext_ref, pieces, group):
     own, from_next, from_last, from_up, from_down = pieces
-    middle = slice(HALO, HALO + ROWS)
-    ext_ref[middle, 0:COLS, :] = own[:, :, lanes]
-    ext_ref[middle, COLS : COLS + HALO, :] = from_next[:, :, lanes]
-    ext_ref[middle, COLS + HALO : EXT_C, :] = from_last[:, :, lanes]
-    ext_ref[HALO + ROWS : EXT_R] = from_up[:, :, lanes]
-    ext_ref[0:HALO] = from_down[:, :, lanes]
+    for r in range(ROWS):
+        ext_ref[HALO + r, 0:HALO, :] = from_last[block(r, group, HALO), :]
+        ext_ref[HALO + r, HALO : HALO + COLS, :] = own[block(r, group, COLS), :]
+        ext_ref[HALO + r, HALO + COLS : EXT_C, :] = from_next[block(r, group, HALO), :]
+    for r in range(HALO):
+        ext_ref[HALO + ROWS + r] = from_up[block(r, group, EXT_C), :]
+        ext_ref[r] = from_down[block(r, group, EXT_C), :]
+
+
+def fill_cells(cell_ref, pieces):
+    own, from_next, from_last, from_up, from_down = pieces
+
+    def take(ref, row, col, cols, ext_row, ext_col):
+        start = (ext_row * EXT_C + ext_col) * MAIN
+        cell_ref[start : start + MAIN, :] = ref[pl.ds(row * KEPT * cols + col, MAIN, stride=cols), :]
+
+    for r in range(ROWS):
+        for c in range(COLS):
+            take(own, r, c, COLS, HALO + r, HALO + c)
+        for c in range(HALO):
+            take(from_next, r, c, HALO, HALO + r, HALO + COLS + c)
+            take(from_last, r, c, HALO, HALO + r, c)
+    for r in range(HALO):
+        for c in range(EXT_C):
+            take(from_up, r, c, EXT_C, HALO + ROWS + r, c)
+            take(from_down, r, c, EXT_C, r, c)
 
 
 def swap_blocks(tiles):
@@ -106,53 +132,60 @@
 
 
 def spread_kernel(x_hbm, o_hbm, half_ref, chunk_ref, in_sems, out_sems):
-    copies = [rows_copy(x_hbm, half_ref, in_sems, group, False) for group in direction_groups()]
+    groups = list(direction_groups())
+    copies = [rows_copy(x_hbm, half_ref, in_sems, group, False) for group in groups]
     for copy in copies:
         copy.start()
     sent = []
-    for index, count, half, slot in direction_groups():
-        copies[slot].wait()
-        tiles = [half_ref[slot, pl.ds(r, count, stride=ROWS), :] for r in range(ROWS)]
-        for i, tile in enumerate(swap_blocks(tiles)):
-            for j in range(count // 4):
-                chunk_ref[half * ROWS + i, 2 * index + j] = tile[4 * j : 4 * j + 4]
-        if half:
-            part = pl.ds(2 * index, count // 4)
-            sent.append(
-                pltpu.make_async_copy(chunk_ref.at[:, part], o_hbm.at[:, part], out_sems.at[index])
-            )
-            sent[-1].start()
+    for batch, quads in ((groups[:6], pl.ds(0, 6)), (groups[6:], pl.ds(6, 3))):
+        for group in batch:
+            copies[group[3]].wait()
+        for index, count, half, slot in batch:
+            tiles = [half_ref[slot, pl.ds(r, count, stride=ROWS), :] for r in range(ROWS)]
+            for i, tile in enumerate(swap_blocks(tiles)):
+                for j in range(count // 4):
+                    chunk_ref[half * ROWS + i, 2 * index + j] = tile[4 * j : 4 * j + 4]
+        far = o_hbm.at[:, quads]
+        sent.append(pltpu.make_async_copy(chunk_ref.at[:, quads], far, out_sems.at[len(sent)]))
+        sent[-1].start()
     for copy in sent:
         copy.wait()
 
 
 def collect_kernel(x_ref, o_hbm, half_ref, sems):
+    groups = list(direction_groups())
     copies = []
-    for group in direction_groups():
-        index, count, half, slot = group
-        tiles = []
-        for i in range(ROWS):
-            quads = [x_ref[half * ROWS + i, 2 * index + j] for j in range(count // 4)]
-            tiles.append(jnp.concatenate(quads, axis=0))
-        for r, tile in enumerate(swap_blocks(tiles)):
-            half_ref[slot, pl.ds(r, count, stride=ROWS), :] = tile
-        copies.append(rows_copy(o_hbm, half_ref, sems, group, True))
-        copies[-1].start()
+    for batch in (groups[:6], groups[6:]):
+        for index, count, half, slot in batch:
+            tiles = []
+            for i in range(ROWS):
+                quads = [x_ref[half * ROWS + i, 2 * index + j] for j in range(count // 4)]
+                tiles.append(jnp.concatenate(quads, axis=0))
+            for r, tile in enumerate(swap_blocks(tiles)):
+                half_ref[slot, pl.ds(r, count, stride=ROWS), :] = tile
+        for group in batch:
+            copies.append(rows_copy(o_hbm, half_ref, sems, group, True))
+            copies[-1].start()
     for copy in copies:
         copy.wait()
 
 
 def ends_kernel(own, from_next, from_last, first_ref, last_ref):
-    for ref, rows in ((first_ref, slice(0, HALO)), (last_ref, slice(ROWS - HALO, ROWS))):
-        ref[:, 0:COLS, :] = own[rows]
-        ref[:, COLS : COLS + HALO, :] = from_next[rows]
-        ref[:, COLS + HALO : EXT_C, :] = from_last[rows]
-
-
-def put(value, refs, lanes):
-    refs[0][:, :, lanes] = value
-    refs[1][:, :, lanes] = value[:, :HALO, :]
-    refs[2][:, :, lanes] = value[:, HALO:, :]
+    for ref, start in ((first_ref, 0), (last_ref, ROWS - HALO)):
+        for r in range(HALO):
+            for k in range(KEPT):
+                at = block(r, k, EXT_C).start
+                ref[at : at + HALO, :] = from_last[block(start + r, k, HALO), :]
+                ref[at + HALO : at + HALO + COLS, :] = own[block(start + r, k, COLS), :]
+                ref[at + HALO + COLS : at + EXT_C, :] = from_next[block(start + r, k, HALO), :]
+
+
+def put(value, refs, group):
+    for r in range(ROWS):
+        row = value[r * COLS : (r + 1) * COLS, :]
+        refs[0][block(r, group, COLS), :] = row
+        refs[1][block(r, group, HALO), :] = row[:HALO]
+        refs[2][block(r, group, HALO), :] = row[HALO:]
 
 
 def unpack_kernel(x_ref, u_ref, *rest):
@@ -160,9 +193,8 @@
     for q in range(QUADS):
         flat_ref[4 * q : 4 * q + 4, :] = x_ref[q]
     for k in range(GROUPS):
-        lanes = slice(k * LANES, (k + 1) * LANES)
-        put(jnp.transpose(flat_ref[lanes, :]).reshape(ROWS, COLS, LANES), out_refs, lanes)
-    put(u_ref[...], out_refs, slice(COMP, WIDE))
+        put(jnp.transpose(flat_ref[k * LANES : (k + 1) * LANES, :]), out_refs, k)
+    put(u_ref[...], out_refs, GROUPS)
 
 
 def face_flux(lower, upper, half_courant, half_square, second):
@@ -170,7 +202,7 @@
     return lower * (half_courant + q) + upper * (half_courant - q)
 
 
-def courants(ext_ref, lane_ref, pick_ref, face_refs):
+def courants(ext_ref, lane_ref, pick_ref, main_ref, rest_ref):
     lane = lax.broadcasted_iota(jnp.int32, (EXT_C, LANES), 1)
     quarter = (0.25 * 0.15) * jnp.tanh(ext_ref[...])
     faces = []
@@ -185,10 +217,90 @@
     parts = jnp.concatenate([high + pltpu.roll(middle, LANES // 2, 1), rest - middle], axis=1)
     parts = parts.astype(jnp.bfloat16)
     for index in range(2):
-        picked = jnp.dot(parts, pick_ref[index], preferred_element_type=f32)
-        half_courant = (lane_ref[index] + picked).reshape(EXT_R, EXT_C, COMP)
-        face_refs[2 * index][...] = half_courant
-        face_refs[2 * index + 1][...] = (half_courant + half_courant) * half_courant
+        for k in range(GROUPS):
+            lanes = slice(k * LANES, (k + 1) * LANES)
+            picked = jnp.dot(parts, pick_ref[index, :, lanes], preferred_element_type=f32)
+            half_courant = lane_ref[index, :, lanes] + picked
+            square = (half_courant + half_courant) * half_courant
+            for which, value in ((2 * index, half_courant), (2 * index + 1, square)):
+                if k == MAIN:
+                    rest_ref[which] = value.reshape(EXT_R, EXT_C, LANES)
+                    continue
+                for start in range(0, CELLS, 8):
+                    at = (which * CELLS + start) * MAIN + k
+                    main_ref[pl.ds(at, 8, stride=MAIN), :] = value[start : start + 8, :]
+
+
+def advect_cells(cell_ref, face_ref, flag_ref, sea_ref, energy_ref, flag_base):
+    def at(start):
+        return pl.ds(start * MAIN, MAIN)
+
+    def cell(r, c):
+        return cell_ref[at(r * EXT_C + c), :]
+
+    def flux(lower, upper, which, r, c, flag_row):
+        half_courant = face_ref[at(which * CELLS + r * EXT_C + c), :]
+        half_square = face_ref[at((which + 1) * CELLS + r * EXT_C + c), :]
+        second = flag_ref[pl.ds(flag_row * EXT_C + c, MAIN, stride=0), :] != 0.0
+        return face_flux(lower, upper, half_courant, half_square, second)
+
+    for s in range(SUB):
+        cols = range(s, EXT_C - s)
+        flag_top = (flag_base + s) * EXT_R
+
+        def upper_flux(r, c):
+            return flux(cell(r, c), cell(r + 1, c), 2, r, c, flag_top + r + 1)
+
+        def row(r, below):
+            above = [upper_flux(r, c) for c in cols]
+            shifted = [cell(r, c) - (a - b) for c, a, b in zip(cols, above, below)]
+            along = [
+                flux(shifted[i - 1], shifted[i], 0, r, cols[i], flag_top + r)
+                for i in range(1, len(cols))
+            ]
+            for i in range(1, len(cols) - 1):
+                sea = sea_ref[pl.ds(r * EXT_C + cols[i], MAIN, stride=0), :]
+                result = (shifted[i] - (along[i] - along[i - 1])) * sea
+                if s == SUB - 1:
+                    start = (r - HALO) * GROUPS * COLS + cols[i] - HALO
+                    energy_ref[pl.ds(start, MAIN, stride=COLS), :] = result
+                else:
+                    cell_ref[at(r * EXT_C + cols[i]), :] = result
+            return above
+
+        below = [upper_flux(s, c) for c in cols]
+        for r in range(s + 1, EXT_R - 1 - s):
+            below = row(r, below)
+
+
+def advect_rest(tile_ref, face_ref, flag_ref, sea_ref, energy_ref, flag_base):
+    def rows_of(ref, r):
+        return ref[r * EXT_C : (r + 1) * EXT_C, :]
+
+    for s in range(SUB):
+        flag_top = (flag_base + s) * EXT_R
+        here = tile_ref[s]
+        above = tile_ref[s + 1]
+        flag = rows_of(flag_ref, flag_top + s + 1) != 0.0
+        flux_below = face_flux(here, above, face_ref[2, s], face_ref[3, s], flag)
+        for r in range(s + 1, EXT_R - 1 - s):
+            here = above
+            above = tile_ref[r + 1]
+            flag_above = rows_of(flag_ref, flag_top + r + 1) != 0.0
+            flux_above = face_flux(here, above, face_ref[2, r], face_ref[3, r], flag_above)
+            shifted = here - (flux_above - flux_below)
+            flux_east = face_flux(
+                pltpu.roll(shifted, 1, 0), shifted, face_ref[0, r], face_ref[1, r], flag
+            )
+            result = shifted - (pltpu.roll(flux_east, EXT_C - 1, 0) - flux_east)
+            result = result * rows_of(sea_ref, r)
+            if s == SUB - 1:
+                start = ((r - HALO) * GROUPS + MAIN) * COLS
+                energy_ref[start : start + COLS, :] = result[HALO : HALO + COLS]
+            else:
+                tile_ref[r] = result
+            flux_below = flux_above
+            flag = flag_above
 
 
 def cycle_kernel(first, *refs):
@@ -201,72 +313,42 @@
         lane_ref, pick_ref, weight_hi, weight_lo = take(4)
         out_refs = take(3)
         (ext_ref,) = take(1)
-        face_refs = take(4)
+        main_ref, rest_ref = take(2)
     else:
-        face_refs = take(4)
+        main_ref, rest_ref = take(2)
         out_hbm, ext_ref = take(2)
-    tile_ref, energy_ref = take(2)
+    cell_ref, tile_ref, energy_ref = take(3)
     if not first:
         chunk_ref, sems = take(2)
-    fill(ext_ref, pieces, slice(COMP, WIDE))
+    fill(ext_ref, pieces, GROUPS)
     if first:
-        courants(ext_ref, lane_ref, pick_ref, face_refs)
-    east, east_square, north, north_square = face_refs
+        courants(ext_ref, lane_ref, pick_ref, main_ref, rest_ref)
+    fill_cells(cell_ref, pieces)
+    fill(tile_ref, pieces, MAIN)
+    advect_rest(tile_ref, rest_ref, flag_ref, sea_ref, energy_ref, flag_base)
+    advect_cells(cell_ref, main_ref, flag_ref, sea_ref, energy_ref, flag_base)
+
+    def energy_group(k):
+        starts = [(r * GROUPS + k) * COLS for r in range(ROWS)]
+        return jnp.concatenate([energy_ref[a : a + COLS, :] for a in starts], axis=0)
+
     copies = []
-
-    def advect(k, carry):
-        lanes = pl.ds(pl.multiple_of(k * LANES, LANES), LANES)
-        fill(tile_ref, pieces, lanes)
-        for s in range(SUB):
-            here = tile_ref[s]
-            above = tile_ref[s + 1]
-            flag = flag_ref[flag_base + s, s + 1] != 0.0
-            flux_below = face_flux(here, above, north[s, :, lanes], north_square[s, :, lanes], flag)
-            for r in range(s + 1, EXT_R - 1 - s):
-                here = above
-                above = tile_ref[r + 1]
-                flag_above = flag_ref[flag_base + s, r + 1] != 0.0
-                flux_above = face_flux(
-                    here, above, north[r, :, lanes], north_square[r, :, lanes], flag_above
-                )
-                shifted = here - (flux_above - flux_below)
-                flux_east = face_flux(
-                    pltpu.roll(shifted, 1, 0),
-                    shifted,
-                    east[r, :, lanes],
-                    east_square[r, :, lanes],
-                    flag,
-                )
-                result = shifted - (pltpu.roll(flux_east, EXT_C - 1, 0) - flux_east)
-                result = result * sea_ref[r]
-                if s == SUB - 1:
-                    energy_ref[r - HALO, :, lanes] = result[0:COLS]
-                else:
-                    tile_ref[r] = result
-                flux_below = flux_above
-                flag = flag_above
-        return carry
-
-    lax.fori_loop(0, GROUPS, advect, 0)
-    cells = ROWS * COLS
-    energy = energy_ref[...].reshape(cells, COMP)
+    energy = jnp.concatenate([energy_group(k) for k in range(GROUPS)], axis=1)
     rounded = energy.astype(jnp.bfloat16)
     squared = (energy * energy).astype(jnp.bfloat16)
     if first:
         rest = (energy - rounded.astype(f32)).astype(jnp.bfloat16)
         mm = lambda a, b: jnp.dot(a, b, preferred_element_type=f32)
         stokes = mm(rounded, weight_hi[...]) + (mm(rest, weight_hi[...]) + mm(rounded, weight_lo[...]))
-        stokes = stokes.reshape(ROWS, COLS, LANES)
-        put(stokes, out_refs, pl.ds(COMP, LANES))
+        put(stokes, out_refs, GROUPS)
     nt = (((1,), (1,)), ((), ()))
     for k in range(GROUPS):
         lanes = pl.ds(k * LANES, LANES)
         gain = lax.dot_general(rounded, gain_ref[lanes, :], nt, preferred_element_type=f32)
         quartic = lax.dot_general(squared, quad_ref[lanes, :], nt, preferred_element_type=f32)
-        before = energy_ref[:, :, lanes].reshape(cells, LANES)
-        updated = before * (1.0 + 0.5 * jnp.tanh(gain) - 0.25 * jnp.tanh(quartic))
+        updated = energy_group(k) * (1.0 + 0.5 * jnp.tanh(gain) - 0.25 * jnp.tanh(quartic))
         if first:
-            put(updated.reshape(ROWS, COLS, LANES), out_refs, lanes)
+            put(updated, out_refs, k)
         else:
             flat = jnp.transpose(updated)
             for q in range(32):
@@ -301,9 +383,9 @@
             tendency = (
                 viscous * laplace + turning + mixing * (over + under - 2.0 * here) - friction * here
             )
-            result = jnp.where(used, (here + ocean_dt * tendency) * sea_ref[r], 0.0)
+            result = jnp.where(used, (here + ocean_dt * tendency) * sea_ref[r * EXT_C : (r + 1) * EXT_C, :], 0.0)
             if s == OSTEPS - 1:
-                o_ref[r - HALO] = result[0:COLS]
+                o_ref[r - HALO] = result[HALO : HALO + COLS]
             else:
                 now_ref[r] = result
             below, here = here, above
@@ -336,7 +418,7 @@
 
 def spread(x):
     x = x.reshape(DIR * ROWS, 2 * LANES)
-    scratch = [halves, chunks_dims, sems((10,)), sems((5,))]
+    scratch = [halves, chunks_dims, sems((10,)), sems((2,))]
     out = call(spread_kernel, "spread", [x], shape_of(*chunks_dims), scratch, 4, [hbm], hbm)
     return out.reshape(QUADS, 4, LANES)
 
@@ -349,9 +431,8 @@
     return out.reshape(1, DIR, ROWS, 2 * LANES)
 
 
-tile_shapes = [shape_of(ROWS, COLS, WIDE)] + [shape_of(ROWS, HALO, WIDE)] * 2
+tile_shapes = [shape_of(ROWS * KEPT * COLS, LANES)] + [shape_of(ROWS * KEPT * HALO, LANES)] * 2
 ext_shape = shape_of(EXT_R, EXT_C, LANES)
-face_shape = shape_of(EXT_R, EXT_C, COMP)
 
 
 def unpack(x, velocity):
@@ -359,21 +440,22 @@
 
 
 def ends(*pieces):
-    return call(ends_kernel, "ends", pieces, [shape_of(HALO, EXT_C, WIDE)] * 2, [], 4)
+    return call(ends_kernel, "ends", pieces, [shape_of(HALO * KEPT * EXT_C, LANES)] * 2, [], 4)
 
 
 def run_cycle(first, operands):
-    scratch = [(EXT_R, EXT_C, LANES), (ROWS, COLS, COMP)]
+    scratch = [(CELLS * MAIN, LANES), (EXT_R, EXT_C, LANES), (ROWS * GROUPS * COLS, LANES)]
     if first:
-        out_shape = tile_shapes + [ext_shape] + [face_shape] * 4
-        out_specs = [vmem] * 8
+        faces = [shape_of(4 * CELLS * MAIN, LANES), shape_of(4, EXT_R, EXT_C, LANES)]
+        out_shape = tile_shapes + [ext_shape] + faces
+        out_specs = [vmem] * 6
     else:
         out_shape = [shape_of(QUADS, 4, LANES), ext_shape]
         out_specs = [hbm, vmem]
         scratch += [(QUADS, 4, LANES), sems((GROUPS,))]
     kernel = lambda *refs: cycle_kernel(first, *refs)
     name = "cycle_first" if first else "cycle_last"
-    return call(kernel, name, operands, out_shape, scratch, 24, None, out_specs)
+    return call(kernel, name, operands, out_shape, scratch, 20, None, out_specs)
 
 
 def ocean(velocity, stokes, sea):
@@ -396,7 +478,7 @@
     chunks = lax.all_to_all(spread(spectrum), "freq", split_axis=0, concat_axis=0, tiled=True)
 
     tile = jnp.transpose(velocity, (2, 3, 0, 1)).reshape(ROWS, COLS, 2 * LAYERS)
-    tile = jnp.pad(tile, ((0, 0), (0, 0), (0, LANES - 2 * LAYERS)))
+    tile = jnp.pad(tile, ((0, 0), (0, 0), (0, LANES - 2 * LAYERS))).reshape(ROWS * COLS, LANES)
 
     cos_table, sin_table = directions(DIR)
     speeds = speed_of(jnp.arange(FREQS, dtype=jnp.int32), FREQS)
@@ -416,11 +498,10 @@
             (0, band_index * ROWS, freq_index * COLS),
             (grid.shape[0], EXT_R, EXT_C),
         )
-        part = jnp.concatenate([part[:, :, HALO:], part[:, :, :HALO]], axis=2)
-        return jnp.broadcast_to(part[..., None], part.shape + (LANES,))
+        return jnp.broadcast_to(part[..., None], part.shape + (LANES,)).reshape(-1, LANES)
 
     flags = window(limiter_flags)
-    sea = window(sea_mask[None])[0]
+    sea = window(sea_mask[None])
 
     numbers = wavenumber(jnp.arange(FREQS, dtype=jnp.int32), FREQS) * DIR ** (-0.5)
     deposit = deposit_table(stokes_route) * numbers[:, None]
@@ -431,6 +512,9 @@
     weight_lo = (weight - weight_hi).astype(jnp.bfloat16)
     weights = [weight_hi.astype(jnp.bfloat16), weight_lo]
 
+    chunks, tile, flags, sea, waves, picker, weights = lax.optimization_barrier(
+        (chunks, tile, flags, sea, waves, picker, weights)
+    )
     fixed = [flags, sea, gain_matrix, quad_matrix]
     pieces = widen(*unpack(chunks, tile))
     results = run_cycle(True, [*pieces, *fixed, waves, picker, *weights])

time: 129 us -> 130 us (level)
  local copies, waits for them, and re-layouts: 3.97 us -> 7.17 us
  Pallas kernels: 22.8 us -> 20.1 us
  waiting for transfers between devices: 56.3 us -> 54.3 us
  other arithmetic: 1.4 us -> 3.08 us
    unnamed x16 -> x22, local copies, waits for them, and re-layouts: 1.09 us -> 4.29 us
    pallas_call x8, Pallas kernels: 22.8 us -> 20.1 us  [call(): pl.pallas_call(kernel, out_shape=out_shape, in_specs=in_specs or [vmem] *...]
    all_to_all x1, waiting for transfers between devices: 16.3 us -> 14.2 us  [body(): lax.all_to_all(spread(spectrum), 'freq', split_axis=0, concat_axis=0, til...]
  transfers between devices with their start and end apart: 10 -> 10, of which waited for: 10 -> 10; matrix products, arithmetic and copies ran while one was open for 3% -> 4% of each run, Pallas kernels for 0% -> 0%
where the time goes in v5:
time: 130 us; the launch traced here: 129 us
  waiting for transfers between devices  54.3 us (42%)
  starting transfers between devices  43.1 us (33%)
  Pallas kernels  20.1 us (15%)
  local copies, waits for them, and re-layouts  7.17 us (6%)
  other arithmetic  3.08 us (2%)
    pallas_call x8, Pallas kernels, call(): pl.pallas_call(kernel, out_shape=out_shape, in_specs=in_specs or [vmem] *...  20.1 us
    all_to_all x1, waiting for transfers between devices, body(): lax.all_to_all(chunks, 'freq', split_axis=0, concat_axis=0, tiled=True)  16.6 us
    all_to_all x1, waiting for transfers between devices, body(): lax.all_to_all(spread(spectrum), 'freq', split_axis=0, concat_axis=0, til...  14.2 us
    all_to_all x1, starting transfers between devices, body(): lax.all_to_all(spread(spectrum), 'freq', split_axis=0, concat_axis=0, til...  11.5 us
    all_to_all x1, starting transfers between devices, body(): lax.all_to_all(chunks, 'freq', split_axis=0, concat_axis=0, tiled=True)  11 us
    ppermute x2, starting transfers between devices, widen(): from_last = lax.ppermute(to_next, 'freq', line(FREQS, -1))  8.02 us
    ppermute x2, waiting for transfers between devices, widen(): from_next = lax.ppermute(to_last, 'freq', line(FREQS, 1))  7.98 us
    ppermute x2, waiting for transfers between devices, widen(): from_down = lax.ppermute(last, 'band', line(BANDS, -1))  7.64 us
  transfers between devices with their start and end apart: 10, of which 10 were waited for; matrix products, arithmetic and copies ran while one was open for 4% of the time, Pallas kernels for 0%

profile of v5, /device:TPU:34, one launch (start us, length us, event | category | flops | bytes accessed | tf_op | source)
XLA Modules:
  0.0 128.9 jit_solution(18262628139836228830)
XLA Ops:
  0.6 1.1 copy-done.5
  1.7 2.2 %spread.1 = f32[32,9,4,128]{3,2,1,0:T(4,128)} custom-call(f32[576,256]{1,0:T(8,128)S(1)} %bitcast.19), custom_call_target="tpu_custom_call" | custom-call | tf_op jit(solution)/shard_map/spread/pallas_call | solution.py:403
  3.9 11.5 %all-to-all-start = ((f32[288,4,128]{2,1,0:T(4,128)}), f32[288,4,128]{2,1,0:T(4,128)S(1)}, u32[]{:S(2)}, u32[]{:S(2)}) async-start(f32[288,4,128]{2,1,0:T(4,128)} %bitcast.1), calls=%async_computation | async-start | bytes 1179648 | tf_op jit(solution)/shard_map/all_to_all | solution.py:478
  17.7 0.9 fusion.1
  19.1 1.2 add_convert_fusion.refs_10_
  20.2 14.2 %all-to-all-done.x_ref = f32[288,4,128]{2,1,0:T(4,128)S(1)} async-done(((f32[288,4,128]{2,1,0:T(4,128)}), f32[288,4,128]{2,1,0:T(4,128)S(1)}, u32[]{:S(2)}, u32[]{:S(2)}) %all-to-all-start) | async-done | bytes 589856 | tf_op jit(solution)/shard_map/all_to_all | solution.py:478
  35.3 2.1 %collective-permute-start = (f32[640,128]{1,0:T(8,128)S(1)}, f32[640,128]{1,0:T(8,128)S(1)}, u32[]{:S(2)}, u32[]{:S(2)}) collective-permute-start(f32[640,128]{1,0:T(8,128)S(1)} %get-tuple-element.28), channel_id=1, source_target_pairs={{1,0},{2,1},{3,2},{4,3},{5,4},{6,5},{7,6},{8,7},{9,8},{10,9},{11,1... | collective-permute-start | bytes 983048 | tf_op jit(solution)/shard_map/ppermute | solution.py:61
  37.4 3.9 %collective-permute-start.1 = (f32[640,128]{1,0:T(8,128)S(1)}, f32[640,128]{1,0:T(8,128)S(1)}, u32[]{:S(2)}, u32[]{:S(2)}) collective-permute-start(f32[640,128]{1,0:T(8,128)S(1)} %get-tuple-element.29), channel_id=1, source_target_pairs={{0,1},{1,2},{2,3},{3,4},{4,5},{5,6},{6,7},{7,8},{8,9},{9,10},{10,1... | collective-permute-start | bytes 983048 | tf_op jit(solution)/shard_map/ppermute | solution.py:62
  41.3 3.1 %collective-permute-done.from_next.refs_1_ = f32[640,128]{1,0:T(8,128)S(1)} collective-permute-done((f32[640,128]{1,0:T(8,128)S(1)}, f32[640,128]{1,0:T(8,128)S(1)}, u32[]{:S(2)}, u32[]{:S(2)}) %collective-permute-start) | collective-permute-done | bytes 327712 | tf_op jit(solution)/shard_map/ppermute | solution.py:61
  44.4 1.9 %collective-permute-done.1.from_last.refs_2_ = f32[640,128]{1,0:T(8,128)S(1)} collective-permute-done((f32[640,128]{1,0:T(8,128)S(1)}, f32[640,128]{1,0:T(8,128)S(1)}, u32[]{:S(2)}, u32[]{:S(2)}) %collective-permute-start.1) | collective-permute-done | bytes 327712 | tf_op jit(solution)/shard_map/ppermute | solution.py:62
  46.4 1.9 %collective-permute-start.2 = (f32[640,128]{1,0:T(8,128)S(1)}, f32[640,128]{1,0:T(8,128)S(1)}, u32[]{:S(2)}, u32[]{:S(2)}) collective-permute-start(f32[640,128]{1,0:T(8,128)S(1)} %get-tuple-element.30), channel_id=1, source_target_pairs={{32,0},{64,32},{96,64},{128,96},{160,128},{192,160},{224,192},{33,... | collective-permute-start | bytes 983048 | tf_op jit(solution)/shard_map/ppermute | solution.py:64
  48.3 2.4 %collective-permute-start.3 = (f32[640,128]{1,0:T(8,128)S(1)}, f32[640,128]{1,0:T(8,128)S(1)}, u32[]{:S(2)}, u32[]{:S(2)}) collective-permute-start(f32[640,128]{1,0:T(8,128)S(1)} %get-tuple-element.31), channel_id=1, source_target_pairs={{0,32},{32,64},{64,96},{96,128},{128,160},{160,192},{192,224},{1,3... | collective-permute-start | bytes 983048 | tf_op jit(solution)/shard_map/ppermute | solution.py:65
  50.8 2.2 %collective-permute-done.2.refs_3_ = f32[640,128]{1,0:T(8,128)S(1)} collective-permute-done((f32[640,128]{1,0:T(8,128)S(1)}, f32[640,128]{1,0:T(8,128)S(1)}, u32[]{:S(2)}, u32[]{:S(2)}) %collective-permute-start.2) | collective-permute-done | bytes 327712 | tf_op jit(solution)/shard_map/ppermute | solution.py:64
  52.9 3.8 %collective-permute-done.3.refs_4_ = f32[640,128]{1,0:T(8,128)S(1)} collective-permute-done((f32[640,128]{1,0:T(8,128)S(1)}, f32[640,128]{1,0:T(8,128)S(1)}, u32[]{:S(2)}, u32[]{:S(2)}) %collective-permute-start.3) | collective-permute-done | bytes 327712 | tf_op jit(solution)/shard_map/ppermute | solution.py:65
  56.7 1.3 copy-done.2
  58.0 1.0 copy-done.3
  59.0 1.0 copy-done.4
  59.9 8.0 %cycle_first.1 = (f32[1280,128]{1,0:T(8,128)S(1)}, f32[640,128]{1,0:T(8,128)S(1)}, f32[640,128]{1,0:T(8,128)S(1)}, f32[24,16,128]{2,1,0:T(8,128)S(1)}, f32[12288...) custom-call(f32[1280,128]{1,0:T(8,128)S(1)} %get-tuple-element.27.own.refs_0_, ...), custom_call_target="tpu_custom_call" | custom-call | tf_op jit(solution)/shard_map/cycle_first/pallas_call | solution.py:403
  68.0 1.9 %collective-permute-start.4 = (f32[640,128]{1,0:T(8,128)S(1)}, f32[640,128]{1,0:T(8,128)S(1)}, u32[]{:S(2)}, u32[]{:S(2)}) collective-permute-start(f32[640,128]{1,0:T(8,128)S(1)} %get-tuple-element.39), channel_id=1, source_target_pairs={{1,0},{2,1},{3,2},{4,3},{5,4},{6,5},{7,6},{8,7},{9,8},{10,9},{11,1... | collective-permute-start | bytes 983048 | tf_op jit(solution)/shard_map/ppermute | solution.py:61
  69.9 4.1 %collective-permute-start.5 = (f32[640,128]{1,0:T(8,128)S(1)}, f32[640,128]{1,0:T(8,128)S(1)}, u32[]{:S(2)}, u32[]{:S(2)}) collective-permute-start(f32[640,128]{1,0:T(8,128)S(1)} %get-tuple-element.40), channel_id=1, source_target_pairs={{0,1},{1,2},{2,3},{3,4},{4,5},{5,6},{6,7},{7,8},{8,9},{9,10},{10,1... | collective-permute-start | bytes 983048 | tf_op jit(solution)/shard_map/ppermute | solution.py:62
  74.0 4.9 %collective-permute-done.4.from_next.refs_1_ = f32[640,128]{1,0:T(8,128)S(1)} collective-permute-done((f32[640,128]{1,0:T(8,128)S(1)}, f32[640,128]{1,0:T(8,128)S(1)}, u32[]{:S(2)}, u32[]{:S(2)}) %collective-permute-start.4) | collective-permute-done | bytes 327712 | tf_op jit(solution)/shard_map/ppermute | solution.py:61
  78.9 1.6 %collective-permute-done.5.from_last.refs_2_ = f32[640,128]{1,0:T(8,128)S(1)} collective-permute-done((f32[640,128]{1,0:T(8,128)S(1)}, f32[640,128]{1,0:T(8,128)S(1)}, u32[]{:S(2)}, u32[]{:S(2)}) %collective-permute-start.5) | collective-permute-done | bytes 327712 | tf_op jit(solution)/shard_map/ppermute | solution.py:62
  80.6 1.9 %collective-permute-start.6 = (f32[640,128]{1,0:T(8,128)S(1)}, f32[640,128]{1,0:T(8,128)S(1)}, u32[]{:S(2)}, u32[]{:S(2)}) collective-permute-start(f32[640,128]{1,0:T(8,128)S(1)} %get-tuple-element.41), channel_id=1, source_target_pairs={{32,0},{64,32},{96,64},{128,96},{160,128},{192,160},{224,192},{33,... | collective-permute-start | bytes 983048 | tf_op jit(solution)/shard_map/ppermute | solution.py:64
  82.6 2.4 %collective-permute-start.7 = (f32[640,128]{1,0:T(8,128)S(1)}, f32[640,128]{1,0:T(8,128)S(1)}, u32[]{:S(2)}, u32[]{:S(2)}) collective-permute-start(f32[640,128]{1,0:T(8,128)S(1)} %get-tuple-element.42), channel_id=1, source_target_pairs={{0,32},{32,64},{64,96},{96,128},{128,160},{160,192},{192,224},{1,3... | collective-permute-start | bytes 983048 | tf_op jit(solution)/shard_map/ppermute | solution.py:65
  85.0 2.2 %collective-permute-done.6.refs_3_ = f32[640,128]{1,0:T(8,128)S(1)} collective-permute-done((f32[640,128]{1,0:T(8,128)S(1)}, f32[640,128]{1,0:T(8,128)S(1)}, u32[]{:S(2)}, u32[]{:S(2)}) %collective-permute-start.6) | collective-permute-done | bytes 327712 | tf_op jit(solution)/shard_map/ppermute | solution.py:64
  87.1 3.8 %collective-permute-done.7.refs_4_ = f32[640,128]{1,0:T(8,128)S(1)} collective-permute-done((f32[640,128]{1,0:T(8,128)S(1)}, f32[640,128]{1,0:T(8,128)S(1)}, u32[]{:S(2)}, u32[]{:S(2)}) %collective-permute-start.7) | collective-permute-done | bytes 327712 | tf_op jit(solution)/shard_map/ppermute | solution.py:65
  91.0 6.3 %cycle_last.1 = (f32[288,4,128]{2,1,0:T(4,128)}, f32[24,16,128]{2,1,0:T(8,128)S(1)}) custom-call(f32[1280,128]{1,0:T(8,128)S(1)} %get-tuple-element.38.own.refs_0_, f32[640,128]{1,0:T(8,128)S(1)} %collective-permute-done.4.from_next.refs_1_, f32[640,128]{1,0:T(8,128)S(1)} %collective-permute-done.5.from_last.refs_2_, ...), custom_call_target="tpu_custom_call" | custom-call | tf_op jit(solution)/shard_map/cycle_last/pallas_call | solution.py:403
  97.2 11.0 %all-to-all-start.1 = ((f32[288,4,128]{2,1,0:T(4,128)}), f32[288,4,128]{2,1,0:T(4,128)S(1)}, u32[]{:S(2)}, u32[]{:S(2)}) async-start(f32[288,4,128]{2,1,0:T(4,128)} %get-tuple-element.45), calls=%async_computation.1 | async-start | bytes 1179648 | tf_op jit(solution)/shard_map/all_to_all | solution.py:524
  108.2 0.5 ocean.1
  108.9 0.7 copy.22
  109.6 16.6 %all-to-all-done.1 = f32[288,4,128]{2,1,0:T(4,128)S(1)} async-done(((f32[288,4,128]{2,1,0:T(4,128)}), f32[288,4,128]{2,1,0:T(4,128)S(1)}, u32[]{:S(2)}, u32[]{:S(2)}) %all-to-all-start.1) | async-done | bytes 589856 | tf_op jit(solution)/shard_map/all_to_all | solution.py:524
  126.2 2.6 %collect.1 = f32[576,256]{1,0:T(8,128)} custom-call(f32[32,9,4,128]{3,2,1,0:T(4,128)S(1)} %bitcast.18), custom_call_target="tpu_custom_call" | custom-call | tf_op jit(solution)/shard_map/collect/pallas_call | solution.py:403
  (51 shorter events, 3.7 us)
Async XLA Ops:
  0.6 1.1 copy-start.5
  1.7 13.9 %copy-start.7 = (s32[128,256]{1,0:T(8,128)S(1)}, s32[128,256]{1,0:T(8,128)}, u32[]{:S(2)}) copy-start(s32[128,256]{1,0:T(8,128)} %param.14) | copy-start | bytes 393220
  1.7 14.2 %copy-start.10 = (s32[32]{0:T(128)S(1)}, s32[32]{0:T(128)}, u32[]{:S(2)}) copy-start(s32[32]{0:T(128)} %param.15) | copy-start | bytes 388
  1.7 14.6 %copy-start.6 = (s32[8,128,256]{2,1,0:T(8,128)S(1)}, s32[8,128,256]{2,1,0:T(8,128)}, u32[]{:S(2)}) copy-start(s32[8,128,256]{2,1,0:T(8,128)} %param.13) | copy-start | bytes 3145732
  3.9 12.6 %copy-start.8 = (f32[2,24,16,8]{1,3,2,0:T(8,128)S(1)}, f32[2,24,16,8]{1,3,2,0:T(8,128)}, u32[]{:S(2)}) copy-start(f32[2,24,16,8]{1,3,2,0:T(8,128)} %param.10) | copy-start | bytes 73732
  3.9 30.5 %all-to-all-start = ((f32[288,4,128]{2,1,0:T(4,128)}), f32[288,4,128]{2,1,0:T(4,128)S(1)}, u32[]{:S(2)}, u32[]{:S(2)}) async-start(f32[288,4,128]{2,1,0:T(4,128)} %bitcast.1), calls=%async_computation | async-start | bytes 1179648 | tf_op jit(solution)/shard_map/all_to_all | solution.py:478
  15.4 1.3 %copy-start.9 = (s32[32,4]{0,1:T(4,128)S(1)}, s32[32,4]{0,1:T(4,128)}, u32[]{:S(2)}) copy-start(s32[32,4]{0,1:T(4,128)} %param.16) | copy-start | bytes 1540
  19.0 37.7 %copy-start.1 = (bf16[1152,1152]{1,0:T(8,128)(2,1)S(1)}, bf16[1152,1152]{1,0:T(8,128)(2,1)}, u32[]{:S(2)}) copy-start(bf16[1152,1152]{1,0:T(8,128)(2,1)} %refs_8_.3) | copy-start | bytes 7962628
  34.6 22.2 %copy-start = (bf16[1152,1152]{1,0:T(8,128)(2,1)S(1)}, bf16[1152,1152]{1,0:T(8,128)(2,1)}, u32[]{:S(2)}) copy-start(bf16[1152,1152]{1,0:T(8,128)(2,1)} %refs_7_.3) | copy-start | bytes 7962628
  35.3 9.1 %collective-permute-start = (f32[640,128]{1,0:T(8,128)S(1)}, f32[640,128]{1,0:T(8,128)S(1)}, u32[]{:S(2)}, u32[]{:S(2)}) collective-permute-start(f32[640,128]{1,0:T(8,128)S(1)} %get-tuple-element.28), channel_id=1, source_target_pairs={{1,0},{2,1},{3,2},{4,3},{5,4},{6,5},{7,6},{8,7},{9,8},{10,9},{11,1... | collective-permute-start | bytes 983048 | tf_op jit(solution)/shard_map/ppermute | solution.py:61
  37.4 9.0 %collective-permute-start.1 = (f32[640,128]{1,0:T(8,128)S(1)}, f32[640,128]{1,0:T(8,128)S(1)}, u32[]{:S(2)}, u32[]{:S(2)}) collective-permute-start(f32[640,128]{1,0:T(8,128)S(1)} %get-tuple-element.29), channel_id=1, source_target_pairs={{0,1},{1,2},{2,3},{3,4},{4,5},{5,6},{6,7},{7,8},{8,9},{9,10},{10,1... | collective-permute-start | bytes 983048 | tf_op jit(solution)/shard_map/ppermute | solution.py:62
  46.4 6.5 %collective-permute-start.2 = (f32[640,128]{1,0:T(8,128)S(1)}, f32[640,128]{1,0:T(8,128)S(1)}, u32[]{:S(2)}, u32[]{:S(2)}) collective-permute-start(f32[640,128]{1,0:T(8,128)S(1)} %get-tuple-element.30), channel_id=1, source_target_pairs={{32,0},{64,32},{96,64},{128,96},{160,128},{192,160},{224,192},{33,... | collective-permute-start | bytes 983048 | tf_op jit(solution)/shard_map/ppermute | solution.py:64
  48.3 8.4 %collective-permute-start.3 = (f32[640,128]{1,0:T(8,128)S(1)}, f32[640,128]{1,0:T(8,128)S(1)}, u32[]{:S(2)}, u32[]{:S(2)}) collective-permute-start(f32[640,128]{1,0:T(8,128)S(1)} %get-tuple-element.31), channel_id=1, source_target_pairs={{0,32},{32,64},{64,96},{96,128},{128,160},{160,192},{192,224},{1,3... | collective-permute-start | bytes 983048 | tf_op jit(solution)/shard_map/ppermute | solution.py:65
  56.7 1.3 copy-start.2
  58.0 1.0 copy-start.3
  59.0 1.0 copy-start.4
  68.0 10.9 %collective-permute-start.4 = (f32[640,128]{1,0:T(8,128)S(1)}, f32[640,128]{1,0:T(8,128)S(1)}, u32[]{:S(2)}, u32[]{:S(2)}) collective-permute-start(f32[640,128]{1,0:T(8,128)S(1)} %get-tuple-element.39), channel_id=1, source_target_pairs={{1,0},{2,1},{3,2},{4,3},{5,4},{6,5},{7,6},{8,7},{9,8},{10,9},{11,1... | collective-permute-start | bytes 983048 | tf_op jit(solution)/shard_map/ppermute | solution.py:61
  69.9 10.6 %collective-permute-start.5 = (f32[640,128]{1,0:T(8,128)S(1)}, f32[640,128]{1,0:T(8,128)S(1)}, u32[]{:S(2)}, u32[]{:S(2)}) collective-permute-start(f32[640,128]{1,0:T(8,128)S(1)} %get-tuple-element.40), channel_id=1, source_target_pairs={{0,1},{1,2},{2,3},{3,4},{4,5},{5,6},{6,7},{7,8},{8,9},{9,10},{10,1... | collective-permute-start | bytes 983048 | tf_op jit(solution)/shard_map/ppermute | solution.py:62
  80.6 6.5 %collective-permute-start.6 = (f32[640,128]{1,0:T(8,128)S(1)}, f32[640,128]{1,0:T(8,128)S(1)}, u32[]{:S(2)}, u32[]{:S(2)}) collective-permute-start(f32[640,128]{1,0:T(8,128)S(1)} %get-tuple-element.41), channel_id=1, source_target_pairs={{32,0},{64,32},{96,64},{128,96},{160,128},{192,160},{224,192},{33,... | collective-permute-start | bytes 983048 | tf_op jit(solution)/shard_map/ppermute | solution.py:64
  82.6 8.4 %collective-permute-start.7 = (f32[640,128]{1,0:T(8,128)S(1)}, f32[640,128]{1,0:T(8,128)S(1)}, u32[]{:S(2)}, u32[]{:S(2)}) collective-permute-start(f32[640,128]{1,0:T(8,128)S(1)} %get-tuple-element.42), channel_id=1, source_target_pairs={{0,32},{32,64},{64,96},{96,128},{128,160},{160,192},{192,224},{1,3... | collective-permute-start | bytes 983048 | tf_op jit(solution)/shard_map/ppermute | solution.py:65
  97.2 28.9 %all-to-all-start.1 = ((f32[288,4,128]{2,1,0:T(4,128)}), f32[288,4,128]{2,1,0:T(4,128)S(1)}, u32[]{:S(2)}, u32[]{:S(2)}) async-start(f32[288,4,128]{2,1,0:T(4,128)} %get-tuple-element.45), calls=%async_computation.1 | async-start | bytes 1179648 | tf_op jit(solution)/shard_map/all_to_all | solution.py:524

commit v6 on v5

--- a/solution.py
+++ b/solution.py
@@ -202,7 +202,7 @@
     return lower * (half_courant + q) + upper * (half_courant - q)
 
 
-def courants(ext_ref, lane_ref, pick_ref, main_ref, rest_ref):
+def courants(ext_ref, lane_ref, main_ref, rest_ref):
     lane = lax.broadcasted_iota(jnp.int32, (EXT_C, LANES), 1)
     quarter = (0.25 * 0.15) * jnp.tanh(ext_ref[...])
     faces = []
@@ -216,10 +216,15 @@
     middle = rest.astype(jnp.bfloat16).astype(f32)
     parts = jnp.concatenate([high + pltpu.roll(middle, LANES // 2, 1), rest - middle], axis=1)
     parts = parts.astype(jnp.bfloat16)
+    layer = lax.broadcasted_iota(jnp.int32, (2 * LAYERS, LANES), 0).astype(f32)
+    blank = jnp.zeros((LANES, LANES), f32)
+    short, long = blank[: LANES // 2 - 2 * LAYERS], blank[: LANES - 2 * LAYERS]
     for index in range(2):
         for k in range(GROUPS):
             lanes = slice(k * LANES, (k + 1) * LANES)
-            picked = jnp.dot(parts, pick_ref[index, :, lanes], preferred_element_type=f32)
+            hit = jnp.where(layer == lane_ref[2, :, lanes] + LAYERS * index, 1.0, 0.0)
+            picker = jnp.concatenate([hit, short, hit, short, hit, long], axis=0)
+            picked = jnp.dot(parts, picker.astype(jnp.bfloat16), preferred_element_type=f32)
             half_courant = lane_ref[index, :, lanes] + picked
             square = (half_courant + half_courant) * half_courant
             for which, value in ((2 * index, half_courant), (2 * index + 1, square)):
@@ -303,6 +308,13 @@
             flag = flag_above
 
 
+def stokes_weights(angle_ref, deposit_ref, weight_ref):
+    for g in range(FREQS):
+        rows = angle_ref[...] * deposit_ref[g : g + 1, :]
+        for d in range(0, DIR, 4):
+            weight_ref[g * DIR + d : g * DIR + d + 4, :] = rows[d : d + 4]
+
+
 def cycle_kernel(first, *refs):
     refs = list(refs)
     take = lambda n: [refs.pop(0) for _ in range(n)]
@@ -310,7 +322,7 @@
     flag_ref, sea_ref, gain_ref, quad_ref = take(4)
     flag_base = 0 if first else SUB
     if first:
-        lane_ref, pick_ref, weight_hi, weight_lo = take(4)
+        lane_ref, angle_ref, deposit_ref = take(3)
         out_refs = take(3)
         (ext_ref,) = take(1)
         main_ref, rest_ref = take(2)
@@ -318,11 +330,14 @@
         main_ref, rest_ref = take(2)
         out_hbm, ext_ref = take(2)
     cell_ref, tile_ref, energy_ref = take(3)
-    if not first:
+    if first:
+        (weight_ref,) = take(1)
+        stokes_weights(angle_ref, deposit_ref, weight_ref)
+    else:
         chunk_ref, sems = take(2)
     fill(ext_ref, pieces, GROUPS)
     if first:
-        courants(ext_ref, lane_ref, pick_ref, main_ref, rest_ref)
+        courants(ext_ref, lane_ref, main_ref, rest_ref)
     fill_cells(cell_ref, pieces)
     fill(tile_ref, pieces, MAIN)
     advect_rest(tile_ref, rest_ref, flag_ref, sea_ref, energy_ref, flag_base)
@@ -339,7 +354,10 @@
     if first:
         rest = (energy - rounded.astype(f32)).astype(jnp.bfloat16)
         mm = lambda a, b: jnp.dot(a, b, preferred_element_type=f32)
-        stokes = mm(rounded, weight_hi[...]) + (mm(rest, weight_hi[...]) + mm(rounded, weight_lo[...]))
+        weight = weight_ref[...]
+        weight_hi = weight.astype(jnp.bfloat16)
+        weight_lo = (weight - weight_hi.astype(f32)).astype(jnp.bfloat16)
+        stokes = mm(rounded, weight_hi) + (mm(rest, weight_hi) + mm(rounded, weight_lo))
         put(stokes, out_refs, GROUPS)
     nt = (((1,), (1,)), ((), ()))
     for k in range(GROUPS):
@@ -419,7 +437,7 @@
 def spread(x):
     x = x.reshape(DIR * ROWS, 2 * LANES)
     scratch = [halves, chunks_dims, sems((10,)), sems((2,))]
-    out = call(spread_kernel, "spread", [x], shape_of(*chunks_dims), scratch, 4, [hbm], hbm)
+    out = call(spread_kernel, "spread", [x], shape_of(*chunks_dims), scratch, 60, [hbm], hbm)
     return out.reshape(QUADS, 4, LANES)
 
 
@@ -448,6 +466,7 @@
     if first:
         faces = [shape_of(4 * CELLS * MAIN, LANES), shape_of(4, EXT_R, EXT_C, LANES)]
         out_shape = tile_shapes + [ext_shape] + faces
+        scratch += [(COMP, LANES)]
         out_specs = [vmem] * 6
     else:
         out_shape = [shape_of(QUADS, 4, LANES), ext_shape]
@@ -484,12 +503,8 @@
     speeds = speed_of(jnp.arange(FREQS, dtype=jnp.int32), FREQS)
     waves = 0.5 * speeds[None, :, None] * jnp.stack([cos_table, sin_table])[:, None, :]
     waves = waves.reshape(2, 1, COMP)
-    lane_ids = jnp.arange(LANES, dtype=jnp.int32)[None, :, None]
-    routes = jnp.repeat(current_route, DIR)[None, None, :]
-    starts = jnp.array([0, LAYERS], jnp.int32)[:, None, None]
-    wanted = routes + starts
-    high = (lane_ids == wanted) | (lane_ids == wanted + LANES // 2)
-    picker = jnp.concatenate([high, lane_ids == wanted], axis=1).astype(jnp.bfloat16)
+    routes = jnp.repeat(current_route, DIR).astype(f32)[None, None, :]
+    waves = jnp.concatenate([waves, routes], axis=0)
 
     def window(grid):
         padded = jnp.pad(grid, ((0, 0), (HALO, HALO), (HALO, HALO))).astype(f32)
@@ -505,19 +520,15 @@
 
     numbers = wavenumber(jnp.arange(FREQS, dtype=jnp.int32), FREQS) * DIR ** (-0.5)
     deposit = deposit_table(stokes_route) * numbers[:, None]
-    both = jnp.stack([cos_table, sin_table])
-    weight = (both.T[None, :, :, None] * deposit[:, None, None, :]).reshape(COMP, 2 * LAYERS)
-    weight = jnp.pad(weight, ((0, 0), (0, LANES - 2 * LAYERS)))
-    weight_hi = lax.reduce_precision(weight, 8, 7)
-    weight_lo = (weight - weight_hi).astype(jnp.bfloat16)
-    weights = [weight_hi.astype(jnp.bfloat16), weight_lo]
-
-    chunks, tile, flags, sea, waves, picker, weights = lax.optimization_barrier(
-        (chunks, tile, flags, sea, waves, picker, weights)
-    )
+    deposit = jnp.pad(jnp.tile(deposit, (1, 2)), ((0, 0), (0, LANES - 2 * LAYERS)))
+    eastward = jnp.arange(LANES) < LAYERS
+    angles = jnp.where(eastward[None, :], cos_table[:, None], sin_table[:, None])
+
+    tables = [waves, angles, deposit]
+    chunks, tile, flags, sea, tables = lax.optimization_barrier((chunks, tile, flags, sea, tables))
     fixed = [flags, sea, gain_matrix, quad_matrix]
     pieces = widen(*unpack(chunks, tile))
-    results = run_cycle(True, [*pieces, *fixed, waves, picker, *weights])
+    results = run_cycle(True, [*pieces, *fixed, *tables])
     velocity_ext, faces = results[3], results[4:]
     pieces = widen(*results[:3])
     chunks, stokes_ext = run_cycle(False, [*pieces, *fixed, *faces])

time: 130 us -> 129 us (level)
  waiting for transfers between devices: 54.3 us -> 50.2 us
  other arithmetic: 3.08 us -> 4.56 us
    all_to_all x1, waiting for transfers between devices: 14.2 us -> 10.1 us  [body(): lax.all_to_all(spread(spectrum), 'freq', split_axis=0, concat_axis=0, til...]
    unnamed x22 -> x12, local copies, waits for them, and re-layouts: 4.29 us -> 1.77 us
    convert_element_type x2 -> x1, other arithmetic: 2.08 us -> 0.01 us  [body(): routes = jnp.repeat(current_route, DIR).astype(f32)[None, None, :]]
    concatenate x0 -> x1, other arithmetic: none -> 1.3 us  [body(): waves = jnp.concatenate([waves, routes], axis=0)]
  transfers between devices with their start and end apart: 10 -> 10, of which waited for: 10 -> 10; matrix products, arithmetic and copies ran while one was open for 4% -> 7% of each run, Pallas kernels for 0% -> 0%
where the time goes in v6:
time: 129 us; the launch traced here: 128 us
  waiting for transfers between devices  50.2 us (39%)
  starting transfers between devices  42.9 us (33%)
  Pallas kernels  21.1 us (16%)
  local copies, waits for them, and re-layouts  8.01 us (6%)
  other arithmetic  4.56 us (4%)
    pallas_call x8, Pallas kernels, call(): pl.pallas_call(kernel, out_shape=out_shape, in_specs=in_specs or [vmem] *...  21.1 us
    all_to_all x1, waiting for transfers between devices, body(): lax.all_to_all(chunks, 'freq', split_axis=0, concat_axis=0, tiled=True)  16.6 us
    all_to_all x1, starting transfers between devices, body(): lax.all_to_all(spread(spectrum), 'freq', split_axis=0, concat_axis=0, til...  11.4 us
    all_to_all x1, starting transfers between devices, body(): lax.all_to_all(chunks, 'freq', split_axis=0, concat_axis=0, tiled=True)  11 us
    all_to_all x1, waiting for transfers between devices, body(): lax.all_to_all(spread(spectrum), 'freq', split_axis=0, concat_axis=0, til...  10.1 us
    ppermute x2, waiting for transfers between devices, widen(): from_next = lax.ppermute(to_last, 'freq', line(FREQS, 1))  8.15 us
    ppermute x2, starting transfers between devices, widen(): from_last = lax.ppermute(to_next, 'freq', line(FREQS, -1))  7.84 us
    ppermute x2, waiting for transfers between devices, widen(): from_down = lax.ppermute(last, 'band', line(BANDS, -1))  7.64 us
  transfers between devices with their start and end apart: 10, of which 10 were waited for; matrix products, arithmetic and copies ran while one was open for 7% of the time, Pallas kernels for 0%

profile of v6, /device:TPU:34, one launch (start us, length us, event | category | flops | bytes accessed | tf_op | source)
XLA Modules:
  0.0 127.9 jit_solution(17687307142636056238)
XLA Ops:
  0.7 3.2 %spread.1 = f32[32,9,4,128]{3,2,1,0:T(4,128)} custom-call(f32[576,256]{1,0:T(8,128)} %bitcast.16), custom_call_target="tpu_custom_call" | custom-call | tf_op jit(solution)/shard_map/spread/pallas_call | solution.py:421
  3.9 11.4 %all-to-all-start = ((f32[288,4,128]{2,1,0:T(4,128)}), f32[288,4,128]{2,1,0:T(4,128)S(1)}, u32[]{:S(2)}, u32[]{:S(2)}) async-start(f32[288,4,128]{2,1,0:T(4,128)} %bitcast.15), calls=%async_computation | async-start | bytes 1179648 | tf_op jit(solution)/shard_map/all_to_all | solution.py:497
  15.4 0.9 fusion.1
  19.3 0.7 mul.118
  20.1 1.0 copy.16
  21.3 0.8 broadcast_select_fusion.refs_10_
  22.1 0.7 broadcast_multiply_fusion.1
  22.8 1.3 %pad_maximum_fusion.refs_9_ = f32[3,1,1152]{2,1,0:T(1,128)} fusion(f32[1,1,1152]{2,1,0:T(1,128)} %convert_element_type.43, f32[2,1,1152]{2,1,0:T(1,128)S(1)} %broadcast_multiply_fusion.1), kind=kLoop, calls=%fused_computation.7 | loop fusion | flops 3456 | bytes 27648 | tf_op jit(solution)/shard_map/concatenate | solution.py:507
  24.1 10.1 %all-to-all-done.x_ref = f32[288,4,128]{2,1,0:T(4,128)S(1)} async-done(((f32[288,4,128]{2,1,0:T(4,128)}), f32[288,4,128]{2,1,0:T(4,128)S(1)}, u32[]{:S(2)}, u32[]{:S(2)}) %all-to-all-start) | async-done | bytes 589856 | tf_op jit(solution)/shard_map/all_to_all | solution.py:497
  34.3 0.8 broadcast_in_dim.60.refs_6_.sea_ref
  35.8 1.9 %collective-permute-start = (f32[640,128]{1,0:T(8,128)S(1)}, f32[640,128]{1,0:T(8,128)S(1)}, u32[]{:S(2)}, u32[]{:S(2)}) collective-permute-start(f32[640,128]{1,0:T(8,128)S(1)} %get-tuple-element.27), channel_id=1, source_target_pairs={{1,0},{2,1},{3,2},{4,3},{5,4},{6,5},{7,6},{8,7},{9,8},{10,9},{11,1... | collective-permute-start | bytes 983048 | tf_op jit(solution)/shard_map/ppermute | solution.py:61
  37.7 3.9 %collective-permute-start.1 = (f32[640,128]{1,0:T(8,128)S(1)}, f32[640,128]{1,0:T(8,128)S(1)}, u32[]{:S(2)}, u32[]{:S(2)}) collective-permute-start(f32[640,128]{1,0:T(8,128)S(1)} %get-tuple-element.28), channel_id=1, source_target_pairs={{0,1},{1,2},{2,3},{3,4},{4,5},{5,6},{6,7},{7,8},{8,9},{9,10},{10,1... | collective-permute-start | bytes 983048 | tf_op jit(solution)/shard_map/ppermute | solution.py:62
  41.6 3.1 %collective-permute-done.from_next.refs_1_ = f32[640,128]{1,0:T(8,128)S(1)} collective-permute-done((f32[640,128]{1,0:T(8,128)S(1)}, f32[640,128]{1,0:T(8,128)S(1)}, u32[]{:S(2)}, u32[]{:S(2)}) %collective-permute-start) | collective-permute-done | bytes 327712 | tf_op jit(solution)/shard_map/ppermute | solution.py:61
  44.8 1.9 %collective-permute-done.1.from_last.refs_2_ = f32[640,128]{1,0:T(8,128)S(1)} collective-permute-done((f32[640,128]{1,0:T(8,128)S(1)}, f32[640,128]{1,0:T(8,128)S(1)}, u32[]{:S(2)}, u32[]{:S(2)}) %collective-permute-start.1) | collective-permute-done | bytes 327712 | tf_op jit(solution)/shard_map/ppermute | solution.py:62
  46.8 1.9 %collective-permute-start.2 = (f32[640,128]{1,0:T(8,128)S(1)}, f32[640,128]{1,0:T(8,128)S(1)}, u32[]{:S(2)}, u32[]{:S(2)}) collective-permute-start(f32[640,128]{1,0:T(8,128)S(1)} %get-tuple-element.29), channel_id=1, source_target_pairs={{32,0},{64,32},{96,64},{128,96},{160,128},{192,160},{224,192},{33,... | collective-permute-start | bytes 983048 | tf_op jit(solution)/shard_map/ppermute | solution.py:64
  48.7 2.4 %collective-permute-start.3 = (f32[640,128]{1,0:T(8,128)S(1)}, f32[640,128]{1,0:T(8,128)S(1)}, u32[]{:S(2)}, u32[]{:S(2)}) collective-permute-start(f32[640,128]{1,0:T(8,128)S(1)} %get-tuple-element.30), channel_id=1, source_target_pairs={{0,32},{32,64},{64,96},{96,128},{128,160},{160,192},{192,224},{1,3... | collective-permute-start | bytes 983048 | tf_op jit(solution)/shard_map/ppermute | solution.py:65
  51.1 2.2 %collective-permute-done.2.refs_3_ = f32[640,128]{1,0:T(8,128)S(1)} collective-permute-done((f32[640,128]{1,0:T(8,128)S(1)}, f32[640,128]{1,0:T(8,128)S(1)}, u32[]{:S(2)}, u32[]{:S(2)}) %collective-permute-start.2) | collective-permute-done | bytes 327712 | tf_op jit(solution)/shard_map/ppermute | solution.py:64
  53.3 3.8 %collective-permute-done.3.refs_4_ = f32[640,128]{1,0:T(8,128)S(1)} collective-permute-done((f32[640,128]{1,0:T(8,128)S(1)}, f32[640,128]{1,0:T(8,128)S(1)}, u32[]{:S(2)}, u32[]{:S(2)}) %collective-permute-start.3) | collective-permute-done | bytes 327712 | tf_op jit(solution)/shard_map/ppermute | solution.py:65
  57.1 1.7 %copy-done.1 = bf16[1152,1152]{1,0:T(8,128)(2,1)S(1)} copy-done((bf16[1152,1152]{1,0:T(8,128)(2,1)S(1)}, bf16[1152,1152]{1,0:T(8,128)(2,1)}, u32[]{:S(2)}) %copy-start.1) | copy-done | bytes 2654232
  58.8 8.1 %cycle_first.1 = (f32[1280,128]{1,0:T(8,128)S(1)}, f32[640,128]{1,0:T(8,128)S(1)}, f32[640,128]{1,0:T(8,128)S(1)}, f32[24,16,128]{2,1,0:T(8,128)S(1)}, f32[12288...) custom-call(f32[1280,128]{1,0:T(8,128)S(1)} %get-tuple-element.26.own.refs_0_, ...), custom_call_target="tpu_custom_call" | custom-call | tf_op jit(solution)/shard_map/cycle_first/pallas_call | solution.py:421
  67.0 1.9 %collective-permute-start.4 = (f32[640,128]{1,0:T(8,128)S(1)}, f32[640,128]{1,0:T(8,128)S(1)}, u32[]{:S(2)}, u32[]{:S(2)}) collective-permute-start(f32[640,128]{1,0:T(8,128)S(1)} %get-tuple-element.37), channel_id=1, source_target_pairs={{1,0},{2,1},{3,2},{4,3},{5,4},{6,5},{7,6},{8,7},{9,8},{10,9},{11,1... | collective-permute-start | bytes 983048 | tf_op jit(solution)/shard_map/ppermute | solution.py:61
  68.9 3.9 %collective-permute-start.5 = (f32[640,128]{1,0:T(8,128)S(1)}, f32[640,128]{1,0:T(8,128)S(1)}, u32[]{:S(2)}, u32[]{:S(2)}) collective-permute-start(f32[640,128]{1,0:T(8,128)S(1)} %get-tuple-element.38), channel_id=1, source_target_pairs={{0,1},{1,2},{2,3},{3,4},{4,5},{5,6},{6,7},{7,8},{8,9},{9,10},{10,1... | collective-permute-start | bytes 983048 | tf_op jit(solution)/shard_map/ppermute | solution.py:62
  72.8 5.0 %collective-permute-done.4.from_next.refs_1_ = f32[640,128]{1,0:T(8,128)S(1)} collective-permute-done((f32[640,128]{1,0:T(8,128)S(1)}, f32[640,128]{1,0:T(8,128)S(1)}, u32[]{:S(2)}, u32[]{:S(2)}) %collective-permute-start.4) | collective-permute-done | bytes 327712 | tf_op jit(solution)/shard_map/ppermute | solution.py:61
  77.9 1.6 %collective-permute-done.5.from_last.refs_2_ = f32[640,128]{1,0:T(8,128)S(1)} collective-permute-done((f32[640,128]{1,0:T(8,128)S(1)}, f32[640,128]{1,0:T(8,128)S(1)}, u32[]{:S(2)}, u32[]{:S(2)}) %collective-permute-start.5) | collective-permute-done | bytes 327712 | tf_op jit(solution)/shard_map/ppermute | solution.py:62
  79.6 1.9 %collective-permute-start.6 = (f32[640,128]{1,0:T(8,128)S(1)}, f32[640,128]{1,0:T(8,128)S(1)}, u32[]{:S(2)}, u32[]{:S(2)}) collective-permute-start(f32[640,128]{1,0:T(8,128)S(1)} %get-tuple-element.39), channel_id=1, source_target_pairs={{32,0},{64,32},{96,64},{128,96},{160,128},{192,160},{224,192},{33,... | collective-permute-start | bytes 983048 | tf_op jit(solution)/shard_map/ppermute | solution.py:64
  81.5 2.6 %collective-permute-start.7 = (f32[640,128]{1,0:T(8,128)S(1)}, f32[640,128]{1,0:T(8,128)S(1)}, u32[]{:S(2)}, u32[]{:S(2)}) collective-permute-start(f32[640,128]{1,0:T(8,128)S(1)} %get-tuple-element.40), channel_id=1, source_target_pairs={{0,32},{32,64},{64,96},{96,128},{128,160},{160,192},{192,224},{1,3... | collective-permute-start | bytes 983048 | tf_op jit(solution)/shard_map/ppermute | solution.py:65
  84.1 2.0 %collective-permute-done.6.refs_3_ = f32[640,128]{1,0:T(8,128)S(1)} collective-permute-done((f32[640,128]{1,0:T(8,128)S(1)}, f32[640,128]{1,0:T(8,128)S(1)}, u32[]{:S(2)}, u32[]{:S(2)}) %collective-permute-start.6) | collective-permute-done | bytes 327712 | tf_op jit(solution)/shard_map/ppermute | solution.py:64
  86.1 3.8 %collective-permute-done.7.refs_4_ = f32[640,128]{1,0:T(8,128)S(1)} collective-permute-done((f32[640,128]{1,0:T(8,128)S(1)}, f32[640,128]{1,0:T(8,128)S(1)}, u32[]{:S(2)}, u32[]{:S(2)}) %collective-permute-start.7) | collective-permute-done | bytes 327712 | tf_op jit(solution)/shard_map/ppermute | solution.py:65
  89.9 6.2 %cycle_last.1 = (f32[288,4,128]{2,1,0:T(4,128)}, f32[24,16,128]{2,1,0:T(8,128)S(1)}) custom-call(f32[1280,128]{1,0:T(8,128)S(1)} %get-tuple-element.36.own.refs_0_, f32[640,128]{1,0:T(8,128)S(1)} %collective-permute-done.4.from_next.refs_1_, f32[640,128]{1,0:T(8,128)S(1)} %collective-permute-done.5.from_last.refs_2_, ...), custom_call_target="tpu_custom_call" | custom-call | tf_op jit(solution)/shard_map/cycle_last/pallas_call | solution.py:421
  96.2 11.0 %all-to-all-start.1 = ((f32[288,4,128]{2,1,0:T(4,128)}), f32[288,4,128]{2,1,0:T(4,128)S(1)}, u32[]{:S(2)}, u32[]{:S(2)}) async-start(f32[288,4,128]{2,1,0:T(4,128)} %get-tuple-element.43), calls=%async_computation.1 | async-start | bytes 1179648 | tf_op jit(solution)/shard_map/all_to_all | solution.py:535
  108.5 16.6 %all-to-all-done.1 = f32[288,4,128]{2,1,0:T(4,128)S(1)} async-done(((f32[288,4,128]{2,1,0:T(4,128)}), f32[288,4,128]{2,1,0:T(4,128)S(1)}, u32[]{:S(2)}, u32[]{:S(2)}) %all-to-all-start.1) | async-done | bytes 589856 | tf_op jit(solution)/shard_map/all_to_all | solution.py:535
  125.1 2.6 %collect.1 = f32[576,256]{1,0:T(8,128)} custom-call(f32[32,9,4,128]{3,2,1,0:T(4,128)S(1)} %bitcast.13), custom_call_target="tpu_custom_call" | custom-call | tf_op jit(solution)/shard_map/collect/pallas_call | solution.py:421
  (41 shorter events, 5.6 us)
Async XLA Ops:
  0.6 15.6 %copy-start.3 = (s32[8,128,256]{2,1,0:T(8,128)S(1)}, s32[8,128,256]{2,1,0:T(8,128)}, u32[]{:S(2)}) copy-start(s32[8,128,256]{2,1,0:T(8,128)} %param.12) | copy-start | bytes 3145732
  0.6 15.7 %copy-start.4 = (s32[32,4]{0,1:T(4,128)S(1)}, s32[32,4]{0,1:T(4,128)}, u32[]{:S(2)}) copy-start(s32[32,4]{0,1:T(4,128)} %param.15) | copy-start | bytes 1540
  0.7 16.4 %copy-start.5 = (s32[32]{0:T(128)S(1)}, s32[32]{0:T(128)}, u32[]{:S(2)}) copy-start(s32[32]{0:T(128)} %param.14) | copy-start | bytes 388
  3.9 30.4 %all-to-all-start = ((f32[288,4,128]{2,1,0:T(4,128)}), f32[288,4,128]{2,1,0:T(4,128)S(1)}, u32[]{:S(2)}, u32[]{:S(2)}) async-start(f32[288,4,128]{2,1,0:T(4,128)} %bitcast.15), calls=%async_computation | async-start | bytes 1179648 | tf_op jit(solution)/shard_map/all_to_all | solution.py:497
  16.3 40.7 %copy-start = (bf16[1152,1152]{1,0:T(8,128)(2,1)S(1)}, bf16[1152,1152]{1,0:T(8,128)(2,1)}, u32[]{:S(2)}) copy-start(bf16[1152,1152]{1,0:T(8,128)(2,1)} %refs_7_.3) | copy-start | bytes 7962628
  34.3 22.8 %copy-start.2 = (f32[3,1,1152]{2,1,0:T(1,128)S(1)}, f32[3,1,1152]{2,1,0:T(1,128)}, u32[]{:S(2)}) copy-start(f32[3,1,1152]{2,1,0:T(1,128)} %pad_maximum_fusion.refs_9_) | copy-start | bytes 41476
  35.8 9.0 %collective-permute-start = (f32[640,128]{1,0:T(8,128)S(1)}, f32[640,128]{1,0:T(8,128)S(1)}, u32[]{:S(2)}, u32[]{:S(2)}) collective-permute-start(f32[640,128]{1,0:T(8,128)S(1)} %get-tuple-element.27), channel_id=1, source_target_pairs={{1,0},{2,1},{3,2},{4,3},{5,4},{6,5},{7,6},{8,7},{9,8},{10,9},{11,1... | collective-permute-start | bytes 983048 | tf_op jit(solution)/shard_map/ppermute | solution.py:61
  37.7 9.0 %collective-permute-start.1 = (f32[640,128]{1,0:T(8,128)S(1)}, f32[640,128]{1,0:T(8,128)S(1)}, u32[]{:S(2)}, u32[]{:S(2)}) collective-permute-start(f32[640,128]{1,0:T(8,128)S(1)} %get-tuple-element.28), channel_id=1, source_target_pairs={{0,1},{1,2},{2,3},{3,4},{4,5},{5,6},{6,7},{7,8},{8,9},{9,10},{10,1... | collective-permute-start | bytes 983048 | tf_op jit(solution)/shard_map/ppermute | solution.py:62
  46.8 6.5 %collective-permute-start.2 = (f32[640,128]{1,0:T(8,128)S(1)}, f32[640,128]{1,0:T(8,128)S(1)}, u32[]{:S(2)}, u32[]{:S(2)}) collective-permute-start(f32[640,128]{1,0:T(8,128)S(1)} %get-tuple-element.29), channel_id=1, source_target_pairs={{32,0},{64,32},{96,64},{128,96},{160,128},{192,160},{224,192},{33,... | collective-permute-start | bytes 983048 | tf_op jit(solution)/shard_map/ppermute | solution.py:64
  48.7 8.4 %collective-permute-start.3 = (f32[640,128]{1,0:T(8,128)S(1)}, f32[640,128]{1,0:T(8,128)S(1)}, u32[]{:S(2)}, u32[]{:S(2)}) collective-permute-start(f32[640,128]{1,0:T(8,128)S(1)} %get-tuple-element.30), channel_id=1, source_target_pairs={{0,32},{32,64},{64,96},{96,128},{128,160},{160,192},{192,224},{1,3... | collective-permute-start | bytes 983048 | tf_op jit(solution)/shard_map/ppermute | solution.py:65
  57.1 1.8 %copy-start.1 = (bf16[1152,1152]{1,0:T(8,128)(2,1)S(1)}, bf16[1152,1152]{1,0:T(8,128)(2,1)}, u32[]{:S(2)}) copy-start(bf16[1152,1152]{1,0:T(8,128)(2,1)} %refs_8_.3) | copy-start | bytes 7962628
  67.0 10.9 %collective-permute-start.4 = (f32[640,128]{1,0:T(8,128)S(1)}, f32[640,128]{1,0:T(8,128)S(1)}, u32[]{:S(2)}, u32[]{:S(2)}) collective-permute-start(f32[640,128]{1,0:T(8,128)S(1)} %get-tuple-element.37), channel_id=1, source_target_pairs={{1,0},{2,1},{3,2},{4,3},{5,4},{6,5},{7,6},{8,7},{9,8},{10,9},{11,1... | collective-permute-start | bytes 983048 | tf_op jit(solution)/shard_map/ppermute | solution.py:61
  68.9 10.6 %collective-permute-start.5 = (f32[640,128]{1,0:T(8,128)S(1)}, f32[640,128]{1,0:T(8,128)S(1)}, u32[]{:S(2)}, u32[]{:S(2)}) collective-permute-start(f32[640,128]{1,0:T(8,128)S(1)} %get-tuple-element.38), channel_id=1, source_target_pairs={{0,1},{1,2},{2,3},{3,4},{4,5},{5,6},{6,7},{7,8},{8,9},{9,10},{10,1... | collective-permute-start | bytes 983048 | tf_op jit(solution)/shard_map/ppermute | solution.py:62
  79.6 6.5 %collective-permute-start.6 = (f32[640,128]{1,0:T(8,128)S(1)}, f32[640,128]{1,0:T(8,128)S(1)}, u32[]{:S(2)}, u32[]{:S(2)}) collective-permute-start(f32[640,128]{1,0:T(8,128)S(1)} %get-tuple-element.39), channel_id=1, source_target_pairs={{32,0},{64,32},{96,64},{128,96},{160,128},{192,160},{224,192},{33,... | collective-permute-start | bytes 983048 | tf_op jit(solution)/shard_map/ppermute | solution.py:64
  81.5 8.4 %collective-permute-start.7 = (f32[640,128]{1,0:T(8,128)S(1)}, f32[640,128]{1,0:T(8,128)S(1)}, u32[]{:S(2)}, u32[]{:S(2)}) collective-permute-start(f32[640,128]{1,0:T(8,128)S(1)} %get-tuple-element.40), channel_id=1, source_target_pairs={{0,32},{32,64},{64,96},{96,128},{128,160},{160,192},{192,224},{1,3... | collective-permute-start | bytes 983048 | tf_op jit(solution)/shard_map/ppermute | solution.py:65
  96.2 28.9 %all-to-all-start.1 = ((f32[288,4,128]{2,1,0:T(4,128)}), f32[288,4,128]{2,1,0:T(4,128)S(1)}, u32[]{:S(2)}, u32[]{:S(2)}) async-start(f32[288,4,128]{2,1,0:T(4,128)} %get-tuple-element.43), calls=%async_computation.1 | async-start | bytes 1179648 | tf_op jit(solution)/shard_map/all_to_all | solution.py:535

commit v7 on v6

--- a/solution.py
+++ b/solution.py
@@ -437,7 +437,7 @@
 def spread(x):
     x = x.reshape(DIR * ROWS, 2 * LANES)
     scratch = [halves, chunks_dims, sems((10,)), sems((2,))]
-    out = call(spread_kernel, "spread", [x], shape_of(*chunks_dims), scratch, 60, [hbm], hbm)
+    out = call(spread_kernel, "spread", [x], shape_of(*chunks_dims), scratch, 4, [hbm], hbm)
     return out.reshape(QUADS, 4, LANES)
 
 

time: 129 us -> 129 us (level)
    unnamed x12 -> x14, local copies, waits for them, and re-layouts: 1.77 us -> 2.84 us
where the time goes in v7:
time: 129 us; the launch traced here: 128 us
  waiting for transfers between devices  50.4 us (39%)
  starting transfers between devices  42.9 us (33%)
  Pallas kernels  20.1 us (16%)
  local copies, waits for them, and re-layouts  9.14 us (7%)
  other arithmetic  4.4 us (3%)
    pallas_call x8, Pallas kernels, call(): pl.pallas_call(kernel, out_shape=out_shape, in_specs=in_specs or [vmem] *...  20.1 us
    all_to_all x1, waiting for transfers between devices, body(): lax.all_to_all(chunks, 'freq', split_axis=0, concat_axis=0, tiled=True)  16.6 us
    all_to_all x1, starting transfers between devices, body(): lax.all_to_all(spread(spectrum), 'freq', split_axis=0, concat_axis=0, til...  11.4 us
    all_to_all x1, starting transfers between devices, body(): lax.all_to_all(chunks, 'freq', split_axis=0, concat_axis=0, tiled=True)  11 us
    all_to_all x1, waiting for transfers between devices, body(): lax.all_to_all(spread(spectrum), 'freq', split_axis=0, concat_axis=0, til...  10.3 us
    ppermute x2, waiting for transfers between devices, widen(): from_next = lax.ppermute(to_last, 'freq', line(FREQS, 1))  8.17 us
    ppermute x2, starting transfers between devices, widen(): from_last = lax.ppermute(to_next, 'freq', line(FREQS, -1))  7.85 us
    ppermute x2, waiting for transfers between devices, widen(): from_down = lax.ppermute(last, 'band', line(BANDS, -1))  7.64 us
  transfers between devices with their start and end apart: 10, of which 10 were waited for; matrix products, arithmetic and copies ran while one was open for 7% of the time, Pallas kernels for 0%

profile of v7, /device:TPU:34, one launch (start us, length us, event | category | flops | bytes accessed | tf_op | source)
XLA Modules:
  0.0 127.9 jit_solution(9284792990598011783)
XLA Ops:
  0.7 1.1 copy-done.2
  1.7 2.2 %spread.1 = f32[32,9,4,128]{3,2,1,0:T(4,128)} custom-call(f32[576,256]{1,0:T(8,128)S(1)} %bitcast.14), custom_call_target="tpu_custom_call" | custom-call | tf_op jit(solution)/shard_map/spread/pallas_call | solution.py:421
  3.9 11.4 %all-to-all-start = ((f32[288,4,128]{2,1,0:T(4,128)}), f32[288,4,128]{2,1,0:T(4,128)S(1)}, u32[]{:S(2)}, u32[]{:S(2)}) async-start(f32[288,4,128]{2,1,0:T(4,128)} %bitcast.1), calls=%async_computation | async-start | bytes 1179648 | tf_op jit(solution)/shard_map/all_to_all | solution.py:497
  15.4 0.9 fusion.1
  19.3 0.7 mul.118
  20.1 1.0 copy.16
  22.0 0.7 broadcast_multiply_fusion.1
  22.8 1.3 %pad_maximum_fusion.refs_9_ = f32[3,1,1152]{2,1,0:T(1,128)} fusion(f32[1,1,1152]{2,1,0:T(1,128)} %convert_element_type.43, f32[2,1,1152]{2,1,0:T(1,128)S(1)} %broadcast_multiply_fusion.1), kind=kLoop, calls=%fused_computation.7 | loop fusion | flops 3456 | bytes 27648 | tf_op jit(solution)/shard_map/concatenate | solution.py:507
  24.1 10.3 %all-to-all-done.x_ref = f32[288,4,128]{2,1,0:T(4,128)S(1)} async-done(((f32[288,4,128]{2,1,0:T(4,128)}), f32[288,4,128]{2,1,0:T(4,128)S(1)}, u32[]{:S(2)}, u32[]{:S(2)}) %all-to-all-start) | async-done | bytes 589856 | tf_op jit(solution)/shard_map/all_to_all | solution.py:497
  34.3 0.8 broadcast_in_dim.60.refs_6_.sea_ref
  35.9 1.9 %collective-permute-start = (f32[640,128]{1,0:T(8,128)S(1)}, f32[640,128]{1,0:T(8,128)S(1)}, u32[]{:S(2)}, u32[]{:S(2)}) collective-permute-start(f32[640,128]{1,0:T(8,128)S(1)} %get-tuple-element.27), channel_id=1, source_target_pairs={{1,0},{2,1},{3,2},{4,3},{5,4},{6,5},{7,6},{8,7},{9,8},{10,9},{11,1... | collective-permute-start | bytes 983048 | tf_op jit(solution)/shard_map/ppermute | solution.py:61
  37.8 3.9 %collective-permute-start.1 = (f32[640,128]{1,0:T(8,128)S(1)}, f32[640,128]{1,0:T(8,128)S(1)}, u32[]{:S(2)}, u32[]{:S(2)}) collective-permute-start(f32[640,128]{1,0:T(8,128)S(1)} %get-tuple-element.28), channel_id=1, source_target_pairs={{0,1},{1,2},{2,3},{3,4},{4,5},{5,6},{6,7},{7,8},{8,9},{9,10},{10,1... | collective-permute-start | bytes 983048 | tf_op jit(solution)/shard_map/ppermute | solution.py:62
  41.7 3.1 %collective-permute-done.from_next.refs_1_ = f32[640,128]{1,0:T(8,128)S(1)} collective-permute-done((f32[640,128]{1,0:T(8,128)S(1)}, f32[640,128]{1,0:T(8,128)S(1)}, u32[]{:S(2)}, u32[]{:S(2)}) %collective-permute-start) | collective-permute-done | bytes 327712 | tf_op jit(solution)/shard_map/ppermute | solution.py:61
  44.8 1.9 %collective-permute-done.1.from_last.refs_2_ = f32[640,128]{1,0:T(8,128)S(1)} collective-permute-done((f32[640,128]{1,0:T(8,128)S(1)}, f32[640,128]{1,0:T(8,128)S(1)}, u32[]{:S(2)}, u32[]{:S(2)}) %collective-permute-start.1) | collective-permute-done | bytes 327712 | tf_op jit(solution)/shard_map/ppermute | solution.py:62
  46.8 1.9 %collective-permute-start.2 = (f32[640,128]{1,0:T(8,128)S(1)}, f32[640,128]{1,0:T(8,128)S(1)}, u32[]{:S(2)}, u32[]{:S(2)}) collective-permute-start(f32[640,128]{1,0:T(8,128)S(1)} %get-tuple-element.29), channel_id=1, source_target_pairs={{32,0},{64,32},{96,64},{128,96},{160,128},{192,160},{224,192},{33,... | collective-permute-start | bytes 983048 | tf_op jit(solution)/shard_map/ppermute | solution.py:64
  48.8 2.4 %collective-permute-start.3 = (f32[640,128]{1,0:T(8,128)S(1)}, f32[640,128]{1,0:T(8,128)S(1)}, u32[]{:S(2)}, u32[]{:S(2)}) collective-permute-start(f32[640,128]{1,0:T(8,128)S(1)} %get-tuple-element.30), channel_id=1, source_target_pairs={{0,32},{32,64},{64,96},{96,128},{128,160},{160,192},{192,224},{1,3... | collective-permute-start | bytes 983048 | tf_op jit(solution)/shard_map/ppermute | solution.py:65
  51.2 2.2 %collective-permute-done.2.refs_3_ = f32[640,128]{1,0:T(8,128)S(1)} collective-permute-done((f32[640,128]{1,0:T(8,128)S(1)}, f32[640,128]{1,0:T(8,128)S(1)}, u32[]{:S(2)}, u32[]{:S(2)}) %collective-permute-start.2) | collective-permute-done | bytes 327712 | tf_op jit(solution)/shard_map/ppermute | solution.py:64
  53.3 3.8 %collective-permute-done.3.refs_4_ = f32[640,128]{1,0:T(8,128)S(1)} collective-permute-done((f32[640,128]{1,0:T(8,128)S(1)}, f32[640,128]{1,0:T(8,128)S(1)}, u32[]{:S(2)}, u32[]{:S(2)}) %collective-permute-start.3) | collective-permute-done | bytes 327712 | tf_op jit(solution)/shard_map/ppermute | solution.py:65
  57.2 1.7 %copy-done.1 = bf16[1152,1152]{1,0:T(8,128)(2,1)S(1)} copy-done((bf16[1152,1152]{1,0:T(8,128)(2,1)S(1)}, bf16[1152,1152]{1,0:T(8,128)(2,1)}, u32[]{:S(2)}) %copy-start.1) | copy-done | bytes 2654232
  58.9 8.1 %cycle_first.1 = (f32[1280,128]{1,0:T(8,128)S(1)}, f32[640,128]{1,0:T(8,128)S(1)}, f32[640,128]{1,0:T(8,128)S(1)}, f32[24,16,128]{2,1,0:T(8,128)S(1)}, f32[12288...) custom-call(f32[1280,128]{1,0:T(8,128)S(1)} %get-tuple-element.26.own.refs_0_, ...), custom_call_target="tpu_custom_call" | custom-call | tf_op jit(solution)/shard_map/cycle_first/pallas_call | solution.py:421
  67.0 1.9 %collective-permute-start.4 = (f32[640,128]{1,0:T(8,128)S(1)}, f32[640,128]{1,0:T(8,128)S(1)}, u32[]{:S(2)}, u32[]{:S(2)}) collective-permute-start(f32[640,128]{1,0:T(8,128)S(1)} %get-tuple-element.37), channel_id=1, source_target_pairs={{1,0},{2,1},{3,2},{4,3},{5,4},{6,5},{7,6},{8,7},{9,8},{10,9},{11,1... | collective-permute-start | bytes 983048 | tf_op jit(solution)/shard_map/ppermute | solution.py:61
  69.0 3.9 %collective-permute-start.5 = (f32[640,128]{1,0:T(8,128)S(1)}, f32[640,128]{1,0:T(8,128)S(1)}, u32[]{:S(2)}, u32[]{:S(2)}) collective-permute-start(f32[640,128]{1,0:T(8,128)S(1)} %get-tuple-element.38), channel_id=1, source_target_pairs={{0,1},{1,2},{2,3},{3,4},{4,5},{5,6},{6,7},{7,8},{8,9},{9,10},{10,1... | collective-permute-start | bytes 983048 | tf_op jit(solution)/shard_map/ppermute | solution.py:62
  72.9 5.1 %collective-permute-done.4.from_next.refs_1_ = f32[640,128]{1,0:T(8,128)S(1)} collective-permute-done((f32[640,128]{1,0:T(8,128)S(1)}, f32[640,128]{1,0:T(8,128)S(1)}, u32[]{:S(2)}, u32[]{:S(2)}) %collective-permute-start.4) | collective-permute-done | bytes 327712 | tf_op jit(solution)/shard_map/ppermute | solution.py:61
  78.0 1.7 %collective-permute-done.5.from_last.refs_2_ = f32[640,128]{1,0:T(8,128)S(1)} collective-permute-done((f32[640,128]{1,0:T(8,128)S(1)}, f32[640,128]{1,0:T(8,128)S(1)}, u32[]{:S(2)}, u32[]{:S(2)}) %collective-permute-start.5) | collective-permute-done | bytes 327712 | tf_op jit(solution)/shard_map/ppermute | solution.py:62
  79.7 1.9 %collective-permute-start.6 = (f32[640,128]{1,0:T(8,128)S(1)}, f32[640,128]{1,0:T(8,128)S(1)}, u32[]{:S(2)}, u32[]{:S(2)}) collective-permute-start(f32[640,128]{1,0:T(8,128)S(1)} %get-tuple-element.39), channel_id=1, source_target_pairs={{32,0},{64,32},{96,64},{128,96},{160,128},{192,160},{224,192},{33,... | collective-permute-start | bytes 983048 | tf_op jit(solution)/shard_map/ppermute | solution.py:64
  81.6 2.6 %collective-permute-start.7 = (f32[640,128]{1,0:T(8,128)S(1)}, f32[640,128]{1,0:T(8,128)S(1)}, u32[]{:S(2)}, u32[]{:S(2)}) collective-permute-start(f32[640,128]{1,0:T(8,128)S(1)} %get-tuple-element.40), channel_id=1, source_target_pairs={{0,32},{32,64},{64,96},{96,128},{128,160},{160,192},{192,224},{1,3... | collective-permute-start | bytes 983048 | tf_op jit(solution)/shard_map/ppermute | solution.py:65
  84.2 2.0 %collective-permute-done.6.refs_3_ = f32[640,128]{1,0:T(8,128)S(1)} collective-permute-done((f32[640,128]{1,0:T(8,128)S(1)}, f32[640,128]{1,0:T(8,128)S(1)}, u32[]{:S(2)}, u32[]{:S(2)}) %collective-permute-start.6) | collective-permute-done | bytes 327712 | tf_op jit(solution)/shard_map/ppermute | solution.py:64
  86.2 3.8 %collective-permute-done.7.refs_4_ = f32[640,128]{1,0:T(8,128)S(1)} collective-permute-done((f32[640,128]{1,0:T(8,128)S(1)}, f32[640,128]{1,0:T(8,128)S(1)}, u32[]{:S(2)}, u32[]{:S(2)}) %collective-permute-start.7) | collective-permute-done | bytes 327712 | tf_op jit(solution)/shard_map/ppermute | solution.py:65
  90.0 6.2 %cycle_last.1 = (f32[288,4,128]{2,1,0:T(4,128)}, f32[24,16,128]{2,1,0:T(8,128)S(1)}) custom-call(f32[1280,128]{1,0:T(8,128)S(1)} %get-tuple-element.36.own.refs_0_, f32[640,128]{1,0:T(8,128)S(1)} %collective-permute-done.4.from_next.refs_1_, f32[640,128]{1,0:T(8,128)S(1)} %collective-permute-done.5.from_last.refs_2_, ...), custom_call_target="tpu_custom_call" | custom-call | tf_op jit(solution)/shard_map/cycle_last/pallas_call | solution.py:421
  96.3 11.0 %all-to-all-start.1 = ((f32[288,4,128]{2,1,0:T(4,128)}), f32[288,4,128]{2,1,0:T(4,128)S(1)}, u32[]{:S(2)}, u32[]{:S(2)}) async-start(f32[288,4,128]{2,1,0:T(4,128)} %get-tuple-element.43), calls=%async_computation.1 | async-start | bytes 1179648 | tf_op jit(solution)/shard_map/all_to_all | solution.py:535
  108.6 16.6 %all-to-all-done.1 = f32[288,4,128]{2,1,0:T(4,128)S(1)} async-done(((f32[288,4,128]{2,1,0:T(4,128)}), f32[288,4,128]{2,1,0:T(4,128)S(1)}, u32[]{:S(2)}, u32[]{:S(2)}) %all-to-all-start.1) | async-done | bytes 589856 | tf_op jit(solution)/shard_map/all_to_all | solution.py:535
  125.2 2.6 %collect.1 = f32[576,256]{1,0:T(8,128)} custom-call(f32[32,9,4,128]{3,2,1,0:T(4,128)S(1)} %bitcast.13), custom_call_target="tpu_custom_call" | custom-call | tf_op jit(solution)/shard_map/collect/pallas_call | solution.py:421
  (43 shorter events, 6.3 us)
Async XLA Ops:
  0.6 16.4 %copy-start.6 = (s32[32]{0:T(128)S(1)}, s32[32]{0:T(128)}, u32[]{:S(2)}) copy-start(s32[32]{0:T(128)} %param.14) | copy-start | bytes 388
  0.6 1.1 copy-start.2
  1.7 14.6 %copy-start.4 = (s32[8,128,256]{2,1,0:T(8,128)S(1)}, s32[8,128,256]{2,1,0:T(8,128)}, u32[]{:S(2)}) copy-start(s32[8,128,256]{2,1,0:T(8,128)} %param.12) | copy-start | bytes 3145732
  1.7 14.7 %copy-start.5 = (s32[32,4]{0,1:T(4,128)S(1)}, s32[32,4]{0,1:T(4,128)}, u32[]{:S(2)}) copy-start(s32[32,4]{0,1:T(4,128)} %param.15) | copy-start | bytes 1540
  3.9 30.4 %all-to-all-start = ((f32[288,4,128]{2,1,0:T(4,128)}), f32[288,4,128]{2,1,0:T(4,128)S(1)}, u32[]{:S(2)}, u32[]{:S(2)}) async-start(f32[288,4,128]{2,1,0:T(4,128)} %bitcast.1), calls=%async_computation | async-start | bytes 1179648 | tf_op jit(solution)/shard_map/all_to_all | solution.py:497
  16.4 40.8 %copy-start = (bf16[1152,1152]{1,0:T(8,128)(2,1)S(1)}, bf16[1152,1152]{1,0:T(8,128)(2,1)}, u32[]{:S(2)}) copy-start(bf16[1152,1152]{1,0:T(8,128)(2,1)} %refs_7_.3) | copy-start | bytes 7962628
  34.3 22.8 %copy-start.3 = (f32[3,1,1152]{2,1,0:T(1,128)S(1)}, f32[3,1,1152]{2,1,0:T(1,128)}, u32[]{:S(2)}) copy-start(f32[3,1,1152]{2,1,0:T(1,128)} %pad_maximum_fusion.refs_9_) | copy-start | bytes 41476
  35.9 9.0 %collective-permute-start = (f32[640,128]{1,0:T(8,128)S(1)}, f32[640,128]{1,0:T(8,128)S(1)}, u32[]{:S(2)}, u32[]{:S(2)}) collective-permute-start(f32[640,128]{1,0:T(8,128)S(1)} %get-tuple-element.27), channel_id=1, source_target_pairs={{1,0},{2,1},{3,2},{4,3},{5,4},{6,5},{7,6},{8,7},{9,8},{10,9},{11,1... | collective-permute-start | bytes 983048 | tf_op jit(solution)/shard_map/ppermute | solution.py:61
  37.8 9.0 %collective-permute-start.1 = (f32[640,128]{1,0:T(8,128)S(1)}, f32[640,128]{1,0:T(8,128)S(1)}, u32[]{:S(2)}, u32[]{:S(2)}) collective-permute-start(f32[640,128]{1,0:T(8,128)S(1)} %get-tuple-element.28), channel_id=1, source_target_pairs={{0,1},{1,2},{2,3},{3,4},{4,5},{5,6},{6,7},{7,8},{8,9},{9,10},{10,1... | collective-permute-start | bytes 983048 | tf_op jit(solution)/shard_map/ppermute | solution.py:62
  46.8 6.5 %collective-permute-start.2 = (f32[640,128]{1,0:T(8,128)S(1)}, f32[640,128]{1,0:T(8,128)S(1)}, u32[]{:S(2)}, u32[]{:S(2)}) collective-permute-start(f32[640,128]{1,0:T(8,128)S(1)} %get-tuple-element.29), channel_id=1, source_target_pairs={{32,0},{64,32},{96,64},{128,96},{160,128},{192,160},{224,192},{33,... | collective-permute-start | bytes 983048 | tf_op jit(solution)/shard_map/ppermute | solution.py:64
  48.8 8.4 %collective-permute-start.3 = (f32[640,128]{1,0:T(8,128)S(1)}, f32[640,128]{1,0:T(8,128)S(1)}, u32[]{:S(2)}, u32[]{:S(2)}) collective-permute-start(f32[640,128]{1,0:T(8,128)S(1)} %get-tuple-element.30), channel_id=1, source_target_pairs={{0,32},{32,64},{64,96},{96,128},{128,160},{160,192},{192,224},{1,3... | collective-permute-start | bytes 983048 | tf_op jit(solution)/shard_map/ppermute | solution.py:65
  57.2 1.8 %copy-start.1 = (bf16[1152,1152]{1,0:T(8,128)(2,1)S(1)}, bf16[1152,1152]{1,0:T(8,128)(2,1)}, u32[]{:S(2)}) copy-start(bf16[1152,1152]{1,0:T(8,128)(2,1)} %refs_8_.3) | copy-start | bytes 7962628
  67.0 10.9 %collective-permute-start.4 = (f32[640,128]{1,0:T(8,128)S(1)}, f32[640,128]{1,0:T(8,128)S(1)}, u32[]{:S(2)}, u32[]{:S(2)}) collective-permute-start(f32[640,128]{1,0:T(8,128)S(1)} %get-tuple-element.37), channel_id=1, source_target_pairs={{1,0},{2,1},{3,2},{4,3},{5,4},{6,5},{7,6},{8,7},{9,8},{10,9},{11,1... | collective-permute-start | bytes 983048 | tf_op jit(solution)/shard_map/ppermute | solution.py:61
  69.0 10.6 %collective-permute-start.5 = (f32[640,128]{1,0:T(8,128)S(1)}, f32[640,128]{1,0:T(8,128)S(1)}, u32[]{:S(2)}, u32[]{:S(2)}) collective-permute-start(f32[640,128]{1,0:T(8,128)S(1)} %get-tuple-element.38), channel_id=1, source_target_pairs={{0,1},{1,2},{2,3},{3,4},{4,5},{5,6},{6,7},{7,8},{8,9},{9,10},{10,1... | collective-permute-start | bytes 983048 | tf_op jit(solution)/shard_map/ppermute | solution.py:62
  79.7 6.5 %collective-permute-start.6 = (f32[640,128]{1,0:T(8,128)S(1)}, f32[640,128]{1,0:T(8,128)S(1)}, u32[]{:S(2)}, u32[]{:S(2)}) collective-permute-start(f32[640,128]{1,0:T(8,128)S(1)} %get-tuple-element.39), channel_id=1, source_target_pairs={{32,0},{64,32},{96,64},{128,96},{160,128},{192,160},{224,192},{33,... | collective-permute-start | bytes 983048 | tf_op jit(solution)/shard_map/ppermute | solution.py:64
  81.6 8.4 %collective-permute-start.7 = (f32[640,128]{1,0:T(8,128)S(1)}, f32[640,128]{1,0:T(8,128)S(1)}, u32[]{:S(2)}, u32[]{:S(2)}) collective-permute-start(f32[640,128]{1,0:T(8,128)S(1)} %get-tuple-element.40), channel_id=1, source_target_pairs={{0,32},{32,64},{64,96},{96,128},{128,160},{160,192},{192,224},{1,3... | collective-permute-start | bytes 983048 | tf_op jit(solution)/shard_map/ppermute | solution.py:65
  96.3 28.9 %all-to-all-start.1 = ((f32[288,4,128]{2,1,0:T(4,128)}), f32[288,4,128]{2,1,0:T(4,128)S(1)}, u32[]{:S(2)}, u32[]{:S(2)}) async-start(f32[288,4,128]{2,1,0:T(4,128)} %get-tuple-element.43), calls=%async_computation.1 | async-start | bytes 1179648 | tf_op jit(solution)/shard_map/all_to_all | solution.py:535
